TPU v7x, 32 devices: a whole 2x2x4 slice. The times are simulated.
32 devices in a mesh: vec: 4 (over z), row: 8 (over y, x, core).
Axes of the slice: x: 2, y: 2, z: 4, core: 2. Of those that a mesh axis runs over, the one named last changes fastest.
Arguments:
- chol_vectors: float32 [128, 1024, 1024], P('vec', 'row'), may hold values from -16 to 16, as said below
Outputs:
- rotated: float32 [128, 1024, 1024], P('vec', 'row')
- rotation: float32 [1024, 1024], P('row')
Inputs may be any that keep to these rules, and one draw needn't show every extreme that they name: Every matrix chol_vectors[P] is symmetric in its last two dimensions.
All inputs are finite; a program needn't handle non-finite values.
Results may differ from a plain program's by a relative error of at most 0.00014.
Values sent between devices are 32-bit elements; how exact they have to be, the bound alone decides.
No kernel may reach another device: no remote copies, remote signals or barrier semaphores. Data moves between devices by JAX's collectives and lax.ppermute only.
A program may use at most 128 MiB of HBM per device.

v0:
```python
import jax
import jax.numpy as jnp
from jax import lax
from jax.sharding import PartitionSpec as P

ITERS = 2


step_gain = 0.2


def shards(chol_vectors):
    row_count = chol_vectors.shape[1]
    orbitals = chol_vectors.shape[2]
    offset = lax.axis_index("row") * row_count
    highest = lax.Precision.HIGHEST
    local_rows = lax.broadcasted_iota(jnp.int32, (row_count, orbitals), 0) + offset
    local_cols = lax.broadcasted_iota(jnp.int32, (row_count, orbitals), 1)
    identity_rows = (local_rows == local_cols).astype(jnp.float32)
    current = chol_vectors
    rotation = identity_rows
    for iteration in range(ITERS):
        block = lax.dynamic_slice_in_dim(current, offset, row_count, 2)
        diagonal = jnp.diagonal(block, axis1=1, axis2=2)
        own_part = jnp.einsum("pjk,pj->jk", current, diagonal, precision=highest)
        diagonal_all = lax.all_gather(diagonal, "row", axis=1, tiled=True)
        other_part = jnp.einsum("pjk,pk->jk", current, diagonal_all, precision=highest)
        gradient = lax.psum(own_part - other_part, "vec")
        squares = lax.psum(jnp.sum(gradient * gradient), "row")
        norm = jnp.sqrt(squares / (orbitals * orbitals) + 1e-06)
        generator = step_gain / jnp.sqrt(jnp.float32(orbitals)) * gradient / norm
        generator_full = lax.all_gather(generator, "row", axis=0, tiled=True)
        identity_full = jnp.eye(orbitals, dtype=jnp.float32)
        step_full = (
            identity_full
            + generator_full
            + 0.5 * jnp.dot(generator_full, generator_full, precision=highest)
        )
        step_local = lax.dynamic_slice_in_dim(step_full, offset, row_count, 0)
        if iteration == 0:
            rotation = step_local
        else:
            rotation = jnp.dot(rotation, step_full, precision=highest)
        product_left = jnp.einsum("pjk,kl->pjl", current, step_full, precision=highest)
        columns = lax.all_to_all(product_left, "row", split_axis=2, concat_axis=1, tiled=True)
        current = jnp.einsum("pim,ik->pmk", columns, step_full, precision=highest)
    return (current, rotation)


def solution(mesh):
    placed = (P("vec", "row", None),)
    return jax.shard_map(
        shards,
        mesh=mesh,
        in_specs=placed,
        out_specs=(P("vec", "row", None), P("row", None)),
        check_vma=False,
    )
```

profile of v0, /device:TPU:0, one launch (start us, length us, event | category | flops | bytes accessed | tf_op | source)
XLA Modules:
  0.0 1111.5 jit_solution(9601472853553550261)
XLA Ops:
  7.2 1.7 constant_dynamic-slice_fusion.1
  9.0 4.7 copy.37
  13.6 1.9 gather_fusion
  15.5 11.3 %all_gather.12 = f32[32,1024]{0,1:T(8,128)S(1)} all-gather(f32[32,128]{0,1:T(8,128)S(1)} %bitcast.73), channel_id=1, replica_groups=mesh['vec'=4,'row'=8] {'row'}, dimensions={1}, use_global_device_ids=true | all-gather | bytes 147456 | tf_op jit(solution)/shard_map/all_gather | solution.py:26
  26.8 0.2 copy.38
  27.0 8.4 multiply_reduce_fusion.1
  35.4 22.4 %fusion.2 = f32[128,1,1024]{2,1,0:T(1,128)S(1)} fusion(f32[32,128,1]{0,2,1:T(1,128)S(1)} %bitcast.74, f32[32,128,1024]{2,1,0:T(8,128)} %param.1), kind=kOutput, calls=%fused_computation.6 | convolution fusion | flops 50331648 | bytes 17317888 | tf_op jit(solution)/shard_map/pjk,pj->jk/dot_general | solution.py:25
  57.7 0.9 bitcast_subtract_fusion.1
  58.7 0.0 all-gather.3.cloned.1.call-start
  58.7 38.9 %all-reduce.3.cloned.1.call-done = f32[128,1024]{1,0:T(8,128)} async-done(((f32[128,1024]{1,0:T(8,128)}), f32[128,1024]{1,0:T(8,128)}) %all-reduce.3.cloned.1.call-update) | async-done | bytes 524304 | tf_op jit(solution)/shard_map/psum | solution.py:28
  97.6 1.8 multiply_reduce_fusion.3
  99.4 13.3 %psum.29 = f32[]{:T(128)} all-reduce(f32[]{:T(128)} %multiply_reduce_fusion.3), channel_id=1, replica_groups=mesh['vec'=4,'row'=8] {'row'}, use_global_device_ids=true, to_apply=%region_2.3 | all-reduce | flops 1 | bytes 8 | tf_op jit(solution)/shard_map/psum | solution.py:29
  113.5 1.9 multiply_divide_fusion.1
  115.4 0.5 all-reduce.5.cloned.1.call-start
  115.9 34.2 %all-gather.3.cloned.1.call-done = f32[1024,1024]{1,0:T(8,128)} async-done(((f32[128,1024]{1,0:T(8,128)}), f32[1024,1024]{1,0:T(8,128)}) %all-gather.3.cloned.1.call-update) | async-done | bytes 4194320 | tf_op jit(solution)/shard_map/all_gather | solution.py:32
  150.1 18.2 %fusion.4 = f32[1024,1024]{1,0:T(8,128)S(1)} fusion(f32[1024,1024]{1,0:T(8,128)} %all-gather.3.cloned.1.call-done), kind=kOutput, calls=%fused_computation.13 | convolution fusion | flops 12890144768 | bytes 8388608 | tf_op jit(solution)/shard_map/dot_general | solution.py:37
  168.3 1.9 copy-done.2
  170.2 109.4 %convolution_bitcast_fusion = f32[32,128,1024]{1,2,0:T(8,128)} fusion(f32[32,128,1024]{2,1,0:T(8,128)} %param.1, f32[1024,1024]{1,0:T(8,128)S(1)} %fusion.4), kind=kOutput, calls=%fused_computation.10 | convolution fusion | flops 51539607552 | bytes 37748736 | tf_op jit(solution)/shard_map/pjk,kl->pjl/dot_general | solution.py:44
  279.7 15.2 %copy.10 = f32[32,128,1024]{1,0,2:T(8,128)S(1)} copy(f32[32,128,1024]{1,2,0:T(8,128)} %convolution_bitcast_fusion) | data formatting | bytes 33554432 | tf_op jit(solution)/shard_map/pjk,kl->pjl/dot_general | solution.py:44
  294.9 186.6 %all_to_all.36 = f32[32,128,1024]{1,0,2:T(8,128)S(1)} all-to-all(f32[32,128,1024]{1,0,2:T(8,128)S(1)} %copy.10), channel_id=1, replica_groups=mesh['vec'=4,'row'=8] {'row'}, dimensions={2} | all-to-all | bytes 33554432 | tf_op jit(solution)/shard_map/all_to_all | solution.py:45
  481.5 19.3 %copy.51 = f32[32,128,8,128]{1,2,3,0:T(8,128)} copy(f32[32,128,8,128]{1,0,3,2:T(8,128)S(1)} %bitcast.66) | data formatting | bytes 33554432 | tf_op jit(solution)/shard_map/all_to_all | solution.py:45
  500.8 18.0 %all_to_all.29 = f32[32,1024,128]{1,2,0:T(8,128)} reshape(f32[32,8,128,128]{2,1,3,0:T(8,128)} %bitcast.67) | data formatting | bytes 33554432 | tf_op jit(solution)/shard_map/all_to_all | solution.py:45
  518.8 57.8 %fusion.10 = f32[32,128,1024]{2,1,0:T(8,128)S(1)} fusion(f32[32,1024,128]{1,2,0:T(8,128)} %all_to_all.29, f32[1024,1024]{1,0:T(8,128)} %copy-done.2), kind=kOutput, calls=%fused_computation.19 | convolution fusion | flops 51539607552 | bytes 37748736 | tf_op jit(solution)/shard_map/pim,ik->pmk/dot_general | solution.py:46
  576.7 6.2 copy-done
  582.8 0.3 constant_dynamic-slice_fusion
  583.2 4.7 copy.12
  587.8 1.8 gather_fusion.1
  589.6 8.9 all_gather.14
  598.5 0.2 copy.39
  598.7 8.3 multiply_reduce_fusion
  607.0 22.2 %fusion = f32[128,1,1024]{2,1,0:T(1,128)S(1)} fusion(f32[32,128,1]{0,2,1:T(1,128)S(1)} %bitcast.72, f32[32,128,1024]{2,1,0:T(8,128)} %copy-done), kind=kOutput, calls=%fused_computation.3 | convolution fusion | flops 50331648 | bytes 17317888 | tf_op jit(solution)/shard_map/pjk,pj->jk/dot_general | solution.py:25
  629.2 0.9 bitcast_subtract_fusion
  630.2 0.0 all-gather.5.cloned.1.call-start
  630.2 38.8 %all-reduce.5.cloned.1.call-done = f32[128,1024]{1,0:T(8,128)} async-done(((f32[128,1024]{1,0:T(8,128)}), f32[128,1024]{1,0:T(8,128)}) %all-reduce.5.cloned.1.call-update) | async-done | bytes 524304 | tf_op jit(solution)/shard_map/psum | solution.py:28
  669.0 1.8 multiply_reduce_fusion.2
  670.8 13.3 %psum.31 = f32[]{:T(128)} all-reduce(f32[]{:T(128)} %multiply_reduce_fusion.2), channel_id=1, replica_groups=mesh['vec'=4,'row'=8] {'row'}, use_global_device_ids=true, to_apply=%region_5.6 | all-reduce | flops 1 | bytes 8 | tf_op jit(solution)/shard_map/psum | solution.py:29
  684.8 1.9 multiply_divide_fusion
  686.7 34.7 %all-gather.5.cloned.1.call-done = f32[1024,1024]{1,0:T(8,128)} async-done(((f32[128,1024]{1,0:T(8,128)}), f32[1024,1024]{1,0:T(8,128)}) %all-gather.5.cloned.1.call-update) | async-done | bytes 4194320 | tf_op jit(solution)/shard_map/all_gather | solution.py:32
  721.5 18.2 %fusion.5 = f32[1024,1024]{1,0:T(8,128)S(1)} fusion(f32[1024,1024]{1,0:T(8,128)} %all-gather.5.cloned.1.call-done), kind=kOutput, calls=%fused_computation.14 | convolution fusion | flops 12890144768 | bytes 8388608 | tf_op jit(solution)/shard_map/dot_general | solution.py:37
  739.7 2.0 copy-done.1
  741.6 58.7 %fusion.8 = f32[32,128,1024]{2,1,0:T(8,128)} fusion(f32[32,128,1024]{2,1,0:T(8,128)} %copy-done, f32[1024,1024]{1,0:T(8,128)S(1)} %fusion.5), kind=kOutput, calls=%fused_computation.17 | convolution fusion | flops 51539607552 | bytes 37748736 | tf_op jit(solution)/shard_map/pjk,kl->pjl/dot_general | solution.py:44
  800.4 17.4 %copy.13 = f32[32,128,1024]{1,0,2:T(8,128)} copy(f32[32,128,1024]{2,1,0:T(8,128)} %fusion.8) | data formatting | bytes 33554432 | tf_op jit(solution)/shard_map/pjk,kl->pjl/dot_general | solution.py:44
  817.7 5.9 all-to-all-start.1
  823.7 5.6 fusion.13
  829.2 178.2 %all-to-all-done.1 = f32[32,128,1024]{1,0,2:T(8,128)} async-done(((f32[32,128,1024]{1,0,2:T(8,128)}), f32[32,128,1024]{1,0,2:T(8,128)}, u32[]{:S(2)}, u32[]{:S(2)}) %all-to-all-start.1) | async-done | bytes 16777248 | tf_op jit(solution)/shard_map/all_to_all | solution.py:45
  1007.4 17.8 %copy.50 = f32[32,128,8,128]{1,2,3,0:T(8,128)} copy(f32[32,128,8,128]{1,0,3,2:T(8,128)} %bitcast.21) | data formatting | bytes 33554432 | tf_op jit(solution)/shard_map/all_to_all | solution.py:45
  1025.2 18.0 %all_to_all.33 = f32[32,1024,128]{1,2,0:T(8,128)} reshape(f32[32,8,128,128]{2,1,3,0:T(8,128)} %bitcast.68) | data formatting | bytes 33554432 | tf_op jit(solution)/shard_map/all_to_all | solution.py:45
  1043.2 61.6 %fusion.6 = f32[32,128,1024]{2,1,0:T(8,128)} fusion(f32[32,1024,128]{1,2,0:T(8,128)} %all_to_all.33, f32[1024,1024]{1,0:T(8,128)} %copy-done.1), kind=kOutput, calls=%fused_computation.15 | convolution fusion | flops 51539607552 | bytes 37748736 | tf_op jit(solution)/shard_map/pim,ik->pmk/dot_general | solution.py:46
  (9 shorter events, 0.1 us)
Async XLA Ops:
  7.2 90.5 %all-reduce.3.cloned.1.call-start = ((), (), s32[]{:S(2)}) async-start(), calls=%async_computation.2 | async-start | bytes 1048576 | tf_op jit(solution)/shard_map/psum | solution.py:28
  58.7 91.4 %all-gather.3.cloned.1.call-start = ((), (), s32[]{:S(2)}) async-start(), calls=%async_computation.3 | async-start | bytes 4718592 | tf_op jit(solution)/shard_map/all_gather | solution.py:32
  115.4 553.6 %all-reduce.5.cloned.1.call-start = ((), (), s32[]{:S(2)}) async-start(), calls=%async_computation.4 | async-start | bytes 1048576 | tf_op jit(solution)/shard_map/psum | solution.py:28
  168.3 1.9 copy-start.2
  576.7 6.2 copy-start
  630.2 91.3 %all-gather.5.cloned.1.call-start = ((), (), s32[]{:S(2)}) async-start(), calls=%async_computation.5 | async-start | bytes 4718592 | tf_op jit(solution)/shard_map/all_gather | solution.py:32
  739.7 2.0 copy-start.1
  817.7 189.7 %all-to-all-start.1 = ((f32[32,128,1024]{1,0,2:T(8,128)}), f32[32,128,1024]{1,0,2:T(8,128)}, u32[]{:S(2)}, u32[]{:S(2)}) async-start(f32[32,128,1024]{1,0,2:T(8,128)} %copy.13), calls=%async_computation.1 | async-start | bytes 33554432 | tf_op jit(solution)/shard_map/all_to_all | solution.py:45
Sparse Core Ops, SparseCore 0:
  58.8 38.7 all-reduce.2
  115.5 34.5 all-gather.2
  630.3 38.6 all-reduce.4
  686.9 34.5 all-gather.4
where the time goes:
time: 1120 us; the launch traced here: 1110 us
  matrix products  374 us (33%)
  waiting for transfers between devices  325 us (29%)
  blocking collectives  234 us (21%)
  local copies, waits for them, and re-layouts  131 us (12%)
  other arithmetic  25.9 us (2%)
  between operations  15.5 us (1%)
    all_to_all x1, blocking collectives, shards(): lax.all_to_all(product_left, 'row', split_axis=2, concat_axis=1, tiled=True)  187 us
    all_to_all x1, waiting for transfers between devices, shards(): lax.all_to_all(product_left, 'row', split_axis=2, concat_axis=1, tiled=True)  178 us
    dot_general x2, matrix products, shards(): jnp.einsum('pjk,kl->pjl', current, step_full, precision=highest)  168 us
    dot_general x2, matrix products, shards(): current = jnp.einsum('pim,ik->pmk', columns, step_full, precision=highest)  119 us
    psum x2, waiting for transfers between devices, shards(): gradient = lax.psum(own_part - other_part, 'vec')  77.7 us
    all_to_all x4, local copies, waits for them, and re-layouts, shards(): lax.all_to_all(product_left, 'row', split_axis=2, concat_axis=1, tiled=True)  73.1 us
    all_gather x2, waiting for transfers between devices, shards(): generator_full = lax.all_gather(generator, 'row', axis=0, tiled=True)  69 us
    dot_general x2, matrix products, shards(): own_part = jnp.einsum('pjk,pj->jk', current, diagonal, precision=highest)  44.6 us
  transfers between devices with their start and end apart: 5, of which 5 were waited for; matrix products, arithmetic and copies ran while one was open for 0% of the time, Pallas kernels for 0%

commit v1 on v0

v1 whole, which is shorter than its diff:
```python
import functools

import jax
import jax.numpy as jnp
from jax import lax
from jax.experimental import pallas as pl
from jax.experimental.pallas import tpu as pltpu
from jax.sharding import PartitionSpec as P


step_gain = 0.2
chunk_count = 4
high = lax.Precision.HIGH


def swap(x, k):
    count = lax.axis_size("row")
    return lax.ppermute(x, "row", [(i, i ^ k) for i in range(count)])


def turn(x, k):
    count = lax.axis_size("vec")
    return lax.ppermute(x, "vec", [(i, (i + k) % count) for i in range(count)])


def cut(x, index, size, axis):
    return lax.dynamic_slice_in_dim(x, index * size, size, axis)


def place(whole, part, index):
    return lax.dynamic_update_slice_in_dim(whole, part, index * part.shape[0], 0)


def sum_over_vec(part):
    count = lax.axis_size("vec")
    me = lax.axis_index("vec")
    size = part.shape[0] // count
    total = cut(part, me, size, 0)
    for k in range(1, count):
        total = total + turn(cut(part, (me + k) % count, size, 0), k)
    whole = place(jnp.zeros_like(part), total, me)
    for k in range(1, count):
        whole = place(whole, turn(total, k), (me - k) % count)
    return whole


def gather_rows(part):
    count = lax.axis_size("row")
    me = lax.axis_index("row")
    whole = jnp.zeros((count * part.shape[0], part.shape[1]), part.dtype)
    for k in range(0, count, 2):
        mine = part if k == 0 else swap(part, k)
        whole = place(whole, mine, me ^ k)
        whole = place(whole, swap(mine, 1), me ^ k ^ 1)
    return whole


def sum_over_row(part):
    pair = part + swap(part, 1)
    total = pair
    for k in range(2, lax.axis_size("row"), 2):
        total = total + swap(pair, k)
    return total


def step_of(gradient):
    orbitals = gradient.shape[0]
    norm = jnp.sqrt(jnp.sum(gradient * gradient) / (orbitals * orbitals) + 1e-06)
    generator = step_gain / jnp.sqrt(jnp.float32(orbitals)) * gradient / norm
    square = jnp.dot(generator, generator, precision=high)
    return jnp.eye(orbitals, dtype=jnp.float32) + generator + 0.5 * square


def plain_shards(chol_vectors):
    vectors, rows, orbitals = chol_vectors.shape
    devices = lax.axis_size("row")
    me = lax.axis_index("row")
    chunk = vectors // chunk_count

    block = cut(chol_vectors, me, rows, 2)
    here = jnp.eye(rows, dtype=jnp.bool_)
    diagonal = jnp.sum(jnp.where(here, block, 0.0), axis=2)
    part = jnp.sum(chol_vectors * diagonal[:, :, None], axis=0)
    terms = gather_rows(sum_over_vec(part))
    step = step_of(terms - terms.T)

    step_rows = cut(step, me, rows, 0)
    lefts = []
    part = jnp.zeros((rows, orbitals), jnp.float32)
    for c in range(chunk_count):
        own = chol_vectors[c * chunk : (c + 1) * chunk]
        left = jnp.einsum("pab,bm->pam", own, step, precision=high)
        lefts.append(left)
        diagonal = sum_over_row(jnp.sum(left * step_rows, axis=1))
        part = part + jnp.sum(left * diagonal[:, None, :], axis=0)
    terms = gather_rows(sum_over_vec(part))
    terms = lax.dot_general(step, terms, (((0,), (0,)), ((), ())), precision=high)
    step_next = step_of(terms.T - terms)
    rotation = jnp.dot(step, step_next, precision=high)
    order = me ^ jnp.arange(devices)
    rotation_order = rotation.reshape(devices, rows, orbitals)[order].reshape(orbitals, orbitals)

    outs = []
    for c in range(chunk_count):
        left = jnp.einsum("pab,bm->pam", lefts[c], step_next, precision=high)
        pieces = []
        for k in range(devices):
            piece = cut(left, me ^ k, rows, 2)
            pieces.append(piece if k == 0 else swap(piece, k))
        columns = jnp.concatenate(pieces, axis=1)
        outs.append(jnp.einsum("pam,ak->pmk", columns, rotation_order, precision=high))
    return jnp.concatenate(outs, axis=0), cut(rotation, me, rows, 0)


lane = 128
quad = 4
bf16, f32 = jnp.bfloat16, jnp.float32


def split(x):
    upper = x.astype(bf16)
    return upper, (x - upper.astype(f32)).astype(bf16)


def product(left, right):
    dot = functools.partial(jnp.dot, preferred_element_type=f32)
    return dot(left[0], right[0]) + (dot(left[0], right[1]) + dot(left[1], right[0]))


def whole_spec():
    return pl.BlockSpec(memory_space=pltpu.VMEM)


def resident(shape):
    return pl.BlockSpec(shape, lambda i: (0,) * len(shape), pipeline_mode=pl.Buffered(1))


def cost(flops, data):
    return pl.CostEstimate(flops=flops, bytes_accessed=data, transcendentals=0)


def gradient_kernel(me_ref, vectors_ref, slab_ref, out_ref):
    size, width = slab_ref.shape[1:]
    row = lax.broadcasted_iota(jnp.int32, (size, width), 0) + pl.program_id(0) * size
    here = lax.broadcasted_iota(jnp.int32, (size, width), 1) == row
    total = jnp.zeros(out_ref.shape, f32)
    for p in range(vectors_ref.shape[0]):
        diagonal = jnp.sum(jnp.where(here, slab_ref[p], 0.0), axis=1, keepdims=True)
        total = total + vectors_ref[p] * diagonal
    out_ref[...] = total


def gradient_terms(chol_vectors, me):
    vectors, rows, orbitals = chol_vectors.shape
    size = 16
    return pl.pallas_call(
        gradient_kernel,
        grid_spec=pltpu.PrefetchScalarGridSpec(
            num_scalar_prefetch=1,
            grid=(rows // size,),
            in_specs=[
                pl.BlockSpec((vectors, size, orbitals), lambda i, me: (0, i, 0)),
                pl.BlockSpec((vectors, size, rows), lambda i, me: (0, i, me[0])),
            ],
            out_specs=pl.BlockSpec((size, orbitals), lambda i, me: (i, 0)),
        ),
        out_shape=jax.ShapeDtypeStruct((rows, orbitals), f32),
        cost_estimate=cost(2 * chol_vectors.size, 4 * chol_vectors.size),
        name="gradient_terms",
    )(me, chol_vectors, chol_vectors)


def skew_part(terms_ref, sign, skew_ref, upper_ref, lower_ref):
    def body(i, total):
        at = pl.ds(pl.multiple_of(i * lane, lane), lane)
        skew = sign * (terms_ref[at, :] - terms_ref[:, at].T)
        skew_ref[at, :] = skew
        upper_ref[at, :], lower_ref[at, :] = split(skew)
        return total + jnp.sum(skew * skew, axis=(0, 1), keepdims=True)

    return lax.fori_loop(0, skew_ref.shape[0] // lane, body, jnp.zeros((1, 1), f32))


def step_parts(total, skew_ref, upper_ref, lower_ref, store):
    orbitals = skew_ref.shape[0]
    norm = jnp.sqrt(total / (orbitals * orbitals) + 1e-06)
    scale = step_gain / jnp.sqrt(jnp.full((1, 1), orbitals, f32)) / norm
    tile = orbitals // 2

    @pl.loop(0, 2)
    def _(t):
        at = pl.ds(pl.multiple_of(t * tile, tile), tile)
        square = product(
            (upper_ref[at, :], lower_ref[at, :]), (upper_ref[...], lower_ref[...])
        )
        row = lax.broadcasted_iota(jnp.int32, (tile, orbitals), 0) + t * tile
        column = lax.broadcasted_iota(jnp.int32, (tile, orbitals), 1)
        even = jnp.where(row == column, 1.0, 0.0) + (0.5 * scale * scale) * square
        store(at, even, scale * skew_ref[at, :])


def first_kernel(devices, me_ref, *refs):
    shards, refs = refs[:devices], refs[devices:]
    step, turned = refs[:2], refs[2:4]
    terms, skew, upper, lower = refs[4:]
    rows = shards[0].shape[0]
    for k in range(devices):
        terms[pl.ds(pl.multiple_of((me_ref[0] ^ k) * rows, rows), rows), :] = shards[k][...]
    total = skew_part(terms, 1.0, skew, upper, lower)

    def store(at, even, odd):
        step[0][at, :], step[1][at, :] = split(even + odd)
        turned[0][at, :], turned[1][at, :] = split(even - odd)

    step_parts(total, skew, upper, lower, store)


def second_kernel(devices, me_ref, *refs):
    shards, turned, refs = refs[:devices], refs[devices : devices + 2], refs[devices + 2 :]
    step, ordered = refs[:2], refs[2:4]
    terms, skew, upper, lower = refs[4:]
    rows = shards[0].shape[0]
    orbitals = terms.shape[0]
    me = me_ref[0]
    for k in range(devices):
        at = pl.ds(pl.multiple_of((me ^ k) * rows, rows), rows)
        upper[at, :], lower[at, :] = split(shards[k][...])
    tile = orbitals // 2

    @pl.loop(0, 2)
    def _(t):
        at = pl.ds(pl.multiple_of(t * tile, tile), tile)
        terms[at, :] = product(
            (turned[0][at, :], turned[1][at, :]), (upper[...], lower[...])
        )

    total = skew_part(terms, -1.0, skew, upper, lower)

    def store(at, even, odd):
        whole = even + odd
        step[0][at, :], step[1][at, :] = split(whole)
        terms[at, :] = whole
        for k in range(devices):
            source = pl.ds(pl.multiple_of((me ^ k) * rows, rows), rows)
            here = pl.ds(k * rows, rows)
            ordered[0][at, here], ordered[1][at, here] = split(terms[at, source])

    step_parts(total, skew, upper, lower, store)


def make_step(kernel, me, shards, extra):
    devices = len(shards)
    orbitals = shards[0].shape[1]
    square = (orbitals, orbitals)
    part = jax.ShapeDtypeStruct(square, bf16)
    return pl.pallas_call(
        functools.partial(kernel, devices),
        in_specs=[pl.BlockSpec(memory_space=pltpu.SMEM)]
        + [whole_spec()] * (devices + len(extra)),
        out_specs=[whole_spec()] * 4,
        out_shape=[part] * 4,
        scratch_shapes=[
            pltpu.VMEM(square, f32),
            pltpu.VMEM(square, f32),
            pltpu.VMEM(square, bf16),
            pltpu.VMEM(square, bf16),
        ],
        cost_estimate=cost(12 * orbitals**3, 24 * orbitals**2),
    )(me, *shards, *extra)


def compose_kernel(devices, me_ref, left_upper, left_lower, right_upper, right_lower, *refs):
    by_column, by_row, own_ref, whole = refs[:2], refs[2:4], refs[4], refs[5]
    rows = own_ref.shape[0]
    tile = whole.shape[0] // 2
    me = me_ref[0]

    @pl.loop(0, 2)
    def _(t):
        at = pl.ds(pl.multiple_of(t * tile, tile), tile)
        whole[at, :] = product(
            (left_upper[at, :], left_lower[at, :]), (right_upper[...], right_lower[...])
        )

    own_ref[...] = whole[pl.ds(pl.multiple_of(me * rows, rows), rows), :]
    for k in range(devices):
        source = pl.ds(pl.multiple_of((me ^ k) * rows, rows), rows)
        here = pl.ds(k * rows, rows)
        by_column[0][:, here], by_column[1][:, here] = split(whole[:, source])
        by_row[0][here, :], by_row[1][here, :] = split(whole[source, :])


def compose(me, left, right, devices):
    orbitals = left[0].shape[0]
    square = (orbitals, orbitals)
    part = jax.ShapeDtypeStruct(square, bf16)
    out = pl.pallas_call(
        functools.partial(compose_kernel, devices),
        in_specs=[pl.BlockSpec(memory_space=pltpu.SMEM)] + [whole_spec()] * 4,
        out_specs=[whole_spec()] * 5,
        out_shape=[part] * 4 + [jax.ShapeDtypeStruct((orbitals // devices, orbitals), f32)],
        scratch_shapes=[pltpu.VMEM(square, f32)],
        cost_estimate=cost(6 * orbitals**3, 16 * orbitals**2),
        name="compose",
    )(me, *left, *right)
    return out[:2], out[2:4], out[4]


def first_product_kernel(vectors_ref, upper, lower, rows_upper, rows_lower, out_upper, out_lower, diagonal):
    size, rows, orbitals = vectors_ref.shape
    own = rows_upper[...].astype(f32) + rows_lower[...].astype(f32)
    for q in range(0, size, quad):
        at = pl.ds(q, quad)
        vectors = vectors_ref[at].reshape(quad * rows, orbitals)
        left = product(split(vectors), (upper[...], lower[...])).reshape(quad, rows, orbitals)
        out_upper[at], out_lower[at] = split(left)
        diagonal[at] = jnp.sum(left * own[None], axis=1)


def first_product(chol_vectors, step, me):
    vectors, rows, orbitals = chol_vectors.shape
    size = 2 * quad
    part = jax.ShapeDtypeStruct(chol_vectors.shape, bf16)
    block = pl.BlockSpec((size, rows, orbitals), lambda i, me: (i, 0, 0))
    square = pl.BlockSpec(
        (orbitals, orbitals), lambda i, me: (0, 0), pipeline_mode=pl.Buffered(1)
    )
    own = pl.BlockSpec((rows, orbitals), lambda i, me: (me[0], 0))
    out = pl.pallas_call(
        lambda me_ref, *refs: first_product_kernel(*refs),
        grid_spec=pltpu.PrefetchScalarGridSpec(
            num_scalar_prefetch=1,
            grid=(vectors // size,),
            in_specs=[block, square, square, own, own],
            out_specs=[block, block, pl.BlockSpec((size, orbitals), lambda i, me: (i, 0))],
        ),
        out_shape=[part, part, jax.ShapeDtypeStruct((vectors, orbitals), f32)],
        cost_estimate=cost(6 * chol_vectors.size * orbitals, 8 * chol_vectors.size),
        name="first_product",
    )(me, chol_vectors, *step, *step)
    return out[:2], out[2]


def pieces_kernel(rows, left_upper, left_lower, upper, lower, *outs):
    count = left_upper.shape[0]
    left = tuple(r[...].reshape(count * rows, -1) for r in (left_upper, left_lower))
    value = product(left, (upper[...], lower[...]))
    for k, out in enumerate(outs):
        for p in range(count):
            out[p] = value[p * rows : (p + 1) * rows, k * rows : (k + 1) * rows].T


def plain_pieces(lefts, right, vectors, devices):
    rows, orbitals = lefts[0].shape[1:]
    block = pl.BlockSpec((quad, rows, orbitals), lambda i: (i, 0, 0))
    return pl.pallas_call(
        functools.partial(pieces_kernel, rows),
        grid=(vectors // quad,),
        in_specs=[block] * 2 + [resident((orbitals, orbitals))] * 2,
        out_specs=[pl.BlockSpec((quad, rows, rows), lambda i: (i, 0, 0))] * devices,
        out_shape=[jax.ShapeDtypeStruct((vectors, rows, rows), f32)] * devices,
        cost_estimate=cost(6 * vectors * rows * orbitals**2, 8 * vectors * rows * orbitals),
        name="plain_pieces",
    )(*lefts, *right)


def turns(side):
    return (lambda i: jnp.minimum(i, 1)) if side == 0 else (lambda i: jnp.maximum(i - 2, 0))


def shared_pieces_kernel(near, rows, own, one, two, upper, lower, *outs):
    count = own.shape[0]
    half = len(outs) // 2
    for side, other in enumerate((one, two)):
        @pl.when(pl.program_id(0) // 2 == side)
        def _():
            right = tuple(
                jnp.concatenate([r[:, k * rows : (k + 1) * rows] for k in near[side]], axis=1)
                for r in (upper, lower)
            )
            left = jnp.concatenate([own[...], other[...]], axis=0)
            value = product(split(left.reshape(2 * count * rows, -1)), right)
            for b in range(half):
                for p in range(2 * count):
                    block = value[p * rows : (p + 1) * rows, b * rows : (b + 1) * rows]
                    outs[side * half + b][p % count, p // count] = block.T


def shared_pieces(near, chol_vectors, starts, others, right):
    _, rows, orbitals = chol_vectors.shape
    half = len(near[0])
    first, second = (start // 2 for start in starts)
    specs = [
        pl.BlockSpec(
            (2, rows, orbitals), lambda i: (jnp.where(i < 2, first + i, second + i - 2), 0, 0)
        )
    ]
    outs = []
    for side in range(2):
        turn_of = turns(side)
        specs.append(pl.BlockSpec((2, rows, orbitals), lambda i, t=turn_of: (t(i), 0, 0)))
        outs += [
            pl.BlockSpec((2, 2, rows, rows), lambda i, t=turn_of: (t(i), 0, 0, 0))
        ] * half
    out = pl.pallas_call(
        functools.partial(shared_pieces_kernel, near, rows),
        grid=(4,),
        in_specs=specs + [resident((orbitals, orbitals))] * 2,
        out_specs=outs,
        out_shape=[jax.ShapeDtypeStruct((quad, 2, rows, rows), f32)] * (2 * half),
        cost_estimate=cost(
            12 * quad * rows * orbitals**2, 16 * quad * rows * orbitals
        ),
        name="shared_pieces",
    )(chol_vectors, *others, *right)
    return out[:half], out[half:]


def rotated_kernel(upper, lower, *refs):
    parts, out_ref = refs[:-1], refs[-1]
    count, rows, _ = out_ref.shape
    left = jnp.concatenate([r[...].reshape(count * rows, rows) for r in parts], axis=1)
    out_ref[...] = product(split(left), (upper[...], lower[...])).reshape(out_ref.shape)


def plain_rotated(shape, parts, right):
    vectors, rows = parts[0].shape[:2]
    orbitals = shape[2]
    part = pl.BlockSpec((quad, rows, rows), lambda i: (i, 0, 0))
    return pl.pallas_call(
        rotated_kernel,
        grid=(vectors // quad,),
        in_specs=[resident((orbitals, orbitals))] * 2
        + [part] * len(parts),
        out_specs=pl.BlockSpec((quad, rows, orbitals), lambda i: (i, 0, 0)),
        out_shape=jax.ShapeDtypeStruct(shape, f32),
        cost_estimate=cost(6 * vectors * rows * orbitals**2, 8 * vectors * rows * orbitals),
        name="plain_rotated",
    )(*right, *parts)


def shared_rotated_kernel(orders, upper, lower, *refs):
    out_ref = refs[-1]
    count, rows, _ = out_ref.shape
    half = len(orders[0]) // 2
    for side, order in enumerate(orders):
        @pl.when(pl.program_id(0) // 2 == side)
        def _():
            columns = [
                refs[side * half + index][:, which].reshape(count * rows, rows)
                for index, which in order
            ]
            left = split(jnp.concatenate(columns, axis=1))
            out_ref[...] = product(left, (upper[...], lower[...])).reshape(out_ref.shape)


def shared_rotated(previous, parts, orders, starts, right, shape):
    _, rows, orbitals = shape
    fresh = previous is None
    first, second = (start // 2 for start in starts)
    specs = []
    for side in range(2):
        turn_of = turns(side)
        specs += [
            pl.BlockSpec((2, 2, rows, rows), lambda i, t=turn_of: (t(i), 0, 0, 0))
        ] * len(parts[side])
    count = 2 + len(specs)
    return pl.pallas_call(
        functools.partial(shared_rotated_kernel, orders),
        grid=(4,),
        in_specs=[resident((orbitals, orbitals))] * 2
        + specs
        + ([] if fresh else [pl.BlockSpec(memory_space=pl.ANY)]),
        out_specs=pl.BlockSpec(
            (2, rows, orbitals), lambda i: (jnp.where(i < 2, first + i, second + i - 2), 0, 0)
        ),
        out_shape=jax.ShapeDtypeStruct(shape, f32),
        input_output_aliases={} if fresh else {count: 0},
        cost_estimate=cost(12 * quad * rows * orbitals**2, 16 * quad * rows * orbitals),
        name="shared_rotated",
    )(*right, *parts[0], *parts[1], *([] if fresh else [previous]))


def second_terms_kernel(upper_ref, lower_ref, diagonal_ref, out_ref):
    total = jnp.zeros(out_ref.shape, f32)
    for p in range(upper_ref.shape[0]):
        left = upper_ref[p].astype(f32) + lower_ref[p].astype(f32)
        total = total + left * diagonal_ref[p : p + 1, :]
    out_ref[...] = total


def second_terms(lefts, diagonal):
    vectors, rows, orbitals = lefts[0].shape
    size = 16
    block = pl.BlockSpec((vectors, size, orbitals), lambda i: (0, i, 0))
    return pl.pallas_call(
        second_terms_kernel,
        grid=(rows // size,),
        in_specs=[block, block, pl.BlockSpec((vectors, orbitals), lambda i: (0, 0))],
        out_specs=pl.BlockSpec((size, orbitals), lambda i: (i, 0)),
        out_shape=jax.ShapeDtypeStruct((rows, orbitals), f32),
        cost_estimate=cost(2 * lefts[0].size, 4 * lefts[0].size),
        name="second_terms",
    )(*lefts, diagonal)


def flip(x, k):
    count = lax.axis_size("vec")
    return lax.ppermute(x, "vec", [(i, i ^ k) for i in range(count)])


def sum_halves(part):
    bits = lax.axis_size("vec").bit_length() - 1
    masks = [2 ** (b + 1) - 1 for b in range(bits)]
    half = part.shape[0] // 2
    one, two = part[:half], part[half:]
    for a, b in zip(masks, reversed(masks)):
        one, two = one + flip(one, a), two + flip(two, b)
    return jnp.concatenate([one, two], axis=0)


def shards_of(part):
    out = []
    for k in range(0, lax.axis_size("row"), 2):
        mine = part if k == 0 else swap(part, k)
        out += [mine, swap(mine, 1)]
    return out


def after(x, *others):
    return lax.optimization_barrier((x,) + others)[0]


def tiled_shards(chol_vectors):
    shape = chol_vectors.shape
    vectors, _, _ = shape
    devices = lax.axis_size("row")
    me = lax.axis_index("row").astype(jnp.int32)[None]
    groups = shared_groups(vectors)
    plain = vectors - 2 * quad * groups
    bits = (devices // 2, devices // 4)
    everyone = list(range(devices))
    near = [[k for k in everyone if not k & bit] for bit in bits]
    orders = [
        [(near[s].index(k & ~bit), int(bool(k & bit))) for k in everyone]
        for s, bit in enumerate(bits)
    ]
    starts = [
        [plain + (s * groups + g) * quad for s in range(2)] for g in range(groups)
    ]

    own = [[chol_vectors[start : start + quad] for start in starts[g]] for g in range(groups)]
    early = {}

    def send_early(g, *others):
        for s, bit in enumerate(bits):
            early[g, s] = swap(after(own[g][s], *others), bit)

    part = gradient_terms(chol_vectors, me)
    part = sum_halves(part)
    gathered = shards_of(part)
    for g in range(groups - 1):
        send_early(g, *gathered)
    *step, turned_upper, turned_lower = make_step(first_kernel, me, gathered, ())
    lefts, diagonal = first_product(chol_vectors, step, me)
    diagonal = sum_over_row(diagonal)
    part = second_terms(lefts, diagonal)
    gathered = shards_of(sum_halves(part))
    send_early(groups - 1, *gathered)
    *next_step, ordered_upper, ordered_lower = make_step(
        second_kernel, me, gathered, (turned_upper, turned_lower)
    )
    sent = plain_pieces(lefts, (ordered_upper, ordered_lower), plain, devices)
    plain_parts = [sent[0]] + [swap(sent[k], k) for k in everyone[1:]]
    next_step = lax.optimization_barrier((*next_step, *sent))[:2]
    by_column, by_row, rotation = compose(me, step, next_step, devices)

    shared_parts = []
    for g in range(groups):
        others = (early[g, 0], early[g, 1])
        sent = shared_pieces(near, chol_vectors, starts[g], others, by_column)
        shared_parts.append(
            [
                [pieces[0]] + [swap(pieces[i], near[s][i]) for i in range(1, len(near[s]))]
                for s, pieces in enumerate(sent)
            ]
        )
        by_column = lax.optimization_barrier((*by_column, *sent[0], *sent[1]))[:2]
    rotated = plain_rotated(shape, plain_parts, by_row)
    for g in range(groups):
        rotated = shared_rotated(rotated, shared_parts[g], orders, starts[g], by_row, shape)
    return rotated, rotation


def shared_groups(vectors):
    return (3 * vectors // 4) // (2 * quad)


def shards(chol_vectors):
    vectors, rows, _ = chol_vectors.shape
    devices, groups = lax.axis_size("row"), lax.axis_size("vec")
    tiled = rows % lane == 0 and vectors % (2 * quad) == 0 and devices >= 8
    if tiled and devices & (devices - 1) == 0 and groups & (groups - 1) == 0:
        return tiled_shards(chol_vectors)
    return plain_shards(chol_vectors)


def solution(mesh):
    return jax.shard_map(
        shards,
        mesh=mesh,
        in_specs=(P("vec", "row", None),),
        out_specs=(P("vec", "row", None), P("row", None)),
        check_vma=False,
    )
```

time: 1120 us -> 507 us (0.45)
  matrix products: 374 us -> 0 us
  blocking collectives: 234 us -> 0 us
  Pallas kernels: 0 us -> 210 us
  local copies, waits for them, and re-layouts: 131 us -> 14.1 us
  waiting for transfers between devices: 325 us -> 209 us
  starting transfers between devices: 6.56 us -> 62.4 us
  other arithmetic: 25.9 us -> 4 us
  between operations: 15.5 us -> 1.2 us
    dot_general x9 -> x0, matrix products: 374 us -> none  [the longest x2 168 us: shards(): jnp.einsum('pjk,kl->pjl', current, step_full, precision=highest)]
    pallas_call x0 -> x14, Pallas kernels: none -> 210 us  [the longest x2 43.2 us: make_step(): pl.pallas_call(functools.partial(kernel, devices), in_specs=[pl.BlockSpec...]
    ppermute x0 -> x57, waiting for transfers between devices: none -> 209 us  [the longest x49 164 us: swap(): return lax.ppermute(x, 'row', [(i, i ^ k) for i in range(count)])]
    all_to_all x1 -> x0, blocking collectives: 187 us -> none  [shards(): lax.all_to_all(product_left, 'row', split_axis=2, concat_axis=1, tiled=True)]
    all_to_all x1 -> x0, waiting for transfers between devices: 178 us -> none  [shards(): lax.all_to_all(product_left, 'row', split_axis=2, concat_axis=1, tiled=True)]
    psum x2 -> x0, waiting for transfers between devices: 77.7 us -> none  [shards(): gradient = lax.psum(own_part - other_part, 'vec')]
    all_to_all x4 -> x0, local copies, waits for them, and re-layouts: 73.1 us -> none  [shards(): lax.all_to_all(product_left, 'row', split_axis=2, concat_axis=1, tiled=True)]
    all_gather x2 -> x0, waiting for transfers between devices: 69 us -> none  [shards(): generator_full = lax.all_gather(generator, 'row', axis=0, tiled=True)]
  transfers between devices with their start and end apart: 5 -> 57, of which waited for: 5 -> 29; matrix products, arithmetic and copies ran while one was open for 0% -> 2% of each run, Pallas kernels for 0% -> 25%
where the time goes in v1:
time: 507 us; the launch traced here: 500 us
  Pallas kernels  210 us (41%)
  waiting for transfers between devices  209 us (41%)
  starting transfers between devices  62.4 us (12%)
  local copies, waits for them, and re-layouts  14.1 us (3%)
    ppermute x49, waiting for transfers between devices, swap(): return lax.ppermute(x, 'row', [(i, i ^ k) for i in range(count)])  164 us
    ppermute x49, starting transfers between devices, swap(): return lax.ppermute(x, 'row', [(i, i ^ k) for i in range(count)])  47.6 us
    ppermute x8, waiting for transfers between devices, flip(): return lax.ppermute(x, 'vec', [(i, i ^ k) for i in range(count)])  44.5 us
    pallas_call x2, Pallas kernels, make_step(): pl.pallas_call(functools.partial(kernel, devices), in_specs=[pl.BlockSpec...  43.2 us
    pallas_call x3, Pallas kernels, shared_pieces(): pl.pallas_call(functools.partial(shared_pieces_kernel, near, rows), grid=...  39.9 us
    pallas_call x3, Pallas kernels, shared_rotated(): pl.pallas_call(functools.partial(shared_rotated_kernel, orders), grid=(4,...  34.6 us
    pallas_call x1, Pallas kernels, first_product(): pl.pallas_call(lambda me_ref, *refs: first_product_kernel(*refs), grid_sp...  34 us
    pallas_call x1, Pallas kernels, compose(): pl.pallas_call(functools.partial(compose_kernel, devices), in_specs=[pl.B...  15.5 us
  transfers between devices with their start and end apart: 57, of which 29 were waited for; matrix products, arithmetic and copies ran while one was open for 2% of the time, Pallas kernels for 25%

profile of v1, /device:TPU:0, one launch (start us, length us, event | category | flops | bytes accessed | tf_op | source)
XLA Modules:
  0.0 499.9 jit_solution(5027066629183054121)
XLA Ops:
  0.6 9.2 %gradient_terms.1 = f32[128,1024]{1,0:T(8,128)} custom-call(s32[1]{0:T(128)} %bitcast.me_ref, f32[32,128,1024]{2,1,0:T(8,128)} %own.5, f32[32,128,1024]{2,1,0:T(8,128)} %own.5), custom_call_target="tpu_custom_call" | custom-call | flops 8388608 | bytes 16777216 | tf_op jit(solution)/shard_map/gradient_terms/pallas_call | solution.py:156
  10.9 3.1 collective-permute-start
  14.0 2.5 collective-permute-start.2
  16.5 4.2 collective-permute-done
  20.7 7.5 %collective-permute-done.2 = f32[64,1024]{1,0:T(8,128)S(1)} collective-permute-done((f32[64,1024]{1,0:T(8,128)S(1)}, f32[64,1024]{1,0:T(8,128)S(1)}, u32[]{:S(2)}, u32[]{:S(2)}) %collective-permute-start.2) | collective-permute-done | bytes 262176 | tf_op jit(solution)/shard_map/ppermute | solution.py:509
  30.9 2.2 collective-permute-start.3
  33.1 7.4 %collective-permute-done.1 = f32[64,1024]{1,0:T(8,128)S(1)} collective-permute-done((f32[64,1024]{1,0:T(8,128)S(1)}, f32[64,1024]{1,0:T(8,128)S(1)}, u32[]{:S(2)}, u32[]{:S(2)}) %collective-permute-start.1) | collective-permute-done | bytes 262176 | tf_op jit(solution)/shard_map/ppermute | solution.py:509
  40.5 2.7 collective-permute-done.3
  43.3 2.5 collective-permute-start.9
  46.9 12.2 %collective-permute-done.9.refs_6_ = f32[128,1024]{1,0:T(8,128)S(1)} collective-permute-done((f32[128,1024]{1,0:T(8,128)S(1)}, f32[128,1024]{1,0:T(8,128)S(1)}, u32[]{:S(2)}, u32[]{:S(2)}) %collective-permute-start.9) | collective-permute-done | bytes 524320 | tf_op jit(solution)/shard_map/ppermute | solution.py:18
  59.1 9.5 %collective-permute-done.7.refs_4_ = f32[128,1024]{1,0:T(8,128)S(1)} collective-permute-done((f32[128,1024]{1,0:T(8,128)S(1)}, f32[128,1024]{1,0:T(8,128)S(1)}, u32[]{:S(2)}, u32[]{:S(2)}) %collective-permute-start.7) | collective-permute-done | bytes 524320 | tf_op jit(solution)/shard_map/ppermute | solution.py:18
  71.5 16.8 %shard_map.30 = (bf16[1024,1024]{1,0:T(8,128)(2,1)}, bf16[1024,1024]{1,0:T(8,128)(2,1)}, bf16[1024,1024]{1,0:T(8,128)(2,1)}, bf16[1024,1024]{1,0:T(8,128)(2,1)}) custom-call(s32[1]{0:T(128)} %bitcast.me_ref, f32[128,1024]{1,0:T(8,128)} %copy-done.12, f32[128,1024]{1,0:T(8,128)} %copy-done.23, f32[128,1024]{1,0:T(8,128)} %copy-done.22, ...), custom_call_target="tpu_custom_call" | custom-call | flops 12884901888 | bytes 25165824 | tf_op jit(solution)/shard_map/pallas_call | solution.py:256
  88.3 34.0 %first_product.1 = (bf16[32,128,1024]{2,1,0:T(8,128)(2,1)}, bf16[32,128,1024]{2,1,0:T(8,128)(2,1)}, f32[32,1024]{1,0:T(8,128)}) custom-call(s32[1]{0:T(128)} %bitcast.me_ref, f32[32,128,1024]{2,1,0:T(8,128)} %own.5, bf16[1024,1024]{1,0:T(8,128)(2,1)} %get-tuple-element.62.refs_1_.refs_3_.left_upper, ...), custom_call_target="tpu_custom_call" | custom-call | flops 25769803776 | bytes 33554432 | tf_op jit(solution)/shard_map/first_product/pallas_call | solution.py:329
  128.4 3.8 collective-permute-done.14
  134.3 10.5 %second_terms.1 = f32[128,1024]{1,0:T(8,128)} custom-call(bf16[32,128,1024]{2,1,0:T(8,128)(2,1)} %get-tuple-element.64.upper_ref.left_upper, bf16[32,128,1024]{2,1,0:T(8,128)(2,1)} %get-tuple-element.65.lower_ref.left_lower, f32[32,1024]{1,0:T(8,128)} %add_add_fusion.diagonal_ref), custom_call_target="tpu_custom_call" | custom-call | flops 8388608 | bytes 16777216 | tf_op jit(solution)/shard_map/second_terms/pallas_call | solution.py:496
  145.9 2.9 collective-permute-start.17
  148.8 4.9 collective-permute-done.15
  153.7 6.7 %collective-permute-done.17 = f32[64,1024]{1,0:T(8,128)S(1)} collective-permute-done((f32[64,1024]{1,0:T(8,128)S(1)}, f32[64,1024]{1,0:T(8,128)S(1)}, u32[]{:S(2)}, u32[]{:S(2)}) %collective-permute-start.17) | collective-permute-done | bytes 262176 | tf_op jit(solution)/shard_map/ppermute | solution.py:509
  161.6 1.7 collective-permute-start.16
  164.1 8.5 %collective-permute-done.16 = f32[64,1024]{1,0:T(8,128)S(1)} collective-permute-done((f32[64,1024]{1,0:T(8,128)S(1)}, f32[64,1024]{1,0:T(8,128)S(1)}, u32[]{:S(2)}, u32[]{:S(2)}) %collective-permute-start.16) | collective-permute-done | bytes 262176 | tf_op jit(solution)/shard_map/ppermute | solution.py:509
  172.6 2.4 collective-permute-done.18
  175.2 2.2 collective-permute-start.24
  178.7 12.2 %collective-permute-done.24.refs_6_ = f32[128,1024]{1,0:T(8,128)S(1)} collective-permute-done((f32[128,1024]{1,0:T(8,128)S(1)}, f32[128,1024]{1,0:T(8,128)S(1)}, u32[]{:S(2)}, u32[]{:S(2)}) %collective-permute-start.24) | collective-permute-done | bytes 524320 | tf_op jit(solution)/shard_map/ppermute | solution.py:18
  191.0 9.2 %collective-permute-done.22.refs_4_ = f32[128,1024]{1,0:T(8,128)S(1)} collective-permute-done((f32[128,1024]{1,0:T(8,128)S(1)}, f32[128,1024]{1,0:T(8,128)S(1)}, u32[]{:S(2)}, u32[]{:S(2)}) %collective-permute-start.22) | collective-permute-done | bytes 524320 | tf_op jit(solution)/shard_map/ppermute | solution.py:18
  200.6 9.5 %fusion = (f32[4,128,1024]{2,1,0:T(8,128)}, f32[4,128,1024]{2,1,0:T(8,128)}, f32[4,128,1024]{2,1,0:T(8,128)}, f32[4,128,1024]{2,1,0:T(8,128)}, f32[4,128,1024]{2,1,0:T(8,128)S(1)}, /*index=5*/f32[4,128,1024]{2,1,0:T(8,128)}) fusion(f32[32,128,1024]{2,1,0:T(8,128)} %own.5), kind=kLoop, calls=%fused_computation.7 | loop fusion | bytes 25165824 | tf_op jit(solution)/shard_map/slice | solution.py:552
  210.2 1.8 collective-permute-start.28
  215.1 26.3 %shard_map.31 = (bf16[1024,1024]{1,0:T(8,128)(2,1)}, bf16[1024,1024]{1,0:T(8,128)(2,1)}, bf16[1024,1024]{1,0:T(8,128)(2,1)}, bf16[1024,1024]{1,0:T(8,128)(2,1)}) custom-call(s32[1]{0:T(128)} %bitcast.me_ref, f32[128,1024]{1,0:T(8,128)} %copy-done.11, f32[128,1024]{1,0:T(8,128)} %copy-done.16, f32[128,1024]{1,0:T(8,128)} %copy-done.15, ...), custom_call_target="tpu_custom_call" | custom-call | flops 12884901888 | bytes 25165824 | tf_op jit(solution)/shard_map/pallas_call | solution.py:256
  241.5 11.1 %plain_pieces.1 = (f32[8,128,128]{2,1,0:T(8,128)}, f32[8,128,128]{2,1,0:T(8,128)}, f32[8,128,128]{2,1,0:T(8,128)}, f32[8,128,128]{2,1,0:T(8,128)}, f32[8,128,128...) custom-call(bf16[32,128,1024]{2,1,0:T(8,128)(2,1)} %get-tuple-element.64.upper_ref.left_upp, ...), custom_call_target="tpu_custom_call" | custom-call | flops 6442450944 | bytes 8388608 | tf_op jit(solution)/shard_map/plain_pieces/pallas_call | solution.py:356
  252.7 6.4 %collective-permute-done.28.one = f32[4,128,1024]{2,1,0:T(8,128)} collective-permute-done((f32[4,128,1024]{2,1,0:T(8,128)}, f32[4,128,1024]{2,1,0:T(8,128)}, u32[]{:S(2)}, u32[]{:S(2)}) %collective-permute-start.28) | collective-permute-done | bytes 2097184 | tf_op jit(solution)/shard_map/ppermute | solution.py:18
  259.0 1.7 collective-permute-start.26
  261.4 15.5 %compose.1 = (bf16[1024,1024]{1,0:T(8,128)(2,1)}, bf16[1024,1024]{1,0:T(8,128)(2,1)}, bf16[1024,1024]{1,0:T(8,128)(2,1)}, bf16[1024,1024]{1,0:T(8,128)(2,1)}, f32[128,1024]{1,0:T(8,128)}) custom-call(s32[1]{0:T(128)} %bitcast.me_ref, bf16[1024,1024]{1,0:T(8,128)(2,1)} %get-tuple-element.62.refs_1_.refs_3_.left_upper, ...), custom_call_target="tpu_custom_call" | custom-call | flops 6442450944 | bytes 16777216 | tf_op jit(solution)/shard_map/compose/pallas_call | solution.py:297
  276.9 27.1 %collective-permute-done.30.one = f32[4,128,1024]{2,1,0:T(8,128)} collective-permute-done((f32[4,128,1024]{2,1,0:T(8,128)}, f32[4,128,1024]{2,1,0:T(8,128)}, u32[]{:S(2)}, u32[]{:S(2)}) %collective-permute-start.30) | collective-permute-done | bytes 2097184 | tf_op jit(solution)/shard_map/ppermute | solution.py:18
  304.0 1.9 collective-permute-start.51
  306.4 13.3 %shared_pieces.3 = (f32[4,2,128,128]{3,2,1,0:T(8,128)}, f32[4,2,128,128]{3,2,1,0:T(8,128)}, f32[4,2,128,128]{3,2,1,0:T(8,128)}, f32[4,2,128,128]{3,2,1,0:T(8,128...) custom-call(f32[32,128,1024]{2,1,0:T(8,128)} %own.5, ...), custom_call_target="tpu_custom_call" | custom-call | flops 6442450944 | bytes 8388608 | tf_op jit(solution)/shard_map/shared_pieces/pallas_call | solution.py:405
  319.7 42.1 %collective-permute-done.51.refs_2_ = f32[8,128,128]{2,1,0:T(8,128)S(1)} collective-permute-done((f32[8,128,128]{2,1,0:T(8,128)}, f32[8,128,128]{2,1,0:T(8,128)S(1)}, u32[]{:S(2)}, u32[]{:S(2)}) %collective-permute-start.51) | collective-permute-done | bytes 524320 | tf_op jit(solution)/shard_map/ppermute | solution.py:18
  361.8 9.2 %collective-permute-done.52.refs_3_ = f32[8,128,128]{2,1,0:T(8,128)} collective-permute-done((f32[8,128,128]{2,1,0:T(8,128)}, f32[8,128,128]{2,1,0:T(8,128)}, u32[]{:S(2)}, u32[]{:S(2)}) %collective-permute-start.52) | collective-permute-done | bytes 524320 | tf_op jit(solution)/shard_map/ppermute | solution.py:18
  372.6 1.8 collective-permute-start.56
  374.5 13.3 %shared_pieces.4 = (f32[4,2,128,128]{3,2,1,0:T(8,128)}, f32[4,2,128,128]{3,2,1,0:T(8,128)}, f32[4,2,128,128]{3,2,1,0:T(8,128)}, f32[4,2,128,128]{3,2,1,0:T(8,128...) custom-call(f32[32,128,1024]{2,1,0:T(8,128)} %own.5, ...), custom_call_target="tpu_custom_call" | custom-call | flops 6442450944 | bytes 8388608 | tf_op jit(solution)/shard_map/shared_pieces/pallas_call | solution.py:405
  387.9 11.5 %collective-permute-start.39 = (f32[4,2,128,128]{3,2,1,0:T(8,128)}, f32[4,2,128,128]{3,2,1,0:T(8,128)S(1)}, u32[]{:S(2)}, u32[]{:S(2)}) collective-permute-start(f32[4,2,128,128]{3,2,1,0:T(8,128)} %get-tuple-element.105), channel_id=1, source_target_pairs={{0,2},{1,3},{2,0},{3,1},{4,6},{5,7},{6,4},{7,5},{8,10},{9,11},{10,... | collective-permute-start | bytes 1572872 | tf_op jit(solution)/shard_map/ppermute | solution.py:18
  399.5 11.5 %plain_rotated.1.refs_8_ = f32[32,128,1024]{2,1,0:T(8,128)} custom-call(bf16[1024,1024]{1,0:T(8,128)(2,1)} %get-tuple-element.83.upper, bf16[1024,1024]{1,0:T(8,128)(2,1)} %get-tuple-element.84.lower, f32[8,128,128]{2,1,0:T(8,128)} %get-tuple-element.73.refs_0_, f32[8,128,128]{2,1,0:T(8,128)} %copy-done.9, f32[8,128,128]{2,1,0:T(8,128)} %copy-done.10, ...), custom_call_target="tpu_custom_call" | custom-call | flops 6442450944 | bytes 8388608 | tf_op jit(solution)/shard_map/plain_rotated/pallas_call | solution.py:430
  415.4 13.3 %shared_pieces.5 = (f32[4,2,128,128]{3,2,1,0:T(8,128)}, f32[4,2,128,128]{3,2,1,0:T(8,128)}, f32[4,2,128,128]{3,2,1,0:T(8,128)}, f32[4,2,128,128]{3,2,1,0:T(8,128...) custom-call(f32[32,128,1024]{2,1,0:T(8,128)} %own.5, ...), custom_call_target="tpu_custom_call" | custom-call | flops 6442450944 | bytes 8388608 | tf_op jit(solution)/shard_map/shared_pieces/pallas_call | solution.py:405
  429.3 6.9 %collective-permute-done.46.refs_3_ = f32[4,2,128,128]{3,2,1,0:T(8,128)} collective-permute-done((f32[4,2,128,128]{3,2,1,0:T(8,128)}, f32[4,2,128,128]{3,2,1,0:T(8,128)}, u32[]{:S(2)}, u32[]{:S(2)}) %collective-permute-start.46) | collective-permute-done | bytes 524320 | tf_op jit(solution)/shard_map/ppermute | solution.py:18
  440.4 11.5 %shared_rotated.3.refs_8_ = f32[32,128,1024]{2,1,0:T(8,128)} custom-call(bf16[1024,1024]{1,0:T(8,128)(2,1)} %get-tuple-element.83.upper, bf16[1024,1024]{1,0:T(8,128)(2,1)} %get-tuple-element.84.lower, f32[4,2,128,128]{3,2,1,0:T(8,128)} %get-tuple-element.91.refs_0_, ...), custom_call_target="tpu_custom_call", output_to_operand_aliasing={{}: (10, {})} | custom-call | flops 6442450944 | bytes 8388608 | tf_op jit(solution)/shard_map/shared_rotated/pallas_call | solution.py:468
  454.2 7.6 %collective-permute-done.43.refs_7_ = f32[4,2,128,128]{3,2,1,0:T(8,128)S(1)} collective-permute-done((f32[4,2,128,128]{3,2,1,0:T(8,128)}, f32[4,2,128,128]{3,2,1,0:T(8,128)S(1)}, u32[]{:S(2)}, u32[]{:S(2)}) %collective-permute-start.43) | collective-permute-done | bytes 524320 | tf_op jit(solution)/shard_map/ppermute | solution.py:18
  462.4 1.8 collective-permute-start.37
  464.2 11.6 %shared_rotated.4.refs_8_ = f32[32,128,1024]{2,1,0:T(8,128)} custom-call(bf16[1024,1024]{1,0:T(8,128)(2,1)} %get-tuple-element.83.upper, bf16[1024,1024]{1,0:T(8,128)(2,1)} %get-tuple-element.84.lower, f32[4,2,128,128]{3,2,1,0:T(8,128)} %get-tuple-element.103.refs_0_, f32[4,2,128,128]{3,2,1,0:T(8,128)} %copy-done, ...), custom_call_target="tpu_custom_call", output_to_operand_aliasing={{}: (10, {})} | custom-call | flops 6442450944 | bytes 8388608 | tf_op jit(solution)/shard_map/shared_rotated/pallas_call | solution.py:468
  476.8 11.4 %collective-permute-done.37.refs_7_ = f32[4,2,128,128]{3,2,1,0:T(8,128)} collective-permute-done((f32[4,2,128,128]{3,2,1,0:T(8,128)}, f32[4,2,128,128]{3,2,1,0:T(8,128)}, u32[]{:S(2)}, u32[]{:S(2)}) %collective-permute-start.37) | collective-permute-done | bytes 524320 | tf_op jit(solution)/shard_map/ppermute | solution.py:18
  488.1 11.5 %shared_rotated.5 = f32[32,128,1024]{2,1,0:T(8,128)} custom-call(bf16[1024,1024]{1,0:T(8,128)(2,1)} %get-tuple-element.83.upper, bf16[1024,1024]{1,0:T(8,128)(2,1)} %get-tuple-element.84.lower, f32[4,2,128,128]{3,2,1,0:T(8,128)} %get-tuple-element.113.refs_0_, f32[4,2,128,128]{3,2,1,0:T(8,128)} %copy-done.3, ...), custom_call_target="tpu_custom_call", output_to_operand_aliasing={{}: (10, {})} | custom-call | flops 6442450944 | bytes 8388608 | tf_op jit(solution)/shard_map/shared_rotated/pallas_call | solution.py:468
  (145 shorter events, 39.9 us)
Async XLA Ops:
  14.0 14.2 %collective-permute-start.2 = (f32[64,1024]{1,0:T(8,128)S(1)}, f32[64,1024]{1,0:T(8,128)S(1)}, u32[]{:S(2)}, u32[]{:S(2)}) collective-permute-start(f32[64,1024]{1,0:T(8,128)S(1)} %get-tuple-element.135), channel_id=1, source_target_pairs={{0,24},{8,16},{16,8},{24,0},{1,25},{9,17},{17,9},{25,1},{2,26},{10... | collective-permute-start | bytes 786440 | tf_op jit(solution)/shard_map/ppermute | solution.py:509
  29.4 11.1 %collective-permute-start.1 = (f32[64,1024]{1,0:T(8,128)S(1)}, f32[64,1024]{1,0:T(8,128)S(1)}, u32[]{:S(2)}, u32[]{:S(2)}) collective-permute-start(f32[64,1024]{1,0:T(8,128)S(1)} %get-tuple-element.132), channel_id=1, source_target_pairs={{0,24},{8,16},{16,8},{24,0},{1,25},{9,17},{17,9},{25,1},{2,26},{10... | collective-permute-start | bytes 786440 | tf_op jit(solution)/shard_map/ppermute | solution.py:509
  30.9 12.3 %collective-permute-start.3 = (f32[64,1024]{1,0:T(8,128)S(1)}, f32[64,1024]{1,0:T(8,128)S(1)}, u32[]{:S(2)}, u32[]{:S(2)}) collective-permute-start(f32[64,1024]{1,0:T(8,128)S(1)} %get-tuple-element.133), channel_id=1, source_target_pairs={{0,8},{8,0},{16,24},{24,16},{1,9},{9,1},{17,25},{25,17},{2,10},{10... | collective-permute-start | bytes 786440 | tf_op jit(solution)/shard_map/ppermute | solution.py:509
  43.3 15.8 %collective-permute-start.9 = (f32[128,1024]{1,0:T(8,128)S(1)}, f32[128,1024]{1,0:T(8,128)S(1)}, u32[]{:S(2)}, u32[]{:S(2)}) collective-permute-start(f32[128,1024]{1,0:T(8,128)S(1)} %pad_maximum_fusion.refs_0_), channel_id=1, source_target_pairs={{0,6},{1,7},{2,4},{3,5},{4,2},{5,3},{6,0},{7,1},{8,14},{9,15},{10,... | collective-permute-start | bytes 1572872 | tf_op jit(solution)/shard_map/ppermute | solution.py:18
  45.8 22.8 %collective-permute-start.7 = (f32[128,1024]{1,0:T(8,128)S(1)}, f32[128,1024]{1,0:T(8,128)S(1)}, u32[]{:S(2)}, u32[]{:S(2)}) collective-permute-start(f32[128,1024]{1,0:T(8,128)S(1)} %pad_maximum_fusion.refs_0_), channel_id=1, source_target_pairs={{0,4},{1,5},{2,6},{3,7},{4,0},{5,1},{6,2},{7,3},{8,12},{9,13},{10,... | collective-permute-start | bytes 1572872 | tf_op jit(solution)/shard_map/ppermute | solution.py:18
  46.4 22.4 %collective-permute-start.5 = (f32[128,1024]{1,0:T(8,128)S(1)}, f32[128,1024]{1,0:T(8,128)S(1)}, u32[]{:S(2)}, u32[]{:S(2)}) collective-permute-start(f32[128,1024]{1,0:T(8,128)S(1)} %pad_maximum_fusion.refs_0_), channel_id=1, source_target_pairs={{0,2},{1,3},{2,0},{3,1},{4,6},{5,7},{6,4},{7,5},{8,10},{9,11},{10,... | collective-permute-start | bytes 1572872 | tf_op jit(solution)/shard_map/ppermute | solution.py:18
  46.9 22.3 %collective-permute-start.4 = (f32[128,1024]{1,0:T(8,128)S(1)}, f32[128,1024]{1,0:T(8,128)S(1)}, u32[]{:S(2)}, u32[]{:S(2)}) collective-permute-start(f32[128,1024]{1,0:T(8,128)S(1)} %pad_maximum_fusion.refs_0_), channel_id=1, source_target_pairs={{0,1},{1,0},{2,3},{3,2},{4,5},{5,4},{6,7},{7,6},{8,9},{9,8},{10,11... | collective-permute-start | bytes 1572872 | tf_op jit(solution)/shard_map/ppermute | solution.py:18
  145.9 14.5 %collective-permute-start.17 = (f32[64,1024]{1,0:T(8,128)S(1)}, f32[64,1024]{1,0:T(8,128)S(1)}, u32[]{:S(2)}, u32[]{:S(2)}) collective-permute-start(f32[64,1024]{1,0:T(8,128)S(1)} %get-tuple-element.131), channel_id=1, source_target_pairs={{0,24},{8,16},{16,8},{24,0},{1,25},{9,17},{17,9},{25,1},{2,26},{10... | collective-permute-start | bytes 786440 | tf_op jit(solution)/shard_map/ppermute | solution.py:509
  161.6 11.0 %collective-permute-start.16 = (f32[64,1024]{1,0:T(8,128)S(1)}, f32[64,1024]{1,0:T(8,128)S(1)}, u32[]{:S(2)}, u32[]{:S(2)}) collective-permute-start(f32[64,1024]{1,0:T(8,128)S(1)} %get-tuple-element.128), channel_id=1, source_target_pairs={{0,24},{8,16},{16,8},{24,0},{1,25},{9,17},{17,9},{25,1},{2,26},{10... | collective-permute-start | bytes 786440 | tf_op jit(solution)/shard_map/ppermute | solution.py:509
  163.3 11.8 %collective-permute-start.18 = (f32[64,1024]{1,0:T(8,128)S(1)}, f32[64,1024]{1,0:T(8,128)S(1)}, u32[]{:S(2)}, u32[]{:S(2)}) collective-permute-start(f32[64,1024]{1,0:T(8,128)S(1)} %get-tuple-element.129), channel_id=1, source_target_pairs={{0,8},{8,0},{16,24},{24,16},{1,9},{9,1},{17,25},{25,17},{2,10},{10... | collective-permute-start | bytes 786440 | tf_op jit(solution)/shard_map/ppermute | solution.py:509
  175.2 15.8 %collective-permute-start.24 = (f32[128,1024]{1,0:T(8,128)S(1)}, f32[128,1024]{1,0:T(8,128)S(1)}, u32[]{:S(2)}, u32[]{:S(2)}) collective-permute-start(f32[128,1024]{1,0:T(8,128)S(1)} %pad_maximum_fusion.1.refs_0_), channel_id=1, source_target_pairs={{0,6},{1,7},{2,4},{3,5},{4,2},{5,3},{6,0},{7,1},{8,14},{9,15},{10,... | collective-permute-start | bytes 1572872 | tf_op jit(solution)/shard_map/ppermute | solution.py:18
  177.4 22.7 %collective-permute-start.22 = (f32[128,1024]{1,0:T(8,128)S(1)}, f32[128,1024]{1,0:T(8,128)S(1)}, u32[]{:S(2)}, u32[]{:S(2)}) collective-permute-start(f32[128,1024]{1,0:T(8,128)S(1)} %pad_maximum_fusion.1.refs_0_), channel_id=1, source_target_pairs={{0,4},{1,5},{2,6},{3,7},{4,0},{5,1},{6,2},{7,3},{8,12},{9,13},{10,... | collective-permute-start | bytes 1572872 | tf_op jit(solution)/shard_map/ppermute | solution.py:18
  178.6 21.9 %collective-permute-start.20 = (f32[128,1024]{1,0:T(8,128)S(1)}, f32[128,1024]{1,0:T(8,128)S(1)}, u32[]{:S(2)}, u32[]{:S(2)}) collective-permute-start(f32[128,1024]{1,0:T(8,128)S(1)} %pad_maximum_fusion.1.refs_0_), channel_id=1, source_target_pairs={{0,2},{1,3},{2,0},{3,1},{4,6},{5,7},{6,4},{7,5},{8,10},{9,11},{10,... | collective-permute-start | bytes 1572872 | tf_op jit(solution)/shard_map/ppermute | solution.py:18
  178.7 33.3 %collective-permute-start.19 = (f32[128,1024]{1,0:T(8,128)S(1)}, f32[128,1024]{1,0:T(8,128)S(1)}, u32[]{:S(2)}, u32[]{:S(2)}) collective-permute-start(f32[128,1024]{1,0:T(8,128)S(1)} %pad_maximum_fusion.1.refs_0_), channel_id=1, source_target_pairs={{0,1},{1,0},{2,3},{3,2},{4,5},{5,4},{6,7},{7,6},{8,9},{9,8},{10,11... | collective-permute-start | bytes 1572872 | tf_op jit(solution)/shard_map/ppermute | solution.py:18
  191.0 21.6 %collective-permute-start.25 = (f32[128,1024]{1,0:T(8,128)S(1)}, f32[128,1024]{1,0:T(8,128)S(1)}, u32[]{:S(2)}, u32[]{:S(2)}) collective-permute-start(f32[128,1024]{1,0:T(8,128)S(1)} %collective-permute-done.24.refs_6_), channel_id=1, source_target_pairs={{0,1},{1,0},{2,3},{3,2},{4,5},{5,4},{6,7},{7,6},{8,9},{9,8},{10,11... | collective-permute-start | bytes 1572872 | tf_op jit(solution)/shard_map/ppermute | solution.py:18
  200.1 14.0 %collective-permute-start.23 = (f32[128,1024]{1,0:T(8,128)S(1)}, f32[128,1024]{1,0:T(8,128)S(1)}, u32[]{:S(2)}, u32[]{:S(2)}) collective-permute-start(f32[128,1024]{1,0:T(8,128)S(1)} %collective-permute-done.22.refs_4_), channel_id=1, source_target_pairs={{0,1},{1,0},{2,3},{3,2},{4,5},{5,4},{6,7},{7,6},{8,9},{9,8},{10,11... | collective-permute-start | bytes 1572872 | tf_op jit(solution)/shard_map/ppermute | solution.py:18
  200.5 13.8 %collective-permute-start.21 = (f32[128,1024]{1,0:T(8,128)S(1)}, f32[128,1024]{1,0:T(8,128)S(1)}, u32[]{:S(2)}, u32[]{:S(2)}) collective-permute-start(f32[128,1024]{1,0:T(8,128)S(1)} %collective-permute-done.20.refs_2_), channel_id=1, source_target_pairs={{0,1},{1,0},{2,3},{3,2},{4,5},{5,4},{6,7},{7,6},{8,9},{9,8},{10,11... | collective-permute-start | bytes 1572872 | tf_op jit(solution)/shard_map/ppermute | solution.py:18
  210.2 48.9 %collective-permute-start.28 = (f32[4,128,1024]{2,1,0:T(8,128)}, f32[4,128,1024]{2,1,0:T(8,128)}, u32[]{:S(2)}, u32[]{:S(2)}) collective-permute-start(f32[4,128,1024]{2,1,0:T(8,128)} %get-tuple-element.89), channel_id=1, source_target_pairs={{0,4},{1,5},{2,6},{3,7},{4,0},{5,1},{6,2},{7,3},{8,12},{9,13},{10,... | collective-permute-start | bytes 6291464 | tf_op jit(solution)/shard_map/ppermute | solution.py:18
  212.0 48.8 %collective-permute-start.29 = (f32[4,128,1024]{2,1,0:T(8,128)}, f32[4,128,1024]{2,1,0:T(8,128)}, u32[]{:S(2)}, u32[]{:S(2)}) collective-permute-start(f32[4,128,1024]{2,1,0:T(8,128)} %get-tuple-element.90), channel_id=1, source_target_pairs={{0,2},{1,3},{2,0},{3,1},{4,6},{5,7},{6,4},{7,5},{8,10},{9,11},{10,... | collective-permute-start | bytes 6291464 | tf_op jit(solution)/shard_map/ppermute | solution.py:18
  212.6 91.4 %collective-permute-start.30 = (f32[4,128,1024]{2,1,0:T(8,128)}, f32[4,128,1024]{2,1,0:T(8,128)}, u32[]{:S(2)}, u32[]{:S(2)}) collective-permute-start(f32[4,128,1024]{2,1,0:T(8,128)} %get-tuple-element.101), channel_id=1, source_target_pairs={{0,4},{1,5},{2,6},{3,7},{4,0},{5,1},{6,2},{7,3},{8,12},{9,13},{10,... | collective-permute-start | bytes 6291464 | tf_op jit(solution)/shard_map/ppermute | solution.py:18
  214.1 91.7 %collective-permute-start.31 = (f32[4,128,1024]{2,1,0:T(8,128)}, f32[4,128,1024]{2,1,0:T(8,128)}, u32[]{:S(2)}, u32[]{:S(2)}) collective-permute-start(f32[4,128,1024]{2,1,0:T(8,128)} %get-tuple-element.102), channel_id=1, source_target_pairs={{0,2},{1,3},{2,0},{3,1},{4,6},{5,7},{6,4},{7,5},{8,10},{9,11},{10,... | collective-permute-start | bytes 6291464 | tf_op jit(solution)/shard_map/ppermute | solution.py:18
  252.6 53.3 %collective-permute-start.50 = (f32[8,128,128]{2,1,0:T(8,128)}, f32[8,128,128]{2,1,0:T(8,128)S(1)}, u32[]{:S(2)}, u32[]{:S(2)}) collective-permute-start(f32[8,128,128]{2,1,0:T(8,128)} %get-tuple-element.74), channel_id=1, source_target_pairs={{0,1},{1,0},{2,3},{3,2},{4,5},{5,4},{6,7},{7,6},{8,9},{9,8},{10,11... | collective-permute-start | bytes 1572872 | tf_op jit(solution)/shard_map/ppermute | solution.py:18
  259.0 154.9 %collective-permute-start.26 = (f32[4,128,1024]{2,1,0:T(8,128)}, f32[4,128,1024]{2,1,0:T(8,128)}, u32[]{:S(2)}, u32[]{:S(2)}) collective-permute-start(f32[4,128,1024]{2,1,0:T(8,128)} %get-tuple-element.85), channel_id=1, source_target_pairs={{0,4},{1,5},{2,6},{3,7},{4,0},{5,1},{6,2},{7,3},{8,12},{9,13},{10,... | collective-permute-start | bytes 6291464 | tf_op jit(solution)/shard_map/ppermute | solution.py:18
  260.8 153.1 %collective-permute-start.27 = (f32[4,128,1024]{2,1,0:T(8,128)S(1)}, f32[4,128,1024]{2,1,0:T(8,128)}, u32[]{:S(2)}, u32[]{:S(2)}) collective-permute-start(f32[4,128,1024]{2,1,0:T(8,128)S(1)} %get-tuple-element.86), channel_id=1, source_target_pairs={{0,2},{1,3},{2,0},{3,1},{4,6},{5,7},{6,4},{7,5},{8,10},{9,11},{10,... | collective-permute-start | bytes 6291464 | tf_op jit(solution)/shard_map/ppermute | solution.py:18
  304.0 57.8 %collective-permute-start.51 = (f32[8,128,128]{2,1,0:T(8,128)}, f32[8,128,128]{2,1,0:T(8,128)S(1)}, u32[]{:S(2)}, u32[]{:S(2)}) collective-permute-start(f32[8,128,128]{2,1,0:T(8,128)} %get-tuple-element.75), channel_id=1, source_target_pairs={{0,2},{1,3},{2,0},{3,1},{4,6},{5,7},{6,4},{7,5},{8,10},{9,11},{10,... | collective-permute-start | bytes 1572872 | tf_op jit(solution)/shard_map/ppermute | solution.py:18
  305.9 65.2 %collective-permute-start.52 = (f32[8,128,128]{2,1,0:T(8,128)}, f32[8,128,128]{2,1,0:T(8,128)}, u32[]{:S(2)}, u32[]{:S(2)}) collective-permute-start(f32[8,128,128]{2,1,0:T(8,128)} %get-tuple-element.76), channel_id=1, source_target_pairs={{0,3},{1,2},{2,1},{3,0},{4,7},{5,6},{6,5},{7,4},{8,11},{9,10},{10,... | collective-permute-start | bytes 1572872 | tf_op jit(solution)/shard_map/ppermute | solution.py:18
  305.9 66.7 %collective-permute-start.53 = (f32[8,128,128]{2,1,0:T(8,128)}, f32[8,128,128]{2,1,0:T(8,128)}, u32[]{:S(2)}, u32[]{:S(2)}) collective-permute-start(f32[8,128,128]{2,1,0:T(8,128)} %get-tuple-element.77), channel_id=1, source_target_pairs={{0,4},{1,5},{2,6},{3,7},{4,0},{5,1},{6,2},{7,3},{8,12},{9,13},{10,... | collective-permute-start | bytes 1572872 | tf_op jit(solution)/shard_map/ppermute | solution.py:18
  361.8 25.9 %collective-permute-start.54 = (f32[8,128,128]{2,1,0:T(8,128)}, f32[8,128,128]{2,1,0:T(8,128)}, u32[]{:S(2)}, u32[]{:S(2)}) collective-permute-start(f32[8,128,128]{2,1,0:T(8,128)} %get-tuple-element.78), channel_id=1, source_target_pairs={{0,5},{1,4},{2,7},{3,6},{4,1},{5,0},{6,3},{7,2},{8,13},{9,12},{10,... | collective-permute-start | bytes 1572872 | tf_op jit(solution)/shard_map/ppermute | solution.py:18
  371.0 16.8 %collective-permute-start.55 = (f32[8,128,128]{2,1,0:T(8,128)}, f32[8,128,128]{2,1,0:T(8,128)}, u32[]{:S(2)}, u32[]{:S(2)}) collective-permute-start(f32[8,128,128]{2,1,0:T(8,128)} %get-tuple-element.79), channel_id=1, source_target_pairs={{0,6},{1,7},{2,4},{3,5},{4,2},{5,3},{6,0},{7,1},{8,14},{9,15},{10,... | collective-permute-start | bytes 1572872 | tf_op jit(solution)/shard_map/ppermute | solution.py:18
  372.6 26.8 %collective-permute-start.56 = (f32[8,128,128]{2,1,0:T(8,128)}, f32[8,128,128]{2,1,0:T(8,128)}, u32[]{:S(2)}, u32[]{:S(2)}) collective-permute-start(f32[8,128,128]{2,1,0:T(8,128)} %get-tuple-element.80), channel_id=1, source_target_pairs={{0,7},{1,6},{2,5},{3,4},{4,3},{5,2},{6,1},{7,0},{8,15},{9,14},{10,... | collective-permute-start | bytes 1572872 | tf_op jit(solution)/shard_map/ppermute | solution.py:18
  387.8 23.2 %collective-permute-start.38 = (f32[4,2,128,128]{3,2,1,0:T(8,128)}, f32[4,2,128,128]{3,2,1,0:T(8,128)S(1)}, u32[]{:S(2)}, u32[]{:S(2)}) collective-permute-start(f32[4,2,128,128]{3,2,1,0:T(8,128)} %get-tuple-element.104), channel_id=1, source_target_pairs={{0,1},{1,0},{2,3},{3,2},{4,5},{5,4},{6,7},{7,6},{8,9},{9,8},{10,11... | collective-permute-start | bytes 1572872 | tf_op jit(solution)/shard_map/ppermute | solution.py:18
  387.9 24.2 %collective-permute-start.39 = (f32[4,2,128,128]{3,2,1,0:T(8,128)}, f32[4,2,128,128]{3,2,1,0:T(8,128)S(1)}, u32[]{:S(2)}, u32[]{:S(2)}) collective-permute-start(f32[4,2,128,128]{3,2,1,0:T(8,128)} %get-tuple-element.105), channel_id=1, source_target_pairs={{0,2},{1,3},{2,0},{3,1},{4,6},{5,7},{6,4},{7,5},{8,10},{9,11},{10,... | collective-permute-start | bytes 1572872 | tf_op jit(solution)/shard_map/ppermute | solution.py:18
  399.4 13.6 %collective-permute-start.44 = (f32[4,2,128,128]{3,2,1,0:T(8,128)}, f32[4,2,128,128]{3,2,1,0:T(8,128)}, u32[]{:S(2)}, u32[]{:S(2)}) collective-permute-start(f32[4,2,128,128]{3,2,1,0:T(8,128)} %get-tuple-element.92), channel_id=1, source_target_pairs={{0,1},{1,0},{2,3},{3,2},{4,5},{5,4},{6,7},{7,6},{8,9},{9,8},{10,11... | collective-permute-start | bytes 1572872 | tf_op jit(solution)/shard_map/ppermute | solution.py:18
  411.0 17.6 %collective-permute-start.45 = (f32[4,2,128,128]{3,2,1,0:T(8,128)}, f32[4,2,128,128]{3,2,1,0:T(8,128)}, u32[]{:S(2)}, u32[]{:S(2)}) collective-permute-start(f32[4,2,128,128]{3,2,1,0:T(8,128)} %get-tuple-element.93), channel_id=1, source_target_pairs={{0,2},{1,3},{2,0},{3,1},{4,6},{5,7},{6,4},{7,5},{8,10},{9,11},{10,... | collective-permute-start | bytes 1572872 | tf_op jit(solution)/shard_map/ppermute | solution.py:18
  412.1 24.2 %collective-permute-start.46 = (f32[4,2,128,128]{3,2,1,0:T(8,128)}, f32[4,2,128,128]{3,2,1,0:T(8,128)}, u32[]{:S(2)}, u32[]{:S(2)}) collective-permute-start(f32[4,2,128,128]{3,2,1,0:T(8,128)} %get-tuple-element.94), channel_id=1, source_target_pairs={{0,3},{1,2},{2,1},{3,0},{4,7},{5,6},{6,5},{7,4},{8,11},{9,10},{10,... | collective-permute-start | bytes 1572872 | tf_op jit(solution)/shard_map/ppermute | solution.py:18
  413.0 24.5 %collective-permute-start.47 = (f32[4,2,128,128]{3,2,1,0:T(8,128)}, f32[4,2,128,128]{3,2,1,0:T(8,128)}, u32[]{:S(2)}, u32[]{:S(2)}) collective-permute-start(f32[4,2,128,128]{3,2,1,0:T(8,128)} %get-tuple-element.96), channel_id=1, source_target_pairs={{0,1},{1,0},{2,3},{3,2},{4,5},{5,4},{6,7},{7,6},{8,9},{9,8},{10,11... | collective-permute-start | bytes 1572872 | tf_op jit(solution)/shard_map/ppermute | solution.py:18
  413.9 23.5 %collective-permute-start.48 = (f32[4,2,128,128]{3,2,1,0:T(8,128)}, f32[4,2,128,128]{3,2,1,0:T(8,128)}, u32[]{:S(2)}, u32[]{:S(2)}) collective-permute-start(f32[4,2,128,128]{3,2,1,0:T(8,128)} %get-tuple-element.97), channel_id=1, source_target_pairs={{0,4},{1,5},{2,6},{3,7},{4,0},{5,1},{6,2},{7,3},{8,12},{9,13},{10,... | collective-permute-start | bytes 1572872 | tf_op jit(solution)/shard_map/ppermute | solution.py:18
  413.9 24.9 %collective-permute-start.49 = (f32[4,2,128,128]{3,2,1,0:T(8,128)}, f32[4,2,128,128]{3,2,1,0:T(8,128)S(1)}, u32[]{:S(2)}, u32[]{:S(2)}) collective-permute-start(f32[4,2,128,128]{3,2,1,0:T(8,128)} %get-tuple-element.98), channel_id=1, source_target_pairs={{0,5},{1,4},{2,7},{3,6},{4,1},{5,0},{6,3},{7,2},{8,13},{9,12},{10,... | collective-permute-start | bytes 1572872 | tf_op jit(solution)/shard_map/ppermute | solution.py:18
  428.7 23.3 %collective-permute-start.40 = (f32[4,2,128,128]{3,2,1,0:T(8,128)}, f32[4,2,128,128]{3,2,1,0:T(8,128)S(1)}, u32[]{:S(2)}, u32[]{:S(2)}) collective-permute-start(f32[4,2,128,128]{3,2,1,0:T(8,128)} %get-tuple-element.106), channel_id=1, source_target_pairs={{0,3},{1,2},{2,1},{3,0},{4,7},{5,6},{6,5},{7,4},{8,11},{9,10},{10,... | collective-permute-start | bytes 1572872 | tf_op jit(solution)/shard_map/ppermute | solution.py:18
  436.3 16.1 %collective-permute-start.41 = (f32[4,2,128,128]{3,2,1,0:T(8,128)}, f32[4,2,128,128]{3,2,1,0:T(8,128)S(1)}, u32[]{:S(2)}, u32[]{:S(2)}) collective-permute-start(f32[4,2,128,128]{3,2,1,0:T(8,128)} %get-tuple-element.108), channel_id=1, source_target_pairs={{0,1},{1,0},{2,3},{3,2},{4,5},{5,4},{6,7},{7,6},{8,9},{9,8},{10,11... | collective-permute-start | bytes 1572872 | tf_op jit(solution)/shard_map/ppermute | solution.py:18
  437.4 15.9 %collective-permute-start.42 = (f32[4,2,128,128]{3,2,1,0:T(8,128)}, f32[4,2,128,128]{3,2,1,0:T(8,128)S(1)}, u32[]{:S(2)}, u32[]{:S(2)}) collective-permute-start(f32[4,2,128,128]{3,2,1,0:T(8,128)} %get-tuple-element.109), channel_id=1, source_target_pairs={{0,4},{1,5},{2,6},{3,7},{4,0},{5,1},{6,2},{7,3},{8,12},{9,13},{10,... | collective-permute-start | bytes 1572872 | tf_op jit(solution)/shard_map/ppermute | solution.py:18
  437.5 24.3 %collective-permute-start.43 = (f32[4,2,128,128]{3,2,1,0:T(8,128)}, f32[4,2,128,128]{3,2,1,0:T(8,128)S(1)}, u32[]{:S(2)}, u32[]{:S(2)}) collective-permute-start(f32[4,2,128,128]{3,2,1,0:T(8,128)} %get-tuple-element.110), channel_id=1, source_target_pairs={{0,5},{1,4},{2,7},{3,6},{4,1},{5,0},{6,3},{7,2},{8,13},{9,12},{10,... | collective-permute-start | bytes 1572872 | tf_op jit(solution)/shard_map/ppermute | solution.py:18
  439.6 22.8 %collective-permute-start.32 = (f32[4,2,128,128]{3,2,1,0:T(8,128)}, f32[4,2,128,128]{3,2,1,0:T(8,128)S(1)}, u32[]{:S(2)}, u32[]{:S(2)}) collective-permute-start(f32[4,2,128,128]{3,2,1,0:T(8,128)} %get-tuple-element.114), channel_id=1, source_target_pairs={{0,1},{1,0},{2,3},{3,2},{4,5},{5,4},{6,7},{7,6},{8,9},{9,8},{10,11... | collective-permute-start | bytes 1572872 | tf_op jit(solution)/shard_map/ppermute | solution.py:18
  451.9 23.8 %collective-permute-start.33 = (f32[4,2,128,128]{3,2,1,0:T(8,128)}, f32[4,2,128,128]{3,2,1,0:T(8,128)S(1)}, u32[]{:S(2)}, u32[]{:S(2)}) collective-permute-start(f32[4,2,128,128]{3,2,1,0:T(8,128)} %get-tuple-element.115), channel_id=1, source_target_pairs={{0,2},{1,3},{2,0},{3,1},{4,6},{5,7},{6,4},{7,5},{8,10},{9,11},{10,... | collective-permute-start | bytes 1572872 | tf_op jit(solution)/shard_map/ppermute | solution.py:18
  452.4 24.1 %collective-permute-start.34 = (f32[4,2,128,128]{3,2,1,0:T(8,128)}, f32[4,2,128,128]{3,2,1,0:T(8,128)}, u32[]{:S(2)}, u32[]{:S(2)}) collective-permute-start(f32[4,2,128,128]{3,2,1,0:T(8,128)} %get-tuple-element.116), channel_id=1, source_target_pairs={{0,3},{1,2},{2,1},{3,0},{4,7},{5,6},{6,5},{7,4},{8,11},{9,10},{10,... | collective-permute-start | bytes 1572872 | tf_op jit(solution)/shard_map/ppermute | solution.py:18
  453.4 23.1 %collective-permute-start.35 = (f32[4,2,128,128]{3,2,1,0:T(8,128)}, f32[4,2,128,128]{3,2,1,0:T(8,128)}, u32[]{:S(2)}, u32[]{:S(2)}) collective-permute-start(f32[4,2,128,128]{3,2,1,0:T(8,128)} %get-tuple-element.118), channel_id=1, source_target_pairs={{0,1},{1,0},{2,3},{3,2},{4,5},{5,4},{6,7},{7,6},{8,9},{9,8},{10,11... | collective-permute-start | bytes 1572872 | tf_op jit(solution)/shard_map/ppermute | solution.py:18
  461.8 15.0 %collective-permute-start.36 = (f32[4,2,128,128]{3,2,1,0:T(8,128)}, f32[4,2,128,128]{3,2,1,0:T(8,128)}, u32[]{:S(2)}, u32[]{:S(2)}) collective-permute-start(f32[4,2,128,128]{3,2,1,0:T(8,128)} %get-tuple-element.119), channel_id=1, source_target_pairs={{0,4},{1,5},{2,6},{3,7},{4,0},{5,1},{6,2},{7,3},{8,12},{9,13},{10,... | collective-permute-start | bytes 1572872 | tf_op jit(solution)/shard_map/ppermute | solution.py:18
  462.4 25.7 %collective-permute-start.37 = (f32[4,2,128,128]{3,2,1,0:T(8,128)}, f32[4,2,128,128]{3,2,1,0:T(8,128)}, u32[]{:S(2)}, u32[]{:S(2)}) collective-permute-start(f32[4,2,128,128]{3,2,1,0:T(8,128)} %get-tuple-element.120), channel_id=1, source_target_pairs={{0,5},{1,4},{2,7},{3,6},{4,1},{5,0},{6,3},{7,2},{8,13},{9,12},{10,... | collective-permute-start | bytes 1572872 | tf_op jit(solution)/shard_map/ppermute | solution.py:18
  (35 other events, 325.0 us)

commit v2 on v1

--- a/solution.py
+++ b/solution.py
@@ -113,6 +113,8 @@
 
 
 lane = 128
+band = 256
+room = pltpu.CompilerParams(vmem_limit_bytes=28 << 20)
 quad = 4
 bf16, f32 = jnp.bfloat16, jnp.float32
 
@@ -166,6 +168,7 @@
         ),
         out_shape=jax.ShapeDtypeStruct((rows, orbitals), f32),
         cost_estimate=cost(2 * chol_vectors.size, 4 * chol_vectors.size),
+        compiler_params=room,
         name="gradient_terms",
     )(me, chol_vectors, chol_vectors)
 
@@ -181,22 +184,25 @@
     return lax.fori_loop(0, skew_ref.shape[0] // lane, body, jnp.zeros((1, 1), f32))
 
 
+def columns_of(t, width):
+    return pl.ds(pl.multiple_of(t * width, width), width)
+
+
 def step_parts(total, skew_ref, upper_ref, lower_ref, store):
     orbitals = skew_ref.shape[0]
     norm = jnp.sqrt(total / (orbitals * orbitals) + 1e-06)
     scale = step_gain / jnp.sqrt(jnp.full((1, 1), orbitals, f32)) / norm
-    tile = orbitals // 2
-
-    @pl.loop(0, 2)
+
+    @pl.loop(0, orbitals // band)
     def _(t):
-        at = pl.ds(pl.multiple_of(t * tile, tile), tile)
+        at = columns_of(t, band)
         square = product(
-            (upper_ref[at, :], lower_ref[at, :]), (upper_ref[...], lower_ref[...])
+            (upper_ref[...], lower_ref[...]), (upper_ref[:, at], lower_ref[:, at])
         )
-        row = lax.broadcasted_iota(jnp.int32, (tile, orbitals), 0) + t * tile
-        column = lax.broadcasted_iota(jnp.int32, (tile, orbitals), 1)
+        row = lax.broadcasted_iota(jnp.int32, (orbitals, band), 0)
+        column = lax.broadcasted_iota(jnp.int32, (orbitals, band), 1) + t * band
         even = jnp.where(row == column, 1.0, 0.0) + (0.5 * scale * scale) * square
-        store(at, even, scale * skew_ref[at, :])
+        store(t, at, even, scale * skew_ref[:, at])
 
 
 def first_kernel(devices, me_ref, *refs):
@@ -208,47 +214,44 @@
         terms[pl.ds(pl.multiple_of((me_ref[0] ^ k) * rows, rows), rows), :] = shards[k][...]
     total = skew_part(terms, 1.0, skew, upper, lower)
 
-    def store(at, even, odd):
-        step[0][at, :], step[1][at, :] = split(even + odd)
-        turned[0][at, :], turned[1][at, :] = split(even - odd)
+    def store(t, at, even, odd):
+        step[0][:, at], step[1][:, at] = split(even + odd)
+        turned[0][:, at], turned[1][:, at] = split(even - odd)
 
     step_parts(total, skew, upper, lower, store)
 
 
 def second_kernel(devices, me_ref, *refs):
     shards, turned, refs = refs[:devices], refs[devices : devices + 2], refs[devices + 2 :]
-    step, ordered = refs[:2], refs[2:4]
-    terms, skew, upper, lower = refs[4:]
+    ordered, (terms, skew, upper, lower) = refs[:2], refs[2:]
     rows = shards[0].shape[0]
     orbitals = terms.shape[0]
     me = me_ref[0]
     for k in range(devices):
         at = pl.ds(pl.multiple_of((me ^ k) * rows, rows), rows)
         upper[at, :], lower[at, :] = split(shards[k][...])
-    tile = orbitals // 2
-
-    @pl.loop(0, 2)
+
+    @pl.loop(0, orbitals // band)
     def _(t):
-        at = pl.ds(pl.multiple_of(t * tile, tile), tile)
-        terms[at, :] = product(
-            (turned[0][at, :], turned[1][at, :]), (upper[...], lower[...])
+        at = columns_of(t, band)
+        terms[:, at] = product(
+            (turned[0][...], turned[1][...]), (upper[:, at], lower[:, at])
         )
 
     total = skew_part(terms, -1.0, skew, upper, lower)
 
-    def store(at, even, odd):
+    def store(t, at, even, odd):
         whole = even + odd
-        step[0][at, :], step[1][at, :] = split(whole)
-        terms[at, :] = whole
-        for k in range(devices):
-            source = pl.ds(pl.multiple_of((me ^ k) * rows, rows), rows)
-            here = pl.ds(k * rows, rows)
-            ordered[0][at, here], ordered[1][at, here] = split(terms[at, source])
+        for b in range(band // rows):
+            column = t * (band // rows) + b
+            here = pl.ds(pl.multiple_of((me ^ column) * rows, rows), rows)
+            part = whole[:, b * rows : (b + 1) * rows]
+            ordered[0][:, here], ordered[1][:, here] = split(part)
 
     step_parts(total, skew, upper, lower, store)
 
 
-def make_step(kernel, me, shards, extra):
+def make_step(kernel, me, shards, extra, count):
     devices = len(shards)
     orbitals = shards[0].shape[1]
     square = (orbitals, orbitals)
@@ -257,8 +260,8 @@
         functools.partial(kernel, devices),
         in_specs=[pl.BlockSpec(memory_space=pltpu.SMEM)]
         + [whole_spec()] * (devices + len(extra)),
-        out_specs=[whole_spec()] * 4,
-        out_shape=[part] * 4,
+        out_specs=[whole_spec()] * count,
+        out_shape=[part] * count,
         scratch_shapes=[
             pltpu.VMEM(square, f32),
             pltpu.VMEM(square, f32),
@@ -266,27 +269,32 @@
             pltpu.VMEM(square, bf16),
         ],
         cost_estimate=cost(12 * orbitals**3, 24 * orbitals**2),
+        compiler_params=room,
     )(me, *shards, *extra)
 
 
 def compose_kernel(devices, me_ref, left_upper, left_lower, right_upper, right_lower, *refs):
     by_column, by_row, own_ref, whole = refs[:2], refs[2:4], refs[4], refs[5]
     rows = own_ref.shape[0]
-    tile = whole.shape[0] // 2
+    orbitals = whole.shape[0]
     me = me_ref[0]
 
-    @pl.loop(0, 2)
+    @pl.loop(0, orbitals // band)
     def _(t):
-        at = pl.ds(pl.multiple_of(t * tile, tile), tile)
-        whole[at, :] = product(
-            (left_upper[at, :], left_lower[at, :]), (right_upper[...], right_lower[...])
+        at = columns_of(t, band)
+        value = product(
+            (left_upper[...], left_lower[...]), (right_upper[:, at], right_lower[:, at])
         )
+        by_column[0][:, at], by_column[1][:, at] = split(value)
+        for b in range(band // rows):
+            column = t * (band // rows) + b
+            here = pl.ds(pl.multiple_of((me ^ column) * rows, rows), rows)
+            whole[:, here] = value[:, b * rows : (b + 1) * rows]
 
     own_ref[...] = whole[pl.ds(pl.multiple_of(me * rows, rows), rows), :]
     for k in range(devices):
         source = pl.ds(pl.multiple_of((me ^ k) * rows, rows), rows)
         here = pl.ds(k * rows, rows)
-        by_column[0][:, here], by_column[1][:, here] = split(whole[:, source])
         by_row[0][here, :], by_row[1][here, :] = split(whole[source, :])
 
 
@@ -301,41 +309,40 @@
         out_shape=[part] * 4 + [jax.ShapeDtypeStruct((orbitals // devices, orbitals), f32)],
         scratch_shapes=[pltpu.VMEM(square, f32)],
         cost_estimate=cost(6 * orbitals**3, 16 * orbitals**2),
+        compiler_params=room,
         name="compose",
     )(me, *left, *right)
     return out[:2], out[2:4], out[4]
 
 
-def first_product_kernel(vectors_ref, upper, lower, rows_upper, rows_lower, out_upper, out_lower, diagonal):
+def first_product_kernel(me_ref, vectors_ref, upper, lower, rows_upper, rows_lower, out_upper, out_lower, diagonal):
     size, rows, orbitals = vectors_ref.shape
     own = rows_upper[...].astype(f32) + rows_lower[...].astype(f32)
-    for q in range(0, size, quad):
-        at = pl.ds(q, quad)
-        vectors = vectors_ref[at].reshape(quad * rows, orbitals)
-        left = product(split(vectors), (upper[...], lower[...])).reshape(quad, rows, orbitals)
-        out_upper[at], out_lower[at] = split(left)
-        diagonal[at] = jnp.sum(left * own[None], axis=1)
+    vectors = vectors_ref[...].reshape(size * rows, orbitals)
+    left = product(split(vectors), (upper[...], lower[...])).reshape(size, rows, orbitals)
+    out_upper[...], out_lower[...] = split(left)
+    diagonal[...] = jnp.sum(left * own[None], axis=1, keepdims=True)
 
 
 def first_product(chol_vectors, step, me):
     vectors, rows, orbitals = chol_vectors.shape
-    size = 2 * quad
     part = jax.ShapeDtypeStruct(chol_vectors.shape, bf16)
-    block = pl.BlockSpec((size, rows, orbitals), lambda i, me: (i, 0, 0))
+    block = pl.BlockSpec((quad, rows, orbitals), lambda i, me: (i, 0, 0))
     square = pl.BlockSpec(
         (orbitals, orbitals), lambda i, me: (0, 0), pipeline_mode=pl.Buffered(1)
     )
     own = pl.BlockSpec((rows, orbitals), lambda i, me: (me[0], 0))
     out = pl.pallas_call(
-        lambda me_ref, *refs: first_product_kernel(*refs),
+        first_product_kernel,
         grid_spec=pltpu.PrefetchScalarGridSpec(
             num_scalar_prefetch=1,
-            grid=(vectors // size,),
+            grid=(vectors // quad,),
             in_specs=[block, square, square, own, own],
-            out_specs=[block, block, pl.BlockSpec((size, orbitals), lambda i, me: (i, 0))],
+            out_specs=[block, block, pl.BlockSpec((quad, 1, orbitals), lambda i, me: (i, 0, 0))],
         ),
-        out_shape=[part, part, jax.ShapeDtypeStruct((vectors, orbitals), f32)],
+        out_shape=[part, part, jax.ShapeDtypeStruct((vectors, 1, orbitals), f32)],
         cost_estimate=cost(6 * chol_vectors.size * orbitals, 8 * chol_vectors.size),
+        compiler_params=room,
         name="first_product",
     )(me, chol_vectors, *step, *step)
     return out[:2], out[2]
@@ -360,6 +367,7 @@
         out_specs=[pl.BlockSpec((quad, rows, rows), lambda i: (i, 0, 0))] * devices,
         out_shape=[jax.ShapeDtypeStruct((vectors, rows, rows), f32)] * devices,
         cost_estimate=cost(6 * vectors * rows * orbitals**2, 8 * vectors * rows * orbitals),
+        compiler_params=room,
         name="plain_pieces",
     )(*lefts, *right)
 
@@ -368,22 +376,32 @@
     return (lambda i: jnp.minimum(i, 1)) if side == 0 else (lambda i: jnp.maximum(i - 2, 0))
 
 
-def shared_pieces_kernel(near, rows, own, one, two, upper, lower, *outs):
-    count = own.shape[0]
+def shared_pieces_kernel(pair, own, *refs):
+    others, (upper, lower), refs = refs[:4], refs[4:6], refs[6:]
+    outs, (left_upper, left_lower, blocks) = refs[:-3], refs[-3:]
+    count, rows, orbitals = own.shape
     half = len(outs) // 2
-    for side, other in enumerate((one, two)):
-        @pl.when(pl.program_id(0) // 2 == side)
+    step = pl.program_id(0)
+    size = count * rows
+    left_upper[:size], left_lower[:size] = split(own[...].reshape(size, orbitals))
+    for i, other in enumerate(others):
+        @pl.when(step == i)
         def _():
-            right = tuple(
-                jnp.concatenate([r[:, k * rows : (k + 1) * rows] for k in near[side]], axis=1)
-                for r in (upper, lower)
-            )
-            left = jnp.concatenate([own[...], other[...]], axis=0)
-            value = product(split(left.reshape(2 * count * rows, -1)), right)
+            left_upper[size:], left_lower[size:] = split(other[...].reshape(size, orbitals))
+
+    left = left_upper[...], left_lower[...]
+    middle = pl.ds(pl.multiple_of((1 + step // 2) * pair, pair), pair)
+    for n, at in enumerate((pl.ds(0, pair), middle)):
+        value = product(left, (upper[:, at], lower[:, at]))
+        for b in range(half // 2):
+            for p in range(2 * count):
+                block = value[p * rows : (p + 1) * rows, b * rows : (b + 1) * rows]
+                blocks[n * (half // 2) + b, p % count, p // count] = block.T
+    for side in range(2):
+        @pl.when(step // 2 == side)
+        def _():
             for b in range(half):
-                for p in range(2 * count):
-                    block = value[p * rows : (p + 1) * rows, b * rows : (b + 1) * rows]
-                    outs[side * half + b][p % count, p // count] = block.T
+                outs[side * half + b][...] = blocks[b]
 
 
 def shared_pieces(near, chol_vectors, starts, others, right):
@@ -394,23 +412,28 @@
         pl.BlockSpec(
             (2, rows, orbitals), lambda i: (jnp.where(i < 2, first + i, second + i - 2), 0, 0)
         )
-    ]
+    ] + [resident((2, rows, orbitals))] * 4
     outs = []
     for side in range(2):
         turn_of = turns(side)
-        specs.append(pl.BlockSpec((2, rows, orbitals), lambda i, t=turn_of: (t(i), 0, 0)))
         outs += [
             pl.BlockSpec((2, 2, rows, rows), lambda i, t=turn_of: (t(i), 0, 0, 0))
         ] * half
     out = pl.pallas_call(
-        functools.partial(shared_pieces_kernel, near, rows),
+        functools.partial(shared_pieces_kernel, orbitals // 4),
         grid=(4,),
         in_specs=specs + [resident((orbitals, orbitals))] * 2,
         out_specs=outs,
         out_shape=[jax.ShapeDtypeStruct((quad, 2, rows, rows), f32)] * (2 * half),
+        scratch_shapes=[
+            pltpu.VMEM((4 * rows, orbitals), bf16),
+            pltpu.VMEM((4 * rows, orbitals), bf16),
+            pltpu.VMEM((half, 2, 2, rows, rows), f32),
+        ],
         cost_estimate=cost(
             12 * quad * rows * orbitals**2, 16 * quad * rows * orbitals
         ),
+        compiler_params=room,
         name="shared_pieces",
     )(chol_vectors, *others, *right)
     return out[:half], out[half:]
@@ -435,23 +458,25 @@
         out_specs=pl.BlockSpec((quad, rows, orbitals), lambda i: (i, 0, 0)),
         out_shape=jax.ShapeDtypeStruct(shape, f32),
         cost_estimate=cost(6 * vectors * rows * orbitals**2, 8 * vectors * rows * orbitals),
+        compiler_params=room,
         name="plain_rotated",
     )(*right, *parts)
 
 
 def shared_rotated_kernel(orders, upper, lower, *refs):
-    out_ref = refs[-1]
+    out_ref, left_upper, left_lower = refs[-3:]
     count, rows, _ = out_ref.shape
     half = len(orders[0]) // 2
     for side, order in enumerate(orders):
         @pl.when(pl.program_id(0) // 2 == side)
         def _():
-            columns = [
-                refs[side * half + index][:, which].reshape(count * rows, rows)
-                for index, which in order
-            ]
-            left = split(jnp.concatenate(columns, axis=1))
-            out_ref[...] = product(left, (upper[...], lower[...])).reshape(out_ref.shape)
+            for k, (index, which) in enumerate(order):
+                here = pl.ds(k * rows, rows)
+                part = refs[side * half + index][:, which].reshape(count * rows, rows)
+                left_upper[:, here], left_lower[:, here] = split(part)
+
+    left = left_upper[...], left_lower[...]
+    out_ref[...] = product(left, (upper[...], lower[...])).reshape(out_ref.shape)
 
 
 def shared_rotated(previous, parts, orders, starts, right, shape):
@@ -476,7 +501,9 @@
         ),
         out_shape=jax.ShapeDtypeStruct(shape, f32),
         input_output_aliases={} if fresh else {count: 0},
+        scratch_shapes=[pltpu.VMEM((2 * rows, orbitals), bf16)] * 2,
         cost_estimate=cost(12 * quad * rows * orbitals**2, 16 * quad * rows * orbitals),
+        compiler_params=room,
         name="shared_rotated",
     )(*right, *parts[0], *parts[1], *([] if fresh else [previous]))
 
@@ -485,7 +512,7 @@
     total = jnp.zeros(out_ref.shape, f32)
     for p in range(upper_ref.shape[0]):
         left = upper_ref[p].astype(f32) + lower_ref[p].astype(f32)
-        total = total + left * diagonal_ref[p : p + 1, :]
+        total = total + left * diagonal_ref[p]
     out_ref[...] = total
 
 
@@ -496,10 +523,11 @@
     return pl.pallas_call(
         second_terms_kernel,
         grid=(rows // size,),
-        in_specs=[block, block, pl.BlockSpec((vectors, orbitals), lambda i: (0, 0))],
+        in_specs=[block, block, pl.BlockSpec((vectors, 1, orbitals), lambda i: (0, 0, 0))],
         out_specs=pl.BlockSpec((size, orbitals), lambda i: (i, 0)),
         out_shape=jax.ShapeDtypeStruct((rows, orbitals), f32),
         cost_estimate=cost(2 * lefts[0].size, 4 * lefts[0].size),
+        compiler_params=room,
         name="second_terms",
     )(*lefts, diagonal)
 
@@ -514,9 +542,12 @@
     masks = [2 ** (b + 1) - 1 for b in range(bits)]
     half = part.shape[0] // 2
     one, two = part[:half], part[half:]
-    for a, b in zip(masks, reversed(masks)):
-        one, two = one + flip(one, a), two + flip(two, b)
-    return jnp.concatenate([one, two], axis=0)
+    for turn_number, (a, b) in enumerate(zip(masks, reversed(masks))):
+        one_more, two_more = flip(one, a), flip(two, b)
+        one, two = one + one_more, two + two_more
+        if turn_number == 0:
+            first = one
+    return jnp.concatenate([one, two], axis=0), first
 
 
 def shards_of(part):
@@ -549,39 +580,53 @@
         [plain + (s * groups + g) * quad for s in range(2)] for g in range(groups)
     ]
 
-    own = [[chol_vectors[start : start + quad] for start in starts[g]] for g in range(groups)]
     early = {}
 
-    def send_early(g, *others):
+    def send_early(h, *others):
+        g, i = h // 2, h % 2
         for s, bit in enumerate(bits):
-            early[g, s] = swap(after(own[g][s], *others), bit)
-
+            start = starts[g][s] + 2 * i
+            early[g, s, i] = swap(after(own[start], *others), bit)
+
+    def copy_own(source, halves):
+        for h in halves:
+            for s in range(2):
+                start = starts[h // 2][s] + 2 * (h % 2)
+                own[start] = source[start : start + 2]
+
+    own = {}
+    copy_own(chol_vectors, [0])
     part = gradient_terms(chol_vectors, me)
-    part = sum_halves(part)
+    part, first = sum_halves(part)
+    send_early(0)
+    copy_own(after(chol_vectors, first), range(1, 2 * groups))
     gathered = shards_of(part)
-    for g in range(groups - 1):
-        send_early(g, *gathered)
-    *step, turned_upper, turned_lower = make_step(first_kernel, me, gathered, ())
+    send_early(1, *gathered)
+    send_early(2, *gathered)
+    *step, turned_upper, turned_lower = make_step(first_kernel, me, gathered, (), 4)
     lefts, diagonal = first_product(chol_vectors, step, me)
     diagonal = sum_over_row(diagonal)
+    send_early(3, diagonal)
     part = second_terms(lefts, diagonal)
-    gathered = shards_of(sum_halves(part))
-    send_early(groups - 1, *gathered)
-    *next_step, ordered_upper, ordered_lower = make_step(
-        second_kernel, me, gathered, (turned_upper, turned_lower)
-    )
-    sent = plain_pieces(lefts, (ordered_upper, ordered_lower), plain, devices)
+    part, _ = sum_halves(part)
+    gathered = shards_of(part)
+    for h in range(4, 2 * groups):
+        send_early(h, *gathered)
+    next_step = make_step(second_kernel, me, gathered, (turned_upper, turned_lower), 2)
+    sent = plain_pieces(lefts, next_step, plain, devices)
     plain_parts = [sent[0]] + [swap(sent[k], k) for k in everyone[1:]]
     next_step = lax.optimization_barrier((*next_step, *sent))[:2]
     by_column, by_row, rotation = compose(me, step, next_step, devices)
 
     shared_parts = []
+
     for g in range(groups):
-        others = (early[g, 0], early[g, 1])
+        others = [early[g, s, i] for s in range(2) for i in range(2)]
         sent = shared_pieces(near, chol_vectors, starts[g], others, by_column)
         shared_parts.append(
             [
-                [pieces[0]] + [swap(pieces[i], near[s][i]) for i in range(1, len(near[s]))]
+                [pieces[0]]
+                + [swap(pieces[i], near[s][i]) for i in range(1, len(near[s]))]
                 for s, pieces in enumerate(sent)
             ]
         )

time: 507 us -> 484 us (0.955); the launches traced: 500 us -> 483 us
  Pallas kernels: 210 us -> 157 us
  waiting for transfers between devices: 209 us -> 231 us
  local copies, waits for them, and re-layouts: 14.1 us -> 35.4 us
    ppermute x49 -> x55, waiting for transfers between devices: 164 us -> 186 us  [swap(): return lax.ppermute(x, 'row', [(i, i ^ k) for i in range(count)])]
    unnamed x52 -> x46, local copies, waits for them, and re-layouts: 2.52 us -> 24 us
    pallas_call x2, Pallas kernels: 43.2 us -> 32.9 us  [make_step(): pl.pallas_call(functools.partial(kernel, devices), in_specs=[pl.BlockSpec...]
    pallas_call x4, Pallas kernels: 73.9 us -> 64.5 us  [the longest x3 33.2 us: shared_pieces(): pl.pallas_call(functools.partial(shared_pieces_kernel, orbitals // 4), gr...]
    pallas_call x1, Pallas kernels: 15.5 us -> 8.66 us  [compose(): pl.pallas_call(functools.partial(compose_kernel, devices), in_specs=[pl.B...]
    ppermute x49 -> x55, starting transfers between devices: 47.6 us -> 40.7 us  [swap(): return lax.ppermute(x, 'row', [(i, i ^ k) for i in range(count)])]
    pallas_call x3, Pallas kernels: 34.6 us -> 28.1 us  [shared_rotated(): pl.pallas_call(functools.partial(shared_rotated_kernel, orders), grid=(4,...]
    pallas_call x1, Pallas kernels: 9.21 us -> 3.21 us  [gradient_terms(): pl.pallas_call(gradient_kernel, grid_spec=pltpu.PrefetchScalarGridSpec(nu...]
  transfers between devices with their start and end apart: 57 -> 63, of which waited for: 29 -> 32; matrix products, arithmetic and copies ran while one was open for 2% -> 2% of each run, Pallas kernels for 25% -> 20%
where the time goes in v2:
time: 484 us; the launch traced here: 483 us
  waiting for transfers between devices  231 us (48%)
  Pallas kernels  157 us (32%)
  starting transfers between devices  58 us (12%)
  local copies, waits for them, and re-layouts  35.4 us (7%)
    ppermute x55, waiting for transfers between devices, swap(): return lax.ppermute(x, 'row', [(i, i ^ k) for i in range(count)])  186 us
    ppermute x8, waiting for transfers between devices, flip(): return lax.ppermute(x, 'vec', [(i, i ^ k) for i in range(count)])  44.5 us
    ppermute x55, starting transfers between devices, swap(): return lax.ppermute(x, 'row', [(i, i ^ k) for i in range(count)])  40.7 us
    pallas_call x3, Pallas kernels, shared_pieces(): pl.pallas_call(functools.partial(shared_pieces_kernel, orbitals // 4), gr...  33.2 us
    pallas_call x2, Pallas kernels, make_step(): pl.pallas_call(functools.partial(kernel, devices), in_specs=[pl.BlockSpec...  32.9 us
    pallas_call x1, Pallas kernels, first_product(): pl.pallas_call(first_product_kernel, grid_spec=pltpu.PrefetchScalarGridSp...  31.3 us
    pallas_call x3, Pallas kernels, shared_rotated(): pl.pallas_call(functools.partial(shared_rotated_kernel, orders), grid=(4,...  28.1 us
    unnamed x46, local copies, waits for them, and re-layouts  24 us
  transfers between devices with their start and end apart: 63, of which 32 were waited for; matrix products, arithmetic and copies ran while one was open for 2% of the time, Pallas kernels for 20%

profile of v2, /device:TPU:0, one launch (start us, length us, event | category | flops | bytes accessed | tf_op | source)
XLA Modules:
  0.0 483.2 jit_solution(2711497846263234501)
XLA Ops:
  0.6 5.8 %copy-done = f32[32,128,1024]{2,1,0:T(8,128)S(1)} copy-done((f32[32,128,1024]{2,1,0:T(8,128)S(1)}, f32[32,128,1024]{2,1,0:T(8,128)}, u32[]{:S(2)}) %copy-start) | copy-done | bytes 16777240
  6.4 3.2 gradient_terms.1
  9.7 3.1 collective-permute-start
  12.8 2.5 collective-permute-start.2
  15.3 4.2 collective-permute-done
  19.5 7.5 %collective-permute-done.2 = f32[64,1024]{1,0:T(8,128)S(1)} collective-permute-done((f32[64,1024]{1,0:T(8,128)S(1)}, f32[64,1024]{1,0:T(8,128)S(1)}, u32[]{:S(2)}, u32[]{:S(2)}) %collective-permute-start.2) | collective-permute-done | bytes 262176 | tf_op jit(solution)/shard_map/ppermute | solution.py:537
  27.7 2.6 collective-permute-start.1
  30.4 9.5 %collective-permute-done.3 = f32[64,1024]{1,0:T(8,128)S(1)} collective-permute-done((f32[64,1024]{1,0:T(8,128)S(1)}, f32[64,1024]{1,0:T(8,128)S(1)}, u32[]{:S(2)}, u32[]{:S(2)}) %collective-permute-start.3) | collective-permute-done | bytes 262176 | tf_op jit(solution)/shard_map/ppermute | solution.py:537
  40.0 2.5 collective-permute-start.9
  43.6 12.2 %collective-permute-done.9.refs_6_ = f32[128,1024]{1,0:T(8,128)S(1)} collective-permute-done((f32[128,1024]{1,0:T(8,128)S(1)}, f32[128,1024]{1,0:T(8,128)S(1)}, u32[]{:S(2)}, u32[]{:S(2)}) %collective-permute-start.9) | collective-permute-done | bytes 524320 | tf_op jit(solution)/shard_map/ppermute | solution.py:18
  55.8 6.0 %collective-permute-done.7.refs_4_ = f32[128,1024]{1,0:T(8,128)S(1)} collective-permute-done((f32[128,1024]{1,0:T(8,128)S(1)}, f32[128,1024]{1,0:T(8,128)S(1)}, u32[]{:S(2)}, u32[]{:S(2)}) %collective-permute-start.7) | collective-permute-done | bytes 524320 | tf_op jit(solution)/shard_map/ppermute | solution.py:18
  64.5 12.0 %shard_map.30 = (bf16[1024,1024]{1,0:T(8,128)(2,1)S(1)}, bf16[1024,1024]{1,0:T(8,128)(2,1)S(1)}, bf16[1024,1024]{1,0:T(8,128)(2,1)S(1)}, bf16[1024,1024]{1,0:T(8,128)(2,1)S(1)}) custom-call(s32[1]{0:T(128)} %bitcast.me_ref, f32[128,1024]{1,0:T(8,128)S(1)} %pad_maximum_fusion.refs_0_, f32[128,1024]{1,0:T(8,128)S(1)} %collective-permute-done.4.refs_1_, ...), custom_call_target="tpu_custom_call" | custom-call | flops 12884901888 | bytes 25165824 | tf_op jit(solution)/shard_map/pallas_call | solution.py:259
  76.5 31.3 %first_product.1 = (bf16[32,128,1024]{2,1,0:T(8,128)(2,1)S(1)}, bf16[32,128,1024]{2,1,0:T(8,128)(2,1)S(1)}, f32[32,1,1024]{2,1,0:T(1,128)S(1)}) custom-call(s32[1]{0:T(128)} %bitcast.me_ref, f32[32,128,1024]{2,1,0:T(8,128)} %own.5, bf16[1024,1024]{1,0:T(8,128)(2,1)S(1)} %get-tuple-element.65.upper.rows_upper.left_upper, ...), custom_call_target="tpu_custom_call" | custom-call | flops 25769803776 | bytes 33554432 | tf_op jit(solution)/shard_map/first_product/pallas_call | solution.py:335
  113.0 3.8 collective-permute-done.14
  116.8 2.0 collective-permute-done.13
  118.9 4.6 second_terms.1
  123.6 4.8 collective-permute-start.15
  128.4 12.0 %collective-permute-done.15 = f32[64,1024]{1,0:T(8,128)S(1)} collective-permute-done((f32[64,1024]{1,0:T(8,128)S(1)}, f32[64,1024]{1,0:T(8,128)S(1)}, u32[]{:S(2)}, u32[]{:S(2)}) %collective-permute-start.15) | collective-permute-done | bytes 262176 | tf_op jit(solution)/shard_map/ppermute | solution.py:537
  140.5 3.6 collective-permute-start.16
  144.1 7.4 %collective-permute-done.16 = f32[64,1024]{1,0:T(8,128)S(1)} collective-permute-done((f32[64,1024]{1,0:T(8,128)S(1)}, f32[64,1024]{1,0:T(8,128)S(1)}, u32[]{:S(2)}, u32[]{:S(2)}) %collective-permute-start.16) | collective-permute-done | bytes 262176 | tf_op jit(solution)/shard_map/ppermute | solution.py:537
  151.5 3.8 collective-permute-done.18
  159.0 12.2 %collective-permute-done.24.refs_6_ = f32[128,1024]{1,0:T(8,128)S(1)} collective-permute-done((f32[128,1024]{1,0:T(8,128)S(1)}, f32[128,1024]{1,0:T(8,128)S(1)}, u32[]{:S(2)}, u32[]{:S(2)}) %collective-permute-start.24) | collective-permute-done | bytes 524320 | tf_op jit(solution)/shard_map/ppermute | solution.py:18
  171.2 10.2 %collective-permute-done.22.refs_4_ = f32[128,1024]{1,0:T(8,128)S(1)} collective-permute-done((f32[128,1024]{1,0:T(8,128)S(1)}, f32[128,1024]{1,0:T(8,128)S(1)}, u32[]{:S(2)}, u32[]{:S(2)}) %collective-permute-start.22) | collective-permute-done | bytes 524320 | tf_op jit(solution)/shard_map/ppermute | solution.py:18
  182.0 3.1 fusion.1
  186.7 8.2 %fusion = (f32[2,128,1024]{2,1,0:T(8,128)}, f32[2,128,1024]{2,1,0:T(8,128)}, f32[2,128,1024]{2,1,0:T(8,128)}, f32[2,128,1024]{2,1,0:T(8,128)}, f32[2,128,1024]{2...) fusion(f32[32,128,1024]{2,1,0:T(8,128)} %own.5), kind=kLoop, calls=%fused_computation.7 | loop fusion | bytes 20971520 | tf_op jit(solution)/shard_map/slice | solution.py:595
  205.9 20.9 %shard_map.31 = (bf16[1024,1024]{1,0:T(8,128)(2,1)S(1)}, bf16[1024,1024]{1,0:T(8,128)(2,1)S(1)}) custom-call(s32[1]{0:T(128)} %bitcast.me_ref, f32[128,1024]{1,0:T(8,128)S(1)} %pad_maximum_fusion.1.refs_0_, f32[128,1024]{1,0:T(8,128)S(1)} %collective-permute-done.19.refs_1_, f32[128,1024]{1,0:T(8,128)S(1)} %collective-permute-done.20.refs_2_, ...), custom_call_target="tpu_custom_call" | custom-call | flops 12884901888 | bytes 25165824 | tf_op jit(solution)/shard_map/pallas_call | solution.py:259
  226.8 4.9 %copy-done.2 = bf16[32,128,1024]{2,1,0:T(8,128)(2,1)S(1)} copy-done((bf16[32,128,1024]{2,1,0:T(8,128)(2,1)S(1)}, bf16[32,128,1024]{2,1,0:T(8,128)(2,1)}, u32[]{:S(2)}) %copy-start.2) | copy-done | bytes 8388632
  231.7 7.3 %plain_pieces.1 = (f32[8,128,128]{2,1,0:T(8,128)S(1)}, f32[8,128,128]{2,1,0:T(8,128)S(1)}, f32[8,128,128]{2,1,0:T(8,128)S(1)}, f32[8,128,128]{2,1,0:T(8,128)S(1)...) custom-call(bf16[32,128,1024]{2,1,0:T(8,128)(2,1)S(1)} %get-tuple-el, ...), custom_call_target="tpu_custom_call" | custom-call | flops 6442450944 | bytes 8388608 | tf_op jit(solution)/shard_map/plain_pieces/pallas_call | solution.py:363
  246.2 8.7 %compose.1 = (bf16[1024,1024]{1,0:T(8,128)(2,1)S(1)}, bf16[1024,1024]{1,0:T(8,128)(2,1)S(1)}, bf16[1024,1024]{1,0:T(8,128)(2,1)S(1)}, bf16[1024,1024]{1,0:T(8,128)(2,1)S(1)}, f32[128,1024]{1,0:T(8,128)}) custom-call(s32[1]{0:T(128)} %bitcast.me_ref, bf16[1024,1024]{1,0:T(8,128)(2,1)S(1)} %copy-done.12, bf16[1024,1024]{1,0:T(8,128)(2,1)S(1)} %copy-done.14, ...), custom_call_target="tpu_custom_call" | custom-call | flops 6442450944 | bytes 16777216 | tf_op jit(solution)/shard_map/compose/pallas_call | solution.py:305
  256.7 11.6 %shared_pieces.3 = (f32[4,2,128,128]{3,2,1,0:T(8,128)S(1)}, f32[4,2,128,128]{3,2,1,0:T(8,128)S(1)}, f32[4,2,128,128]{3,2,1,0:T(8,128)S(1)}, f32[4,2,128,128]{3,2...) custom-call(f32[32,128,1024]{2,1,0:T(8,128)} %own.5, ...), custom_call_target="tpu_custom_call" | custom-call | flops 6442450944 | bytes 8388608 | tf_op jit(solution)/shard_map/shared_pieces/pallas_call | solution.py:422
  270.1 8.1 %collective-permute-done.35.refs_1_ = f32[2,128,1024]{2,1,0:T(8,128)S(1)} collective-permute-done((f32[2,128,1024]{2,1,0:T(8,128)S(1)}, f32[2,128,1024]{2,1,0:T(8,128)S(1)}, u32[]{:S(2)}, u32[]{:S(2)}) %collective-permute-start.35) | collective-permute-done | bytes 1048608 | tf_op jit(solution)/shard_map/ppermute | solution.py:18
  279.6 9.0 %collective-permute-done.37.refs_3_ = f32[2,128,1024]{2,1,0:T(8,128)S(1)} collective-permute-done((f32[2,128,1024]{2,1,0:T(8,128)S(1)}, f32[2,128,1024]{2,1,0:T(8,128)S(1)}, u32[]{:S(2)}, u32[]{:S(2)}) %collective-permute-start.37) | collective-permute-done | bytes 1048608 | tf_op jit(solution)/shard_map/ppermute | solution.py:18
  289.1 10.8 %collective-permute-done.51.refs_2_ = f32[4,2,128,128]{3,2,1,0:T(8,128)S(1)} collective-permute-done((f32[4,2,128,128]{3,2,1,0:T(8,128)S(1)}, f32[4,2,128,128]{3,2,1,0:T(8,128)S(1)}, u32[]{:S(2)}, u32[]{:S(2)}) %collective-permute-start.51) | collective-permute-done | bytes 524320 | tf_op jit(solution)/shard_map/ppermute | solution.py:18
  301.3 9.8 %collective-permute-done.57.refs_2_ = f32[8,128,128]{2,1,0:T(8,128)S(1)} collective-permute-done((f32[8,128,128]{2,1,0:T(8,128)S(1)}, f32[8,128,128]{2,1,0:T(8,128)S(1)}, u32[]{:S(2)}, u32[]{:S(2)}) %collective-permute-start.57) | collective-permute-done | bytes 524320 | tf_op jit(solution)/shard_map/ppermute | solution.py:18
  311.1 9.5 %collective-permute-done.58.refs_3_ = f32[8,128,128]{2,1,0:T(8,128)S(1)} collective-permute-done((f32[8,128,128]{2,1,0:T(8,128)S(1)}, f32[8,128,128]{2,1,0:T(8,128)S(1)}, u32[]{:S(2)}, u32[]{:S(2)}) %collective-permute-start.58) | collective-permute-done | bytes 524320 | tf_op jit(solution)/shard_map/ppermute | solution.py:18
  323.9 9.6 %collective-permute-done.61.refs_6_ = f32[8,128,128]{2,1,0:T(8,128)S(1)} collective-permute-done((f32[8,128,128]{2,1,0:T(8,128)S(1)}, f32[8,128,128]{2,1,0:T(8,128)S(1)}, u32[]{:S(2)}, u32[]{:S(2)}) %collective-permute-start.61) | collective-permute-done | bytes 524320 | tf_op jit(solution)/shard_map/ppermute | solution.py:18
  335.1 10.8 %shared_pieces.4 = (f32[4,2,128,128]{3,2,1,0:T(8,128)S(1)}, f32[4,2,128,128]{3,2,1,0:T(8,128)S(1)}, f32[4,2,128,128]{3,2,1,0:T(8,128)S(1)}, f32[4,2,128,128]{3,2...) custom-call(f32[32,128,1024]{2,1,0:T(8,128)} %own.5, ...), custom_call_target="tpu_custom_call" | custom-call | flops 6442450944 | bytes 8388608 | tf_op jit(solution)/shard_map/shared_pieces/pallas_call | solution.py:422
  346.0 8.2 %plain_rotated.1.refs_8_ = f32[32,128,1024]{2,1,0:T(8,128)} custom-call(bf16[1024,1024]{1,0:T(8,128)(2,1)S(1)} %get-tuple-element.84.upper, bf16[1024,1024]{1,0:T(8,128)(2,1)S(1)} %get-tuple-element.85.lower, f32[8,128,128]{2,1,0:T(8,128)S(1)} %get-tuple-element.74.refs_0_, f32[8,128,128]{2,1,0:T(8,128)S(1)} %collective-permute-done.56.refs_1_, ...), custom_call_target="tpu_custom_call" | custom-call | flops 6442450944 | bytes 8388608 | tf_op jit(solution)/shard_map/plain_rotated/pallas_call | solution.py:453
  354.2 44.4 %collective-permute-done.52.refs_3_ = f32[4,2,128,128]{3,2,1,0:T(8,128)S(1)} collective-permute-done((f32[4,2,128,128]{3,2,1,0:T(8,128)S(1)}, f32[4,2,128,128]{3,2,1,0:T(8,128)S(1)}, u32[]{:S(2)}, u32[]{:S(2)}) %collective-permute-start.52) | collective-permute-done | bytes 524320 | tf_op jit(solution)/shard_map/ppermute | solution.py:18
  402.5 10.8 %shared_pieces.5 = (f32[4,2,128,128]{3,2,1,0:T(8,128)S(1)}, f32[4,2,128,128]{3,2,1,0:T(8,128)S(1)}, f32[4,2,128,128]{3,2,1,0:T(8,128)S(1)}, f32[4,2,128,128]{3,2...) custom-call(f32[32,128,1024]{2,1,0:T(8,128)} %own.5, ...), custom_call_target="tpu_custom_call" | custom-call | flops 6442450944 | bytes 8388608 | tf_op jit(solution)/shard_map/shared_pieces/pallas_call | solution.py:422
  414.8 8.9 %collective-permute-done.55.refs_7_ = f32[4,2,128,128]{3,2,1,0:T(8,128)S(1)} collective-permute-done((f32[4,2,128,128]{3,2,1,0:T(8,128)S(1)}, f32[4,2,128,128]{3,2,1,0:T(8,128)S(1)}, u32[]{:S(2)}, u32[]{:S(2)}) %collective-permute-start.55) | collective-permute-done | bytes 524320 | tf_op jit(solution)/shard_map/ppermute | solution.py:18
  424.3 1.9 collective-permute-start.49
  426.2 9.4 %shared_rotated.3.refs_8_ = f32[32,128,1024]{2,1,0:T(8,128)} custom-call(bf16[1024,1024]{1,0:T(8,128)(2,1)S(1)} %get-tuple-element.84.upper, bf16[1024,1024]{1,0:T(8,128)(2,1)S(1)} %get-tuple-element.85.lower, f32[4,2,128,128]{3,2,1,0:T(8,128)S(1)} %get-tuple-element.95.refs_0_, ...), custom_call_target="tpu_custom_call", output_to_operand_aliasing={{}: (10, {})} | custom-call | flops 6442450944 | bytes 8388608 | tf_op jit(solution)/shard_map/shared_rotated/pallas_call | solution.py:493
  438.5 11.2 %collective-permute-done.49.refs_7_ = f32[4,2,128,128]{3,2,1,0:T(8,128)S(1)} collective-permute-done((f32[4,2,128,128]{3,2,1,0:T(8,128)S(1)}, f32[4,2,128,128]{3,2,1,0:T(8,128)S(1)}, u32[]{:S(2)}, u32[]{:S(2)}) %collective-permute-start.49) | collective-permute-done | bytes 524320 | tf_op jit(solution)/shard_map/ppermute | solution.py:18
  451.1 9.4 %shared_rotated.4.refs_8_ = f32[32,128,1024]{2,1,0:T(8,128)} custom-call(bf16[1024,1024]{1,0:T(8,128)(2,1)S(1)} %get-tuple-element.84.upper, bf16[1024,1024]{1,0:T(8,128)(2,1)S(1)} %get-tuple-element.85.lower, f32[4,2,128,128]{3,2,1,0:T(8,128)S(1)} %get-tuple-element.109.refs_0_, ...), custom_call_target="tpu_custom_call", output_to_operand_aliasing={{}: (10, {})} | custom-call | flops 6442450944 | bytes 8388608 | tf_op jit(solution)/shard_map/shared_rotated/pallas_call | solution.py:493
  460.6 3.9 collective-permute-done.42.refs_6_
  464.6 9.3 %collective-permute-done.43.refs_7_ = f32[4,2,128,128]{3,2,1,0:T(8,128)S(1)} collective-permute-done((f32[4,2,128,128]{3,2,1,0:T(8,128)S(1)}, f32[4,2,128,128]{3,2,1,0:T(8,128)S(1)}, u32[]{:S(2)}, u32[]{:S(2)}) %collective-permute-start.43) | collective-permute-done | bytes 524320 | tf_op jit(solution)/shard_map/ppermute | solution.py:18
  473.8 9.3 %shared_rotated.5 = f32[32,128,1024]{2,1,0:T(8,128)} custom-call(bf16[1024,1024]{1,0:T(8,128)(2,1)S(1)} %get-tuple-element.84.upper, bf16[1024,1024]{1,0:T(8,128)(2,1)S(1)} %get-tuple-element.85.lower, f32[4,2,128,128]{3,2,1,0:T(8,128)S(1)} %get-tuple-element.119.refs_0_, ...), custom_call_target="tpu_custom_call", output_to_operand_aliasing={{}: (10, {})} | custom-call | flops 6442450944 | bytes 8388608 | tf_op jit(solution)/shard_map/shared_rotated/pallas_call | solution.py:493
  (152 shorter events, 56.1 us)
Async XLA Ops:
  40.0 15.8 %collective-permute-start.9 = (f32[128,1024]{1,0:T(8,128)S(1)}, f32[128,1024]{1,0:T(8,128)S(1)}, u32[]{:S(2)}, u32[]{:S(2)}) collective-permute-start(f32[128,1024]{1,0:T(8,128)S(1)} %pad_maximum_fusion.refs_0_), channel_id=1, source_target_pairs={{0,6},{1,7},{2,4},{3,5},{4,2},{5,3},{6,0},{7,1},{8,14},{9,15},{10,... | collective-permute-start | bytes 1572872 | tf_op jit(solution)/shard_map/ppermute | solution.py:18
  42.5 19.3 %collective-permute-start.7 = (f32[128,1024]{1,0:T(8,128)S(1)}, f32[128,1024]{1,0:T(8,128)S(1)}, u32[]{:S(2)}, u32[]{:S(2)}) collective-permute-start(f32[128,1024]{1,0:T(8,128)S(1)} %pad_maximum_fusion.refs_0_), channel_id=1, source_target_pairs={{0,4},{1,5},{2,6},{3,7},{4,0},{5,1},{6,2},{7,3},{8,12},{9,13},{10,... | collective-permute-start | bytes 1572872 | tf_op jit(solution)/shard_map/ppermute | solution.py:18
  43.0 18.8 %collective-permute-start.5 = (f32[128,1024]{1,0:T(8,128)S(1)}, f32[128,1024]{1,0:T(8,128)S(1)}, u32[]{:S(2)}, u32[]{:S(2)}) collective-permute-start(f32[128,1024]{1,0:T(8,128)S(1)} %pad_maximum_fusion.refs_0_), channel_id=1, source_target_pairs={{0,2},{1,3},{2,0},{3,1},{4,6},{5,7},{6,4},{7,5},{8,10},{9,11},{10,... | collective-permute-start | bytes 1572872 | tf_op jit(solution)/shard_map/ppermute | solution.py:18
  43.6 18.7 %collective-permute-start.4 = (f32[128,1024]{1,0:T(8,128)S(1)}, f32[128,1024]{1,0:T(8,128)S(1)}, u32[]{:S(2)}, u32[]{:S(2)}) collective-permute-start(f32[128,1024]{1,0:T(8,128)S(1)} %pad_maximum_fusion.refs_0_), channel_id=1, source_target_pairs={{0,1},{1,0},{2,3},{3,2},{4,5},{5,4},{6,7},{7,6},{8,9},{9,8},{10,11... | collective-permute-start | bytes 1572872 | tf_op jit(solution)/shard_map/ppermute | solution.py:18
  123.6 16.8 %collective-permute-start.15 = (f32[64,1024]{1,0:T(8,128)S(1)}, f32[64,1024]{1,0:T(8,128)S(1)}, u32[]{:S(2)}, u32[]{:S(2)}) collective-permute-start(f32[64,1024]{1,0:T(8,128)S(1)} %get-tuple-element.142), channel_id=1, source_target_pairs={{0,8},{8,0},{16,24},{24,16},{1,9},{9,1},{17,25},{25,17},{2,10},{10... | collective-permute-start | bytes 786440 | tf_op jit(solution)/shard_map/ppermute | solution.py:537
  155.4 15.8 %collective-permute-start.24 = (f32[128,1024]{1,0:T(8,128)S(1)}, f32[128,1024]{1,0:T(8,128)S(1)}, u32[]{:S(2)}, u32[]{:S(2)}) collective-permute-start(f32[128,1024]{1,0:T(8,128)S(1)} %pad_maximum_fusion.1.refs_0_), channel_id=1, source_target_pairs={{0,6},{1,7},{2,4},{3,5},{4,2},{5,3},{6,0},{7,1},{8,14},{9,15},{10,... | collective-permute-start | bytes 1572872 | tf_op jit(solution)/shard_map/ppermute | solution.py:18
  157.3 24.2 %collective-permute-start.22 = (f32[128,1024]{1,0:T(8,128)S(1)}, f32[128,1024]{1,0:T(8,128)S(1)}, u32[]{:S(2)}, u32[]{:S(2)}) collective-permute-start(f32[128,1024]{1,0:T(8,128)S(1)} %pad_maximum_fusion.1.refs_0_), channel_id=1, source_target_pairs={{0,4},{1,5},{2,6},{3,7},{4,0},{5,1},{6,2},{7,3},{8,12},{9,13},{10,... | collective-permute-start | bytes 1572872 | tf_op jit(solution)/shard_map/ppermute | solution.py:18
  158.5 23.1 %collective-permute-start.20 = (f32[128,1024]{1,0:T(8,128)S(1)}, f32[128,1024]{1,0:T(8,128)S(1)}, u32[]{:S(2)}, u32[]{:S(2)}) collective-permute-start(f32[128,1024]{1,0:T(8,128)S(1)} %pad_maximum_fusion.1.refs_0_), channel_id=1, source_target_pairs={{0,2},{1,3},{2,0},{3,1},{4,6},{5,7},{6,4},{7,5},{8,10},{9,11},{10,... | collective-permute-start | bytes 1572872 | tf_op jit(solution)/shard_map/ppermute | solution.py:18
  159.0 35.9 %collective-permute-start.19 = (f32[128,1024]{1,0:T(8,128)S(1)}, f32[128,1024]{1,0:T(8,128)S(1)}, u32[]{:S(2)}, u32[]{:S(2)}) collective-permute-start(f32[128,1024]{1,0:T(8,128)S(1)} %pad_maximum_fusion.1.refs_0_), channel_id=1, source_target_pairs={{0,1},{1,0},{2,3},{3,2},{4,5},{5,4},{6,7},{7,6},{8,9},{9,8},{10,11... | collective-permute-start | bytes 1572872 | tf_op jit(solution)/shard_map/ppermute | solution.py:18
  171.2 24.5 %collective-permute-start.25 = (f32[128,1024]{1,0:T(8,128)S(1)}, f32[128,1024]{1,0:T(8,128)S(1)}, u32[]{:S(2)}, u32[]{:S(2)}) collective-permute-start(f32[128,1024]{1,0:T(8,128)S(1)} %collective-permute-done.24.refs_6_), channel_id=1, source_target_pairs={{0,1},{1,0},{2,3},{3,2},{4,5},{5,4},{6,7},{7,6},{8,9},{9,8},{10,11... | collective-permute-start | bytes 1572872 | tf_op jit(solution)/shard_map/ppermute | solution.py:18
  181.5 16.4 %collective-permute-start.23 = (f32[128,1024]{1,0:T(8,128)S(1)}, f32[128,1024]{1,0:T(8,128)S(1)}, u32[]{:S(2)}, u32[]{:S(2)}) collective-permute-start(f32[128,1024]{1,0:T(8,128)S(1)} %collective-permute-done.22.refs_4_), channel_id=1, source_target_pairs={{0,1},{1,0},{2,3},{3,2},{4,5},{5,4},{6,7},{7,6},{8,9},{9,8},{10,11... | collective-permute-start | bytes 1572872 | tf_op jit(solution)/shard_map/ppermute | solution.py:18
  181.6 17.5 %collective-permute-start.21 = (f32[128,1024]{1,0:T(8,128)S(1)}, f32[128,1024]{1,0:T(8,128)}, u32[]{:S(2)}, u32[]{:S(2)}) collective-permute-start(f32[128,1024]{1,0:T(8,128)S(1)} %collective-permute-done.20.refs_2_), channel_id=1, source_target_pairs={{0,1},{1,0},{2,3},{3,2},{4,5},{5,4},{6,7},{7,6},{8,9},{9,8},{10,11... | collective-permute-start | bytes 1572872 | tf_op jit(solution)/shard_map/ppermute | solution.py:18
  185.1 53.9 %collective-permute-start.30 = (f32[2,128,1024]{2,1,0:T(8,128)}, f32[2,128,1024]{2,1,0:T(8,128)S(1)}, u32[]{:S(2)}, u32[]{:S(2)}) collective-permute-start(f32[2,128,1024]{2,1,0:T(8,128)} %get-tuple-element.139), channel_id=1, source_target_pairs={{0,4},{1,5},{2,6},{3,7},{4,0},{5,1},{6,2},{7,3},{8,12},{9,13},{10,... | collective-permute-start | bytes 3145736 | tf_op jit(solution)/shard_map/ppermute | solution.py:18
  194.9 60.0 %collective-permute-start.32 = (f32[2,128,1024]{2,1,0:T(8,128)}, f32[2,128,1024]{2,1,0:T(8,128)S(1)}, u32[]{:S(2)}, u32[]{:S(2)}) collective-permute-start(f32[2,128,1024]{2,1,0:T(8,128)} %get-tuple-element.138), channel_id=1, source_target_pairs={{0,2},{1,3},{2,0},{3,1},{4,6},{5,7},{6,4},{7,5},{8,10},{9,11},{10,... | collective-permute-start | bytes 3145736 | tf_op jit(solution)/shard_map/ppermute | solution.py:18
  196.6 59.6 %collective-permute-start.31 = (f32[2,128,1024]{2,1,0:T(8,128)}, f32[2,128,1024]{2,1,0:T(8,128)}, u32[]{:S(2)}, u32[]{:S(2)}) collective-permute-start(f32[2,128,1024]{2,1,0:T(8,128)} %get-tuple-element.93), channel_id=1, source_target_pairs={{0,4},{1,5},{2,6},{3,7},{4,0},{5,1},{6,2},{7,3},{8,12},{9,13},{10,... | collective-permute-start | bytes 3145736 | tf_op jit(solution)/shard_map/ppermute | solution.py:18
  198.6 58.0 %collective-permute-start.33 = (f32[2,128,1024]{2,1,0:T(8,128)}, f32[2,128,1024]{2,1,0:T(8,128)}, u32[]{:S(2)}, u32[]{:S(2)}) collective-permute-start(f32[2,128,1024]{2,1,0:T(8,128)} %get-tuple-element.94), channel_id=1, source_target_pairs={{0,2},{1,3},{2,0},{3,1},{4,6},{5,7},{6,4},{7,5},{8,10},{9,11},{10,... | collective-permute-start | bytes 3145736 | tf_op jit(solution)/shard_map/ppermute | solution.py:18
  199.1 69.3 %collective-permute-start.34 = (f32[2,128,1024]{2,1,0:T(8,128)}, f32[2,128,1024]{2,1,0:T(8,128)S(1)}, u32[]{:S(2)}, u32[]{:S(2)}) collective-permute-start(f32[2,128,1024]{2,1,0:T(8,128)} %get-tuple-element.105), channel_id=1, source_target_pairs={{0,4},{1,5},{2,6},{3,7},{4,0},{5,1},{6,2},{7,3},{8,12},{9,13},{10,... | collective-permute-start | bytes 3145736 | tf_op jit(solution)/shard_map/ppermute | solution.py:18
  239.1 30.9 %collective-permute-start.36 = (f32[2,128,1024]{2,1,0:T(8,128)}, f32[2,128,1024]{2,1,0:T(8,128)S(1)}, u32[]{:S(2)}, u32[]{:S(2)}) collective-permute-start(f32[2,128,1024]{2,1,0:T(8,128)} %get-tuple-element.107), channel_id=1, source_target_pairs={{0,2},{1,3},{2,0},{3,1},{4,6},{5,7},{6,4},{7,5},{8,10},{9,11},{10,... | collective-permute-start | bytes 3145736 | tf_op jit(solution)/shard_map/ppermute | solution.py:18
  254.9 23.4 %collective-permute-start.35 = (f32[2,128,1024]{2,1,0:T(8,128)S(1)}, f32[2,128,1024]{2,1,0:T(8,128)S(1)}, u32[]{:S(2)}, u32[]{:S(2)}) collective-permute-start(f32[2,128,1024]{2,1,0:T(8,128)S(1)} %copy-done.22), channel_id=1, source_target_pairs={{0,4},{1,5},{2,6},{3,7},{4,0},{5,1},{6,2},{7,3},{8,12},{9,13},{10,... | collective-permute-start | bytes 3145736 | tf_op jit(solution)/shard_map/ppermute | solution.py:18
  256.2 32.4 %collective-permute-start.37 = (f32[2,128,1024]{2,1,0:T(8,128)S(1)}, f32[2,128,1024]{2,1,0:T(8,128)S(1)}, u32[]{:S(2)}, u32[]{:S(2)}) collective-permute-start(f32[2,128,1024]{2,1,0:T(8,128)S(1)} %copy-done.21), channel_id=1, source_target_pairs={{0,2},{1,3},{2,0},{3,1},{4,6},{5,7},{6,4},{7,5},{8,10},{9,11},{10,... | collective-permute-start | bytes 3145736 | tf_op jit(solution)/shard_map/ppermute | solution.py:18
  268.3 20.3 %collective-permute-start.50 = (f32[4,2,128,128]{3,2,1,0:T(8,128)S(1)}, f32[4,2,128,128]{3,2,1,0:T(8,128)S(1)}, u32[]{:S(2)}, u32[]{:S(2)}) collective-permute-start(f32[4,2,128,128]{3,2,1,0:T(8,128)S(1)} %get-tuple-element.96), channel_id=1, source_target_pairs={{0,1},{1,0},{2,3},{3,2},{4,5},{5,4},{6,7},{7,6},{8,9},{9,8},{10,11... | collective-permute-start | bytes 1572872 | tf_op jit(solution)/shard_map/ppermute | solution.py:18
  268.4 31.5 %collective-permute-start.51 = (f32[4,2,128,128]{3,2,1,0:T(8,128)S(1)}, f32[4,2,128,128]{3,2,1,0:T(8,128)S(1)}, u32[]{:S(2)}, u32[]{:S(2)}) collective-permute-start(f32[4,2,128,128]{3,2,1,0:T(8,128)S(1)} %get-tuple-element.97), channel_id=1, source_target_pairs={{0,2},{1,3},{2,0},{3,1},{4,6},{5,7},{6,4},{7,5},{8,10},{9,11},{10,... | collective-permute-start | bytes 1572872 | tf_op jit(solution)/shard_map/ppermute | solution.py:18
  270.0 29.9 %collective-permute-start.56 = (f32[8,128,128]{2,1,0:T(8,128)S(1)}, f32[8,128,128]{2,1,0:T(8,128)S(1)}, u32[]{:S(2)}, u32[]{:S(2)}) collective-permute-start(f32[8,128,128]{2,1,0:T(8,128)S(1)} %get-tuple-element.75), channel_id=1, source_target_pairs={{0,1},{1,0},{2,3},{3,2},{4,5},{5,4},{6,7},{7,6},{8,9},{9,8},{10,11... | collective-permute-start | bytes 1572872 | tf_op jit(solution)/shard_map/ppermute | solution.py:18
  278.3 32.8 %collective-permute-start.57 = (f32[8,128,128]{2,1,0:T(8,128)S(1)}, f32[8,128,128]{2,1,0:T(8,128)S(1)}, u32[]{:S(2)}, u32[]{:S(2)}) collective-permute-start(f32[8,128,128]{2,1,0:T(8,128)S(1)} %get-tuple-element.76), channel_id=1, source_target_pairs={{0,2},{1,3},{2,0},{3,1},{4,6},{5,7},{6,4},{7,5},{8,10},{9,11},{10,... | collective-permute-start | bytes 1572872 | tf_op jit(solution)/shard_map/ppermute | solution.py:18
  288.6 32.0 %collective-permute-start.58 = (f32[8,128,128]{2,1,0:T(8,128)S(1)}, f32[8,128,128]{2,1,0:T(8,128)S(1)}, u32[]{:S(2)}, u32[]{:S(2)}) collective-permute-start(f32[8,128,128]{2,1,0:T(8,128)S(1)} %get-tuple-element.77), channel_id=1, source_target_pairs={{0,3},{1,2},{2,1},{3,0},{4,7},{5,6},{6,5},{7,4},{8,11},{9,10},{10,... | collective-permute-start | bytes 1572872 | tf_op jit(solution)/shard_map/ppermute | solution.py:18
  288.6 33.2 %collective-permute-start.59 = (f32[8,128,128]{2,1,0:T(8,128)S(1)}, f32[8,128,128]{2,1,0:T(8,128)S(1)}, u32[]{:S(2)}, u32[]{:S(2)}) collective-permute-start(f32[8,128,128]{2,1,0:T(8,128)S(1)} %get-tuple-element.78), channel_id=1, source_target_pairs={{0,4},{1,5},{2,6},{3,7},{4,0},{5,1},{6,2},{7,3},{8,12},{9,13},{10,... | collective-permute-start | bytes 1572872 | tf_op jit(solution)/shard_map/ppermute | solution.py:18
  299.9 22.8 %collective-permute-start.60 = (f32[8,128,128]{2,1,0:T(8,128)S(1)}, f32[8,128,128]{2,1,0:T(8,128)S(1)}, u32[]{:S(2)}, u32[]{:S(2)}) collective-permute-start(f32[8,128,128]{2,1,0:T(8,128)S(1)} %get-tuple-element.79), channel_id=1, source_target_pairs={{0,5},{1,4},{2,7},{3,6},{4,1},{5,0},{6,3},{7,2},{8,13},{9,12},{10,... | collective-permute-start | bytes 1572872 | tf_op jit(solution)/shard_map/ppermute | solution.py:18
  299.9 33.7 %collective-permute-start.61 = (f32[8,128,128]{2,1,0:T(8,128)S(1)}, f32[8,128,128]{2,1,0:T(8,128)S(1)}, u32[]{:S(2)}, u32[]{:S(2)}) collective-permute-start(f32[8,128,128]{2,1,0:T(8,128)S(1)} %get-tuple-element.80), channel_id=1, source_target_pairs={{0,6},{1,7},{2,4},{3,5},{4,2},{5,3},{6,0},{7,1},{8,14},{9,15},{10,... | collective-permute-start | bytes 1572872 | tf_op jit(solution)/shard_map/ppermute | solution.py:18
  311.1 34.8 %collective-permute-start.62 = (f32[8,128,128]{2,1,0:T(8,128)S(1)}, f32[8,128,128]{2,1,0:T(8,128)S(1)}, u32[]{:S(2)}, u32[]{:S(2)}) collective-permute-start(f32[8,128,128]{2,1,0:T(8,128)S(1)} %get-tuple-element.81), channel_id=1, source_target_pairs={{0,7},{1,6},{2,5},{3,4},{4,3},{5,2},{6,1},{7,0},{8,15},{9,14},{10,... | collective-permute-start | bytes 1572872 | tf_op jit(solution)/shard_map/ppermute | solution.py:18
  320.6 79.0 %collective-permute-start.26 = (f32[2,128,1024]{2,1,0:T(8,128)}, f32[2,128,1024]{2,1,0:T(8,128)S(1)}, u32[]{:S(2)}, u32[]{:S(2)}) collective-permute-start(f32[2,128,1024]{2,1,0:T(8,128)} %get-tuple-element.87), channel_id=1, source_target_pairs={{0,4},{1,5},{2,6},{3,7},{4,0},{5,1},{6,2},{7,3},{8,12},{9,13},{10,... | collective-permute-start | bytes 3145736 | tf_op jit(solution)/shard_map/ppermute | solution.py:18
  321.9 78.3 %collective-permute-start.27 = (f32[2,128,1024]{2,1,0:T(8,128)}, f32[2,128,1024]{2,1,0:T(8,128)S(1)}, u32[]{:S(2)}, u32[]{:S(2)}) collective-permute-start(f32[2,128,1024]{2,1,0:T(8,128)} %get-tuple-element.88), channel_id=1, source_target_pairs={{0,4},{1,5},{2,6},{3,7},{4,0},{5,1},{6,2},{7,3},{8,12},{9,13},{10,... | collective-permute-start | bytes 3145736 | tf_op jit(solution)/shard_map/ppermute | solution.py:18
  322.6 78.4 %collective-permute-start.28 = (f32[2,128,1024]{2,1,0:T(8,128)S(1)}, f32[2,128,1024]{2,1,0:T(8,128)S(1)}, u32[]{:S(2)}, u32[]{:S(2)}) collective-permute-start(f32[2,128,1024]{2,1,0:T(8,128)S(1)} %copy-done.20), channel_id=1, source_target_pairs={{0,2},{1,3},{2,0},{3,1},{4,6},{5,7},{6,4},{7,5},{8,10},{9,11},{10,... | collective-permute-start | bytes 3145736 | tf_op jit(solution)/shard_map/ppermute | solution.py:18
  333.6 68.2 %collective-permute-start.29 = (f32[2,128,1024]{2,1,0:T(8,128)S(1)}, f32[2,128,1024]{2,1,0:T(8,128)S(1)}, u32[]{:S(2)}, u32[]{:S(2)}) collective-permute-start(f32[2,128,1024]{2,1,0:T(8,128)S(1)} %copy-done.19), channel_id=1, source_target_pairs={{0,2},{1,3},{2,0},{3,1},{4,6},{5,7},{6,4},{7,5},{8,10},{9,11},{10,... | collective-permute-start | bytes 3145736 | tf_op jit(solution)/shard_map/ppermute | solution.py:18
  345.9 52.6 %collective-permute-start.52 = (f32[4,2,128,128]{3,2,1,0:T(8,128)S(1)}, f32[4,2,128,128]{3,2,1,0:T(8,128)S(1)}, u32[]{:S(2)}, u32[]{:S(2)}) collective-permute-start(f32[4,2,128,128]{3,2,1,0:T(8,128)S(1)} %get-tuple-element.98), channel_id=1, source_target_pairs={{0,3},{1,2},{2,1},{3,0},{4,7},{5,6},{6,5},{7,4},{8,11},{9,10},{10,... | collective-permute-start | bytes 1572872 | tf_op jit(solution)/shard_map/ppermute | solution.py:18
  398.6 14.7 %collective-permute-start.53 = (f32[4,2,128,128]{3,2,1,0:T(8,128)S(1)}, f32[4,2,128,128]{3,2,1,0:T(8,128)S(1)}, u32[]{:S(2)}, u32[]{:S(2)}) collective-permute-start(f32[4,2,128,128]{3,2,1,0:T(8,128)S(1)} %get-tuple-element.100), channel_id=1, source_target_pairs={{0,1},{1,0},{2,3},{3,2},{4,5},{5,4},{6,7},{7,6},{8,9},{9,8},{10,11... | collective-permute-start | bytes 1572872 | tf_op jit(solution)/shard_map/ppermute | solution.py:18
  399.6 14.8 %collective-permute-start.54 = (f32[4,2,128,128]{3,2,1,0:T(8,128)S(1)}, f32[4,2,128,128]{3,2,1,0:T(8,128)S(1)}, u32[]{:S(2)}, u32[]{:S(2)}) collective-permute-start(f32[4,2,128,128]{3,2,1,0:T(8,128)S(1)} %get-tuple-element.101), channel_id=1, source_target_pairs={{0,4},{1,5},{2,6},{3,7},{4,0},{5,1},{6,2},{7,3},{8,12},{9,13},{10,... | collective-permute-start | bytes 1572872 | tf_op jit(solution)/shard_map/ppermute | solution.py:18
  400.2 23.5 %collective-permute-start.55 = (f32[4,2,128,128]{3,2,1,0:T(8,128)S(1)}, f32[4,2,128,128]{3,2,1,0:T(8,128)S(1)}, u32[]{:S(2)}, u32[]{:S(2)}) collective-permute-start(f32[4,2,128,128]{3,2,1,0:T(8,128)S(1)} %get-tuple-element.102), channel_id=1, source_target_pairs={{0,5},{1,4},{2,7},{3,6},{4,1},{5,0},{6,3},{7,2},{8,13},{9,12},{10,... | collective-permute-start | bytes 1572872 | tf_op jit(solution)/shard_map/ppermute | solution.py:18
  401.0 23.3 %collective-permute-start.44 = (f32[4,2,128,128]{3,2,1,0:T(8,128)S(1)}, f32[4,2,128,128]{3,2,1,0:T(8,128)S(1)}, u32[]{:S(2)}, u32[]{:S(2)}) collective-permute-start(f32[4,2,128,128]{3,2,1,0:T(8,128)S(1)} %get-tuple-element.110), channel_id=1, source_target_pairs={{0,1},{1,0},{2,3},{3,2},{4,5},{5,4},{6,7},{7,6},{8,9},{9,8},{10,11... | collective-permute-start | bytes 1572872 | tf_op jit(solution)/shard_map/ppermute | solution.py:18
  401.8 24.4 %collective-permute-start.45 = (f32[4,2,128,128]{3,2,1,0:T(8,128)S(1)}, f32[4,2,128,128]{3,2,1,0:T(8,128)S(1)}, u32[]{:S(2)}, u32[]{:S(2)}) collective-permute-start(f32[4,2,128,128]{3,2,1,0:T(8,128)S(1)} %get-tuple-element.111), channel_id=1, source_target_pairs={{0,2},{1,3},{2,0},{3,1},{4,6},{5,7},{6,4},{7,5},{8,10},{9,11},{10,... | collective-permute-start | bytes 1572872 | tf_op jit(solution)/shard_map/ppermute | solution.py:18
  413.3 22.2 %collective-permute-start.46 = (f32[4,2,128,128]{3,2,1,0:T(8,128)S(1)}, f32[4,2,128,128]{3,2,1,0:T(8,128)S(1)}, u32[]{:S(2)}, u32[]{:S(2)}) collective-permute-start(f32[4,2,128,128]{3,2,1,0:T(8,128)S(1)} %get-tuple-element.112), channel_id=1, source_target_pairs={{0,3},{1,2},{2,1},{3,0},{4,7},{5,6},{6,5},{7,4},{8,11},{9,10},{10,... | collective-permute-start | bytes 1572872 | tf_op jit(solution)/shard_map/ppermute | solution.py:18
  414.4 21.8 %collective-permute-start.47 = (f32[4,2,128,128]{3,2,1,0:T(8,128)S(1)}, f32[4,2,128,128]{3,2,1,0:T(8,128)S(1)}, u32[]{:S(2)}, u32[]{:S(2)}) collective-permute-start(f32[4,2,128,128]{3,2,1,0:T(8,128)S(1)} %get-tuple-element.114), channel_id=1, source_target_pairs={{0,1},{1,0},{2,3},{3,2},{4,5},{5,4},{6,7},{7,6},{8,9},{9,8},{10,11... | collective-permute-start | bytes 1572872 | tf_op jit(solution)/shard_map/ppermute | solution.py:18
  424.3 25.4 %collective-permute-start.49 = (f32[4,2,128,128]{3,2,1,0:T(8,128)S(1)}, f32[4,2,128,128]{3,2,1,0:T(8,128)S(1)}, u32[]{:S(2)}, u32[]{:S(2)}) collective-permute-start(f32[4,2,128,128]{3,2,1,0:T(8,128)S(1)} %get-tuple-element.116), channel_id=1, source_target_pairs={{0,5},{1,4},{2,7},{3,6},{4,1},{5,0},{6,3},{7,2},{8,13},{9,12},{10,... | collective-permute-start | bytes 1572872 | tf_op jit(solution)/shard_map/ppermute | solution.py:18
  426.2 24.2 %collective-permute-start.38 = (f32[4,2,128,128]{3,2,1,0:T(8,128)S(1)}, f32[4,2,128,128]{3,2,1,0:T(8,128)S(1)}, u32[]{:S(2)}, u32[]{:S(2)}) collective-permute-start(f32[4,2,128,128]{3,2,1,0:T(8,128)S(1)} %get-tuple-element.120), channel_id=1, source_target_pairs={{0,1},{1,0},{2,3},{3,2},{4,5},{5,4},{6,7},{7,6},{8,9},{9,8},{10,11... | collective-permute-start | bytes 1572872 | tf_op jit(solution)/shard_map/ppermute | solution.py:18
  435.5 24.9 %collective-permute-start.39 = (f32[4,2,128,128]{3,2,1,0:T(8,128)S(1)}, f32[4,2,128,128]{3,2,1,0:T(8,128)S(1)}, u32[]{:S(2)}, u32[]{:S(2)}) collective-permute-start(f32[4,2,128,128]{3,2,1,0:T(8,128)S(1)} %get-tuple-element.121), channel_id=1, source_target_pairs={{0,2},{1,3},{2,0},{3,1},{4,6},{5,7},{6,4},{7,5},{8,10},{9,11},{10,... | collective-permute-start | bytes 1572872 | tf_op jit(solution)/shard_map/ppermute | solution.py:18
  436.3 24.4 %collective-permute-start.40 = (f32[4,2,128,128]{3,2,1,0:T(8,128)S(1)}, f32[4,2,128,128]{3,2,1,0:T(8,128)S(1)}, u32[]{:S(2)}, u32[]{:S(2)}) collective-permute-start(f32[4,2,128,128]{3,2,1,0:T(8,128)S(1)} %get-tuple-element.122), channel_id=1, source_target_pairs={{0,3},{1,2},{2,1},{3,0},{4,7},{5,6},{6,5},{7,4},{8,11},{9,10},{10,... | collective-permute-start | bytes 1572872 | tf_op jit(solution)/shard_map/ppermute | solution.py:18
  438.4 22.2 %collective-permute-start.41 = (f32[4,2,128,128]{3,2,1,0:T(8,128)S(1)}, f32[4,2,128,128]{3,2,1,0:T(8,128)S(1)}, u32[]{:S(2)}, u32[]{:S(2)}) collective-permute-start(f32[4,2,128,128]{3,2,1,0:T(8,128)S(1)} %get-tuple-element.124), channel_id=1, source_target_pairs={{0,1},{1,0},{2,3},{3,2},{4,5},{5,4},{6,7},{7,6},{8,9},{9,8},{10,11... | collective-permute-start | bytes 1572872 | tf_op jit(solution)/shard_map/ppermute | solution.py:18
  449.8 14.8 %collective-permute-start.42 = (f32[4,2,128,128]{3,2,1,0:T(8,128)S(1)}, f32[4,2,128,128]{3,2,1,0:T(8,128)S(1)}, u32[]{:S(2)}, u32[]{:S(2)}) collective-permute-start(f32[4,2,128,128]{3,2,1,0:T(8,128)S(1)} %get-tuple-element.125), channel_id=1, source_target_pairs={{0,4},{1,5},{2,6},{3,7},{4,0},{5,1},{6,2},{7,3},{8,12},{9,13},{10,... | collective-permute-start | bytes 1572872 | tf_op jit(solution)/shard_map/ppermute | solution.py:18
  450.3 23.5 %collective-permute-start.43 = (f32[4,2,128,128]{3,2,1,0:T(8,128)S(1)}, f32[4,2,128,128]{3,2,1,0:T(8,128)S(1)}, u32[]{:S(2)}, u32[]{:S(2)}) collective-permute-start(f32[4,2,128,128]{3,2,1,0:T(8,128)S(1)} %get-tuple-element.126), channel_id=1, source_target_pairs={{0,5},{1,4},{2,7},{3,6},{4,1},{5,0},{6,3},{7,2},{8,13},{9,12},{10,... | collective-permute-start | bytes 1572872 | tf_op jit(solution)/shard_map/ppermute | solution.py:18
  (38 other events, 482.7 us)

commit v3 on v2

--- a/solution.py
+++ b/solution.py
@@ -114,7 +114,6 @@
 
 lane = 128
 band = 256
-room = pltpu.CompilerParams(vmem_limit_bytes=28 << 20)
 quad = 4
 bf16, f32 = jnp.bfloat16, jnp.float32
 
@@ -135,6 +134,10 @@
 
 def resident(shape):
     return pl.BlockSpec(shape, lambda i: (0,) * len(shape), pipeline_mode=pl.Buffered(1))
+
+
+def room(mebibytes):
+    return pltpu.CompilerParams(vmem_limit_bytes=mebibytes << 20)
 
 
 def cost(flops, data):
@@ -168,7 +171,7 @@
         ),
         out_shape=jax.ShapeDtypeStruct((rows, orbitals), f32),
         cost_estimate=cost(2 * chol_vectors.size, 4 * chol_vectors.size),
-        compiler_params=room,
+        compiler_params=room(10),
         name="gradient_terms",
     )(me, chol_vectors, chol_vectors)
 
@@ -209,9 +212,10 @@
     shards, refs = refs[:devices], refs[devices:]
     step, turned = refs[:2], refs[2:4]
     terms, skew, upper, lower = refs[4:]
-    rows = shards[0].shape[0]
-    for k in range(devices):
-        terms[pl.ds(pl.multiple_of((me_ref[0] ^ k) * rows, rows), rows), :] = shards[k][...]
+    half = shards[0].shape[0]
+    for i, shard in enumerate(shards):
+        start = (me_ref[0] ^ (i // 2)) * (2 * half) + i % 2 * half
+        terms[pl.ds(pl.multiple_of(start, half), half), :] = shard[...]
     total = skew_part(terms, 1.0, skew, upper, lower)
 
     def store(t, at, even, odd):
@@ -224,12 +228,13 @@
 def second_kernel(devices, me_ref, *refs):
     shards, turned, refs = refs[:devices], refs[devices : devices + 2], refs[devices + 2 :]
     ordered, (terms, skew, upper, lower) = refs[:2], refs[2:]
-    rows = shards[0].shape[0]
+    half = shards[0].shape[0]
+    rows = 2 * half
     orbitals = terms.shape[0]
     me = me_ref[0]
-    for k in range(devices):
-        at = pl.ds(pl.multiple_of((me ^ k) * rows, rows), rows)
-        upper[at, :], lower[at, :] = split(shards[k][...])
+    for i, shard in enumerate(shards):
+        at = pl.ds(pl.multiple_of((me ^ (i // 2)) * rows + i % 2 * half, half), half)
+        upper[at, :], lower[at, :] = split(shard[...])
 
     @pl.loop(0, orbitals // band)
     def _(t):
@@ -269,7 +274,7 @@
             pltpu.VMEM(square, bf16),
         ],
         cost_estimate=cost(12 * orbitals**3, 24 * orbitals**2),
-        compiler_params=room,
+        compiler_params=room(18),
     )(me, *shards, *extra)
 
 
@@ -309,7 +314,7 @@
         out_shape=[part] * 4 + [jax.ShapeDtypeStruct((orbitals // devices, orbitals), f32)],
         scratch_shapes=[pltpu.VMEM(square, f32)],
         cost_estimate=cost(6 * orbitals**3, 16 * orbitals**2),
-        compiler_params=room,
+        compiler_params=room(14),
         name="compose",
     )(me, *left, *right)
     return out[:2], out[2:4], out[4]
@@ -342,52 +347,105 @@
         ),
         out_shape=[part, part, jax.ShapeDtypeStruct((vectors, 1, orbitals), f32)],
         cost_estimate=cost(6 * chol_vectors.size * orbitals, 8 * chol_vectors.size),
-        compiler_params=room,
+        compiler_params=room(20),
         name="first_product",
     )(me, chol_vectors, *step, *step)
     return out[:2], out[2]
 
 
-def pieces_kernel(rows, left_upper, left_lower, upper, lower, *outs):
-    count = left_upper.shape[0]
-    left = tuple(r[...].reshape(count * rows, -1) for r in (left_upper, left_lower))
-    value = product(left, (upper[...], lower[...]))
-    for k, out in enumerate(outs):
-        for p in range(count):
-            out[p] = value[p * rows : (p + 1) * rows, k * rows : (k + 1) * rows].T
-
-
-def plain_pieces(lefts, right, vectors, devices):
-    rows, orbitals = lefts[0].shape[1:]
-    block = pl.BlockSpec((quad, rows, orbitals), lambda i: (i, 0, 0))
+def pack_kernel(kept, me_ref, one, two, one_out, two_out):
+    rows = one.shape[1]
+    for source, out, blocks in ((one, one_out, kept[0]), (two, two_out, kept[1])):
+        for j, k in enumerate(blocks):
+            at = pl.ds(pl.multiple_of((me_ref[0] ^ k) * rows, rows), rows)
+            out[:, :, j * rows : (j + 1) * rows] = source[:, :, at]
+
+
+def pack(chol_vectors, me, kept, first, count):
+    vectors, rows, orbitals = chol_vectors.shape
+    width = len(kept[0]) * rows
+    second = vectors // 2 + first
+    out = pl.BlockSpec((2, rows, width), lambda i, me: (i, 0, 0))
     return pl.pallas_call(
-        functools.partial(pieces_kernel, rows),
-        grid=(vectors // quad,),
-        in_specs=[block] * 2 + [resident((orbitals, orbitals))] * 2,
-        out_specs=[pl.BlockSpec((quad, rows, rows), lambda i: (i, 0, 0))] * devices,
-        out_shape=[jax.ShapeDtypeStruct((vectors, rows, rows), f32)] * devices,
-        cost_estimate=cost(6 * vectors * rows * orbitals**2, 8 * vectors * rows * orbitals),
-        compiler_params=room,
-        name="plain_pieces",
-    )(*lefts, *right)
+        functools.partial(pack_kernel, kept),
+        grid_spec=pltpu.PrefetchScalarGridSpec(
+            num_scalar_prefetch=1,
+            grid=(count // 2,),
+            in_specs=[
+                pl.BlockSpec((2, rows, orbitals), lambda i, me: (i + first // 2, 0, 0)),
+                pl.BlockSpec((2, rows, orbitals), lambda i, me: (i + second // 2, 0, 0)),
+            ],
+            out_specs=[out, out],
+        ),
+        out_shape=[jax.ShapeDtypeStruct((count, rows, width), f32)] * 2,
+        cost_estimate=cost(0, 16 * count * rows * orbitals),
+        compiler_params=room(10),
+        name="pack",
+    )(me, chol_vectors, chol_vectors)
+
+
+def siblings_kernel(me_ref, one, two, one_out, two_out):
+    one_out[...] = one[...]
+    two_out[...] = two[...]
+
+
+def for_siblings(chol_vectors, me, bits):
+    vectors, rows, _ = chol_vectors.shape
+    steps = vectors // 2 // quad
+    block = (quad, rows, rows)
+    out = pl.BlockSpec(block, lambda i, me: (i, 0, 0))
+    return pl.pallas_call(
+        siblings_kernel,
+        grid_spec=pltpu.PrefetchScalarGridSpec(
+            num_scalar_prefetch=1,
+            grid=(steps,),
+            in_specs=[
+                pl.BlockSpec(block, lambda i, me, s=s, b=b: (s * steps + i, 0, me[0] ^ b ^ 1))
+                for s, b in enumerate(bits)
+            ],
+            out_specs=[out, out],
+        ),
+        out_shape=[jax.ShapeDtypeStruct((vectors // 2, rows, rows), f32)] * 2,
+        cost_estimate=cost(0, 8 * vectors * rows * rows),
+        compiler_params=room(6),
+        name="for_siblings",
+    )(me, chol_vectors, chol_vectors)
 
 
 def turns(side):
     return (lambda i: jnp.minimum(i, 1)) if side == 0 else (lambda i: jnp.maximum(i - 2, 0))
 
 
-def shared_pieces_kernel(pair, own, *refs):
-    others, (upper, lower), refs = refs[:4], refs[4:6], refs[6:]
+def shared_pieces_kernel(bits, kept, me_ref, own, *refs):
+    others, siblings, (upper, lower), refs = refs[:4], refs[4:6], refs[6:8], refs[8:]
     outs, (left_upper, left_lower, blocks) = refs[:-3], refs[-3:]
     count, rows, orbitals = own.shape
+    pair = orbitals // 4
     half = len(outs) // 2
     step = pl.program_id(0)
     size = count * rows
+    me = me_ref[0]
+
+    def put(block, start, column):
+        at = pl.ds(pl.multiple_of(column * rows, rows), rows)
+        here = pl.ds(start, block.shape[0])
+        left_upper[here, at], left_lower[here, at] = split(block)
+
     left_upper[:size], left_lower[:size] = split(own[...].reshape(size, orbitals))
     for i, other in enumerate(others):
         @pl.when(step == i)
         def _():
-            left_upper[size:], left_lower[size:] = split(other[...].reshape(size, orbitals))
+            for j, k in enumerate(kept[i // 2]):
+                block = other[:, :, j * rows : (j + 1) * rows].reshape(size, rows)
+                put(block, size, me ^ bits[i // 2] ^ k)
+
+    for side in range(2):
+        @pl.when(step // 2 == side)
+        def _():
+            at = pl.ds(pl.multiple_of((me ^ bits[side]) * rows, rows), rows)
+            for p in range(count):
+                put(own[p, :, at].T, size + p * rows, me)
+                put(siblings[side][p].T, size + p * rows, me ^ 1)
 
     left = left_upper[...], left_lower[...]
     middle = pl.ds(pl.multiple_of((1 + step // 2) * pair, pair), pair)
@@ -404,63 +462,55 @@
                 outs[side * half + b][...] = blocks[b]
 
 
-def shared_pieces(near, chol_vectors, starts, others, right):
+def shared_pieces(bits, kept, near, me, chol_vectors, starts, others, siblings, right):
     _, rows, orbitals = chol_vectors.shape
     half = len(near[0])
     first, second = (start // 2 for start in starts)
     specs = [
         pl.BlockSpec(
-            (2, rows, orbitals), lambda i: (jnp.where(i < 2, first + i, second + i - 2), 0, 0)
-        )
-    ] + [resident((2, rows, orbitals))] * 4
+            (2, rows, orbitals),
+            lambda i, me: (jnp.where(i < 2, first + i, second + i - 2), 0, 0),
+        )
+    ]
+    for x, which in others:
+        specs.append(
+            pl.BlockSpec(
+                (2,) + x.shape[1:], lambda i, me, w=which: (w, 0, 0), pipeline_mode=pl.Buffered(1)
+            )
+        )
     outs = []
     for side in range(2):
         turn_of = turns(side)
+        specs.append(
+            pl.BlockSpec((2, rows, rows), lambda i, me, t=turn_of: (first + t(i), 0, 0))
+        )
         outs += [
-            pl.BlockSpec((2, 2, rows, rows), lambda i, t=turn_of: (t(i), 0, 0, 0))
+            pl.BlockSpec((2, 2, rows, rows), lambda i, me, t=turn_of: (t(i), 0, 0, 0))
         ] * half
+    square = pl.BlockSpec(
+        (orbitals, orbitals), lambda i, me: (0, 0), pipeline_mode=pl.Buffered(1)
+    )
     out = pl.pallas_call(
-        functools.partial(shared_pieces_kernel, orbitals // 4),
-        grid=(4,),
-        in_specs=specs + [resident((orbitals, orbitals))] * 2,
-        out_specs=outs,
+        functools.partial(shared_pieces_kernel, bits, kept),
+        grid_spec=pltpu.PrefetchScalarGridSpec(
+            num_scalar_prefetch=1,
+            grid=(4,),
+            in_specs=specs + [square] * 2,
+            out_specs=outs,
+            scratch_shapes=[
+                pltpu.VMEM((4 * rows, orbitals), bf16),
+                pltpu.VMEM((4 * rows, orbitals), bf16),
+                pltpu.VMEM((half, 2, 2, rows, rows), f32),
+            ],
+        ),
         out_shape=[jax.ShapeDtypeStruct((quad, 2, rows, rows), f32)] * (2 * half),
-        scratch_shapes=[
-            pltpu.VMEM((4 * rows, orbitals), bf16),
-            pltpu.VMEM((4 * rows, orbitals), bf16),
-            pltpu.VMEM((half, 2, 2, rows, rows), f32),
-        ],
         cost_estimate=cost(
             12 * quad * rows * orbitals**2, 16 * quad * rows * orbitals
         ),
-        compiler_params=room,
+        compiler_params=room(32),
         name="shared_pieces",
-    )(chol_vectors, *others, *right)
+    )(me, chol_vectors, *(x for x, _ in others), *siblings, *right)
     return out[:half], out[half:]
-
-
-def rotated_kernel(upper, lower, *refs):
-    parts, out_ref = refs[:-1], refs[-1]
-    count, rows, _ = out_ref.shape
-    left = jnp.concatenate([r[...].reshape(count * rows, rows) for r in parts], axis=1)
-    out_ref[...] = product(split(left), (upper[...], lower[...])).reshape(out_ref.shape)
-
-
-def plain_rotated(shape, parts, right):
-    vectors, rows = parts[0].shape[:2]
-    orbitals = shape[2]
-    part = pl.BlockSpec((quad, rows, rows), lambda i: (i, 0, 0))
-    return pl.pallas_call(
-        rotated_kernel,
-        grid=(vectors // quad,),
-        in_specs=[resident((orbitals, orbitals))] * 2
-        + [part] * len(parts),
-        out_specs=pl.BlockSpec((quad, rows, orbitals), lambda i: (i, 0, 0)),
-        out_shape=jax.ShapeDtypeStruct(shape, f32),
-        cost_estimate=cost(6 * vectors * rows * orbitals**2, 8 * vectors * rows * orbitals),
-        compiler_params=room,
-        name="plain_rotated",
-    )(*right, *parts)
 
 
 def shared_rotated_kernel(orders, upper, lower, *refs):
@@ -503,7 +553,7 @@
         input_output_aliases={} if fresh else {count: 0},
         scratch_shapes=[pltpu.VMEM((2 * rows, orbitals), bf16)] * 2,
         cost_estimate=cost(12 * quad * rows * orbitals**2, 16 * quad * rows * orbitals),
-        compiler_params=room,
+        compiler_params=room(16),
         name="shared_rotated",
     )(*right, *parts[0], *parts[1], *([] if fresh else [previous]))
 
@@ -527,7 +577,7 @@
         out_specs=pl.BlockSpec((size, orbitals), lambda i: (i, 0)),
         out_shape=jax.ShapeDtypeStruct((rows, orbitals), f32),
         cost_estimate=cost(2 * lefts[0].size, 4 * lefts[0].size),
-        compiler_params=room,
+        compiler_params=room(8),
         name="second_terms",
     )(*lefts, diagonal)
 
@@ -542,19 +592,26 @@
     masks = [2 ** (b + 1) - 1 for b in range(bits)]
     half = part.shape[0] // 2
     one, two = part[:half], part[half:]
-    for turn_number, (a, b) in enumerate(zip(masks, reversed(masks))):
+    for a, b in zip(masks, reversed(masks)):
         one_more, two_more = flip(one, a), flip(two, b)
         one, two = one + one_more, two + two_more
-        if turn_number == 0:
-            first = one
-    return jnp.concatenate([one, two], axis=0), first
-
-
-def shards_of(part):
+    return one, two
+
+
+def shards_of(one, two):
+    high, low = lax.axis_size("row") // 2, lax.axis_size("row") // 4
+    one_low, two_high = swap(one, low), swap(two, high)
+    one_high, two_low = swap(one, high), swap(two, low)
+    one_both, two_both = swap(one_low, high), swap(two_high, low)
+    halves = {
+        0: (one, two),
+        low: (one_low, two_low),
+        high: (one_high, two_high),
+        low | high: (one_both, two_both),
+    }
     out = []
-    for k in range(0, lax.axis_size("row"), 2):
-        mine = part if k == 0 else swap(part, k)
-        out += [mine, swap(mine, 1)]
+    for k in sorted(halves):
+        out += [*halves[k], *(swap(x, 1) for x in halves[k])]
     return out
 
 
@@ -567,63 +624,61 @@
     vectors, _, _ = shape
     devices = lax.axis_size("row")
     me = lax.axis_index("row").astype(jnp.int32)[None]
-    groups = shared_groups(vectors)
-    plain = vectors - 2 * quad * groups
+    middle = vectors // 2
     bits = (devices // 2, devices // 4)
     everyone = list(range(devices))
     near = [[k for k in everyone if not k & bit] for bit in bits]
+    kept = [[k for k in everyone if k not in (bit, bit ^ 1)] for bit in bits]
     orders = [
         [(near[s].index(k & ~bit), int(bool(k & bit))) for k in everyone]
         for s, bit in enumerate(bits)
     ]
-    starts = [
-        [plain + (s * groups + g) * quad for s in range(2)] for g in range(groups)
-    ]
-
-    early = {}
-
-    def send_early(h, *others):
-        g, i = h // 2, h % 2
-        for s, bit in enumerate(bits):
-            start = starts[g][s] + 2 * i
-            early[g, s, i] = swap(after(own[start], *others), bit)
-
-    def copy_own(source, halves):
-        for h in halves:
-            for s in range(2):
-                start = starts[h // 2][s] + 2 * (h % 2)
-                own[start] = source[start : start + 2]
-
-    own = {}
-    copy_own(chol_vectors, [0])
+
+    eighth = middle // 8
+    packed, place_of = [], []
+    for part, count in enumerate((eighth, 3 * eighth, 2 * eighth, 2 * eighth)):
+        start = len(place_of) * 2
+        packed.append(pack(chol_vectors, me, kept, start, count))
+        place_of += [(part, i) for i in range(count // 2)]
+    blocks = for_siblings(chol_vectors, me, bits)
+    early = []
+
+    def send_early(*others):
+        part = len(early)
+        early.append(
+            [swap(after(x, *others), bit) for x, bit in zip(packed[part], bits)]
+        )
+
     part = gradient_terms(chol_vectors, me)
-    part, first = sum_halves(part)
-    send_early(0)
-    copy_own(after(chol_vectors, first), range(1, 2 * groups))
-    gathered = shards_of(part)
-    send_early(1, *gathered)
-    send_early(2, *gathered)
+    halves = sum_halves(part)
+    send_early()
+    siblings = [swap(x, 1) for x in blocks]
+    gathered = shards_of(*halves)
+    send_early(*gathered)
     *step, turned_upper, turned_lower = make_step(first_kernel, me, gathered, (), 4)
     lefts, diagonal = first_product(chol_vectors, step, me)
     diagonal = sum_over_row(diagonal)
-    send_early(3, diagonal)
+    send_early(diagonal)
     part = second_terms(lefts, diagonal)
-    part, _ = sum_halves(part)
-    gathered = shards_of(part)
-    for h in range(4, 2 * groups):
-        send_early(h, *gathered)
+    gathered = shards_of(*sum_halves(part))
+    send_early(*gathered)
     next_step = make_step(second_kernel, me, gathered, (turned_upper, turned_lower), 2)
-    sent = plain_pieces(lefts, next_step, plain, devices)
-    plain_parts = [sent[0]] + [swap(sent[k], k) for k in everyone[1:]]
-    next_step = lax.optimization_barrier((*next_step, *sent))[:2]
     by_column, by_row, rotation = compose(me, step, next_step, devices)
 
-    shared_parts = []
+    groups = middle // quad
+    starts = [(g * quad, middle + g * quad) for g in range(groups)]
+    parts = []
 
     for g in range(groups):
-        others = [early[g, s, i] for s in range(2) for i in range(2)]
-        sent = shared_pieces(near, chol_vectors, starts[g], others, by_column)
-        shared_parts.append(
+        others = []
+        for s in range(2):
+            for h in (2 * g, 2 * g + 1):
+                window, which = place_of[h]
+                others.append((early[window][s], which))
+        sent = shared_pieces(
+            bits, kept, near, me, chol_vectors, starts[g], others, siblings, by_column
+        )
+        parts.append(
             [
                 [pieces[0]]
                 + [swap(pieces[i], near[s][i]) for i in range(1, len(near[s]))]
@@ -631,21 +686,17 @@
             ]
         )
         by_column = lax.optimization_barrier((*by_column, *sent[0], *sent[1]))[:2]
-    rotated = plain_rotated(shape, plain_parts, by_row)
+    rotated = None
     for g in range(groups):
-        rotated = shared_rotated(rotated, shared_parts[g], orders, starts[g], by_row, shape)
+        rotated = shared_rotated(rotated, parts[g], orders, starts[g], by_row, shape)
     return rotated, rotation
-
-
-def shared_groups(vectors):
-    return (3 * vectors // 4) // (2 * quad)
 
 
 def shards(chol_vectors):
     vectors, rows, _ = chol_vectors.shape
     devices, groups = lax.axis_size("row"), lax.axis_size("vec")
-    tiled = rows % lane == 0 and vectors % (2 * quad) == 0 and devices >= 8
-    if tiled and devices & (devices - 1) == 0 and groups & (groups - 1) == 0:
+    tiled = rows % lane == 0 and vectors % (8 * quad) == 0 and devices == 8
+    if tiled and groups & (groups - 1) == 0:
         return tiled_shards(chol_vectors)
     return plain_shards(chol_vectors)
 

time: 484 us -> 441 us (0.911)
  waiting for transfers between devices: 231 us -> 193 us
  local copies, waits for them, and re-layouts: 35.4 us -> 12 us
  Pallas kernels: 157 us -> 173 us
    ppermute x55 -> x66, waiting for transfers between devices: 186 us -> 148 us  [swap(): return lax.ppermute(x, 'row', [(i, i ^ k) for i in range(count)])]
    unnamed x46 -> x36, local copies, waits for them, and re-layouts: 24 us -> 11.9 us
    slice x2 -> x0, local copies, waits for them, and re-layouts: 11.3 us -> none  [copy_own(): own[start] = source[start:start + 2]]
    pallas_call x3 -> x4, Pallas kernels: 28.1 us -> 38 us  [shared_rotated(): pl.pallas_call(functools.partial(shared_rotated_kernel, orders), grid=(4,...]
    ppermute x55 -> x66, starting transfers between devices: 40.7 us -> 46.9 us  [swap(): return lax.ppermute(x, 'row', [(i, i ^ k) for i in range(count)])]
    ppermute x8, starting transfers between devices: 17.3 us -> 11.3 us  [flip(): return lax.ppermute(x, 'vec', [(i, i ^ k) for i in range(count)])]
    pallas_call x5 -> x9, Pallas kernels: 48.7 us -> 54.3 us  [the longest x4 47.1 us: shared_pieces(): pl.pallas_call(functools.partial(shared_pieces_kernel, bits, kept), grid_...]
  transfers between devices with their start and end apart: 63 -> 74, of which waited for: 32 -> 30; matrix products, arithmetic and copies ran while one was open for 2% -> 0% of each run, Pallas kernels for 20% -> 27%
where the time goes in v3:
time: 441 us; the launch traced here: 437 us
  waiting for transfers between devices  193 us (44%)
  Pallas kernels  173 us (39%)
  starting transfers between devices  58.2 us (13%)
  local copies, waits for them, and re-layouts  12 us (3%)
    ppermute x66, waiting for transfers between devices, swap(): return lax.ppermute(x, 'row', [(i, i ^ k) for i in range(count)])  148 us
    pallas_call x4, Pallas kernels, shared_pieces(): pl.pallas_call(functools.partial(shared_pieces_kernel, bits, kept), grid_...  47.1 us
    ppermute x66, starting transfers between devices, swap(): return lax.ppermute(x, 'row', [(i, i ^ k) for i in range(count)])  46.9 us
    ppermute x8, waiting for transfers between devices, flip(): return lax.ppermute(x, 'vec', [(i, i ^ k) for i in range(count)])  45.5 us
    pallas_call x4, Pallas kernels, shared_rotated(): pl.pallas_call(functools.partial(shared_rotated_kernel, orders), grid=(4,...  38 us
    pallas_call x2, Pallas kernels, make_step(): pl.pallas_call(functools.partial(kernel, devices), in_specs=[pl.BlockSpec...  31.8 us
    pallas_call x1, Pallas kernels, first_product(): pl.pallas_call(first_product_kernel, grid_spec=pltpu.PrefetchScalarGridSp...  31.5 us
    unnamed x36, local copies, waits for them, and re-layouts  11.9 us
  transfers between devices with their start and end apart: 74, of which 30 were waited for; matrix products, arithmetic and copies ran while one was open for 0% of the time, Pallas kernels for 27%

profile of v3, /device:TPU:0, one launch (start us, length us, event | category | flops | bytes accessed | tf_op | source)
XLA Modules:
  0.0 437.4 jit_solution(1225069137110799781)
XLA Ops:
  0.6 5.8 %copy-done = f32[32,128,1024]{2,1,0:T(8,128)S(1)} copy-done((f32[32,128,1024]{2,1,0:T(8,128)S(1)}, f32[32,128,1024]{2,1,0:T(8,128)}, u32[]{:S(2)}) %copy-start) | copy-done | bytes 16777240
  6.4 3.2 gradient_terms.1
  9.7 5.1 %collective-permute-start.2 = (f32[64,1024]{1,0:T(8,128)S(1)}, f32[64,1024]{1,0:T(8,128)S(1)}, u32[]{:S(2)}, u32[]{:S(2)}) collective-permute-start(f32[64,1024]{1,0:T(8,128)S(1)} %get-tuple-element.144), channel_id=1, source_target_pairs={{0,24},{8,16},{16,8},{24,0},{1,25},{9,17},{17,9},{25,1},{2,26},{10... | collective-permute-start | bytes 786440 | tf_op jit(solution)/shard_map/ppermute | solution.py:587
  14.8 7.2 %collective-permute-done.2 = f32[64,1024]{1,0:T(8,128)S(1)} collective-permute-done((f32[64,1024]{1,0:T(8,128)S(1)}, f32[64,1024]{1,0:T(8,128)S(1)}, u32[]{:S(2)}, u32[]{:S(2)}) %collective-permute-start.2) | collective-permute-done | bytes 262176 | tf_op jit(solution)/shard_map/ppermute | solution.py:587
  22.1 4.8 %collective-permute-done = f32[64,1024]{1,0:T(8,128)S(1)} collective-permute-done((f32[64,1024]{1,0:T(8,128)S(1)}, f32[64,1024]{1,0:T(8,128)S(1)}, u32[]{:S(2)}, u32[]{:S(2)}) %collective-permute-start) | collective-permute-done | bytes 262176 | tf_op jit(solution)/shard_map/ppermute | solution.py:587
  29.1 11.8 %collective-permute-done.3 = f32[64,1024]{1,0:T(8,128)S(1)} collective-permute-done((f32[64,1024]{1,0:T(8,128)S(1)}, f32[64,1024]{1,0:T(8,128)S(1)}, u32[]{:S(2)}, u32[]{:S(2)}) %collective-permute-start.3) | collective-permute-done | bytes 262176 | tf_op jit(solution)/shard_map/ppermute | solution.py:587
  45.1 2.2 collective-permute-done.11.refs_9_
  47.3 3.2 collective-permute-done.7.refs_5_
  50.5 2.5 collective-permute-start.15
  52.9 3.1 collective-permute-done.6.refs_4_
  57.1 2.9 collective-permute-done.15.refs_13_
  60.6 1.9 collective-permute-done.14.refs_12_
  64.0 12.0 %shard_map.30 = (bf16[1024,1024]{1,0:T(8,128)(2,1)S(1)}, bf16[1024,1024]{1,0:T(8,128)(2,1)S(1)}, bf16[1024,1024]{1,0:T(8,128)(2,1)S(1)}, bf16[1024,1024]{1,0:T(8,128)(2,1)S(1)}) custom-call(s32[1]{0:T(128)} %bitcast.me_ref, f32[64,1024]{1,0:T(8,128)S(1)} %add.37.refs_0_, f32[64,1024]{1,0:T(8,128)S(1)} %add.39.refs_1_, ...), custom_call_target="tpu_custom_call" | custom-call | flops 12884901888 | bytes 25165824 | tf_op jit(solution)/shard_map/pallas_call | solution.py:264
  78.8 31.5 %first_product.1 = (bf16[32,128,1024]{2,1,0:T(8,128)(2,1)S(1)}, bf16[32,128,1024]{2,1,0:T(8,128)(2,1)S(1)}, f32[32,1,1024]{2,1,0:T(1,128)S(1)}) custom-call(s32[1]{0:T(128)} %bitcast.me_ref, f32[32,128,1024]{2,1,0:T(8,128)} %own.7, bf16[1024,1024]{1,0:T(8,128)(2,1)S(1)} %get-tuple-element.70.upper.rows_upper.left_upper, ...), custom_call_target="tpu_custom_call" | custom-call | flops 25769803776 | bytes 33554432 | tf_op jit(solution)/shard_map/first_product/pallas_call | solution.py:340
  110.3 3.4 copy-done.1
  115.2 2.0 collective-permute-start.21
  117.2 2.0 collective-permute-start.20
  119.5 2.1 collective-permute-start.46
  122.4 2.2 collective-permute-done.20
  125.6 5.1 %second_terms.1 = f32[128,1024]{1,0:T(8,128)S(1)} custom-call(bf16[32,128,1024]{2,1,0:T(8,128)(2,1)S(1)} %bitcast.9, bf16[32,128,1024]{2,1,0:T(8,128)(2,1)S(1)} %copy-done.3, f32[32,1,1024]{2,1,0:T(1,128)S(1)} %bitcast.10), custom_call_target="tpu_custom_call" | custom-call | flops 8388608 | bytes 16777216 | tf_op jit(solution)/shard_map/second_terms/pallas_call | solution.py:573
  131.6 10.3 %collective-permute-done.24 = f32[64,1024]{1,0:T(8,128)S(1)} collective-permute-done((f32[64,1024]{1,0:T(8,128)S(1)}, f32[64,1024]{1,0:T(8,128)S(1)}, u32[]{:S(2)}, u32[]{:S(2)}) %collective-permute-start.24) | collective-permute-done | bytes 262176 | tf_op jit(solution)/shard_map/ppermute | solution.py:587
  141.9 2.4 collective-permute-done.22
  144.7 3.5 collective-permute-start.23
  148.2 3.5 collective-permute-done.25
  153.2 5.5 %collective-permute-done.23 = f32[64,1024]{1,0:T(8,128)S(1)} collective-permute-done((f32[64,1024]{1,0:T(8,128)S(1)}, f32[64,1024]{1,0:T(8,128)S(1)}, u32[]{:S(2)}, u32[]{:S(2)}) %collective-permute-start.23) | collective-permute-done | bytes 262176 | tf_op jit(solution)/shard_map/ppermute | solution.py:587
  162.1 2.7 pack.6
  164.8 2.7 collective-permute-done.32.refs_8_
  170.1 4.6 %collective-permute-done.37.refs_13_ = f32[64,1024]{1,0:T(8,128)S(1)} collective-permute-done((f32[64,1024]{1,0:T(8,128)S(1)}, f32[64,1024]{1,0:T(8,128)S(1)}, u32[]{:S(2)}, u32[]{:S(2)}) %collective-permute-start.37) | collective-permute-done | bytes 262176 | tf_op jit(solution)/shard_map/ppermute | solution.py:18
  176.3 51.1 %collective-permute-done.36.refs_12_ = f32[64,1024]{1,0:T(8,128)S(1)} collective-permute-done((f32[64,1024]{1,0:T(8,128)S(1)}, f32[64,1024]{1,0:T(8,128)S(1)}, u32[]{:S(2)}, u32[]{:S(2)}) %collective-permute-start.36) | collective-permute-done | bytes 262176 | tf_op jit(solution)/shard_map/ppermute | solution.py:18
  229.3 1.9 pack.4
  233.5 19.8 %shard_map.31 = (bf16[1024,1024]{1,0:T(8,128)(2,1)S(1)}, bf16[1024,1024]{1,0:T(8,128)(2,1)S(1)}) custom-call(s32[1]{0:T(128)} %bitcast.me_ref, f32[64,1024]{1,0:T(8,128)S(1)} %add.45.refs_0_, f32[64,1024]{1,0:T(8,128)S(1)} %add.47.refs_1_, f32[64,1024]{1,0:T(8,128)S(1)} %collective-permute-done.26.refs_2_, f32[64,1024]{1,0:T(8,128)S(1)} %collective-permute-done.27.refs_3_, ...), custom_call_target="tpu_custom_call" | custom-call | flops 12884901888 | bytes 25165824 | tf_op jit(solution)/shard_map/pallas_call | solution.py:264
  253.3 8.7 %compose.1 = (bf16[1024,1024]{1,0:T(8,128)(2,1)S(1)}, bf16[1024,1024]{1,0:T(8,128)(2,1)S(1)}, bf16[1024,1024]{1,0:T(8,128)(2,1)S(1)}, bf16[1024,1024]{1,0:T(8,128)(2,1)S(1)}, f32[128,1024]{1,0:T(8,128)}) custom-call(s32[1]{0:T(128)} %bitcast.me_ref, bf16[1024,1024]{1,0:T(8,128)(2,1)S(1)} %copy-done.5, bf16[1024,1024]{1,0:T(8,128)(2,1)S(1)} %copy-done.7, ...), custom_call_target="tpu_custom_call" | custom-call | flops 6442450944 | bytes 16777216 | tf_op jit(solution)/shard_map/compose/pallas_call | solution.py:310
  264.3 11.8 %shared_pieces.4 = (f32[4,2,128,128]{3,2,1,0:T(8,128)S(1)}, f32[4,2,128,128]{3,2,1,0:T(8,128)S(1)}, f32[4,2,128,128]{3,2,1,0:T(8,128)S(1)}, f32[4,2,128,128]{3,2...) custom-call(s32[1]{0:T(128)} %bitcast.me_ref, ...), custom_call_target="tpu_custom_call" | custom-call | flops 6442450944 | bytes 8388608 | tf_op jit(solution)/shard_map/shared_pieces/pallas_call | solution.py:493
  278.0 11.8 %shared_pieces.5 = (f32[4,2,128,128]{3,2,1,0:T(8,128)S(1)}, f32[4,2,128,128]{3,2,1,0:T(8,128)S(1)}, f32[4,2,128,128]{3,2,1,0:T(8,128)S(1)}, f32[4,2,128,128]{3,2...) custom-call(s32[1]{0:T(128)} %bitcast.me_ref, ...), custom_call_target="tpu_custom_call" | custom-call | flops 6442450944 | bytes 8388608 | tf_op jit(solution)/shard_map/shared_pieces/pallas_call | solution.py:493
  290.2 24.3 %collective-permute-done.69.refs_2_ = f32[4,2,128,128]{3,2,1,0:T(8,128)S(1)} collective-permute-done((f32[4,2,128,128]{3,2,1,0:T(8,128)S(1)}, f32[4,2,128,128]{3,2,1,0:T(8,128)S(1)}, u32[]{:S(2)}, u32[]{:S(2)}) %collective-permute-start.69) | collective-permute-done | bytes 524320 | tf_op jit(solution)/shard_map/ppermute | solution.py:18
  316.2 7.3 %collective-permute-done.70.refs_3_ = f32[4,2,128,128]{3,2,1,0:T(8,128)S(1)} collective-permute-done((f32[4,2,128,128]{3,2,1,0:T(8,128)S(1)}, f32[4,2,128,128]{3,2,1,0:T(8,128)S(1)}, u32[]{:S(2)}, u32[]{:S(2)}) %collective-permute-start.70) | collective-permute-done | bytes 524320 | tf_op jit(solution)/shard_map/ppermute | solution.py:18
  323.5 2.5 collective-permute-start.73
  326.0 11.8 %shared_pieces.6 = (f32[4,2,128,128]{3,2,1,0:T(8,128)S(1)}, f32[4,2,128,128]{3,2,1,0:T(8,128)S(1)}, f32[4,2,128,128]{3,2,1,0:T(8,128)S(1)}, f32[4,2,128,128]{3,2...) custom-call(s32[1]{0:T(128)} %bitcast.me_ref, ...), custom_call_target="tpu_custom_call" | custom-call | flops 6442450944 | bytes 8388608 | tf_op jit(solution)/shard_map/shared_pieces/pallas_call | solution.py:493
  339.7 9.5 %shared_rotated.4.refs_8_ = f32[32,128,1024]{2,1,0:T(8,128)} custom-call(bf16[1024,1024]{1,0:T(8,128)(2,1)S(1)} %get-tuple-element.79.upper, bf16[1024,1024]{1,0:T(8,128)(2,1)S(1)} %get-tuple-element.80.lower, f32[4,2,128,128]{3,2,1,0:T(8,128)S(1)} %get-tuple-element.95.refs_0_, f32[4,2,128,128]{3,2,1,0:T(8,128)S(1)} %collective-permute-done.68.refs_1_, ...), custom_call_target="tpu_custom_call" | custom-call | flops 6442450944 | bytes 8388608 | tf_op jit(solution)/shard_map/shared_rotated/pallas_call | solution.py:543
  349.6 3.1 collective-permute-done.63.refs_2_
  353.1 9.8 %collective-permute-done.64.refs_3_ = f32[4,2,128,128]{3,2,1,0:T(8,128)S(1)} collective-permute-done((f32[4,2,128,128]{3,2,1,0:T(8,128)S(1)}, f32[4,2,128,128]{3,2,1,0:T(8,128)S(1)}, u32[]{:S(2)}, u32[]{:S(2)}) %collective-permute-start.64) | collective-permute-done | bytes 524320 | tf_op jit(solution)/shard_map/ppermute | solution.py:18
  364.9 11.8 %shared_pieces.7 = (f32[4,2,128,128]{3,2,1,0:T(8,128)S(1)}, f32[4,2,128,128]{3,2,1,0:T(8,128)S(1)}, f32[4,2,128,128]{3,2,1,0:T(8,128)S(1)}, f32[4,2,128,128]{3,2...) custom-call(s32[1]{0:T(128)} %bitcast.me_ref, ...), custom_call_target="tpu_custom_call" | custom-call | flops 6442450944 | bytes 8388608 | tf_op jit(solution)/shard_map/shared_pieces/pallas_call | solution.py:493
  379.7 9.5 %shared_rotated.5.refs_8_ = f32[32,128,1024]{2,1,0:T(8,128)} custom-call(bf16[1024,1024]{1,0:T(8,128)(2,1)S(1)} %get-tuple-element.79.upper, bf16[1024,1024]{1,0:T(8,128)(2,1)S(1)} %get-tuple-element.80.lower, f32[4,2,128,128]{3,2,1,0:T(8,128)S(1)} %get-tuple-element.105.refs_0_, ...), custom_call_target="tpu_custom_call", output_to_operand_aliasing={{}: (10, {})} | custom-call | flops 6442450944 | bytes 8388608 | tf_op jit(solution)/shard_map/shared_rotated/pallas_call | solution.py:543
  392.8 9.1 %collective-permute-done.61.refs_7_ = f32[4,2,128,128]{3,2,1,0:T(8,128)S(1)} collective-permute-done((f32[4,2,128,128]{3,2,1,0:T(8,128)S(1)}, f32[4,2,128,128]{3,2,1,0:T(8,128)S(1)}, u32[]{:S(2)}, u32[]{:S(2)}) %collective-permute-start.61) | collective-permute-done | bytes 524320 | tf_op jit(solution)/shard_map/ppermute | solution.py:18
  404.2 9.5 %shared_rotated.6.refs_8_ = f32[32,128,1024]{2,1,0:T(8,128)} custom-call(bf16[1024,1024]{1,0:T(8,128)(2,1)S(1)} %get-tuple-element.79.upper, bf16[1024,1024]{1,0:T(8,128)(2,1)S(1)} %get-tuple-element.80.lower, f32[4,2,128,128]{3,2,1,0:T(8,128)S(1)} %get-tuple-element.119.refs_0_, ...), custom_call_target="tpu_custom_call", output_to_operand_aliasing={{}: (10, {})} | custom-call | flops 6442450944 | bytes 8388608 | tf_op jit(solution)/shard_map/shared_rotated/pallas_call | solution.py:543
  413.7 1.9 collective-permute-done.52.refs_3_
  416.7 11.2 %collective-permute-done.55.refs_7_ = f32[4,2,128,128]{3,2,1,0:T(8,128)S(1)} collective-permute-done((f32[4,2,128,128]{3,2,1,0:T(8,128)S(1)}, f32[4,2,128,128]{3,2,1,0:T(8,128)S(1)}, u32[]{:S(2)}, u32[]{:S(2)}) %collective-permute-start.55) | collective-permute-done | bytes 524320 | tf_op jit(solution)/shard_map/ppermute | solution.py:18
  427.9 9.5 %shared_rotated.7 = f32[32,128,1024]{2,1,0:T(8,128)} custom-call(bf16[1024,1024]{1,0:T(8,128)(2,1)S(1)} %get-tuple-element.79.upper, bf16[1024,1024]{1,0:T(8,128)(2,1)S(1)} %get-tuple-element.80.lower, f32[4,2,128,128]{3,2,1,0:T(8,128)S(1)} %get-tuple-element.129.refs_0_, ...), custom_call_target="tpu_custom_call", output_to_operand_aliasing={{}: (10, {})} | custom-call | flops 6442450944 | bytes 8388608 | tf_op jit(solution)/shard_map/shared_rotated/pallas_call | solution.py:543
  (167 shorter events, 51.3 us)
Async XLA Ops:
  9.7 12.4 %collective-permute-start.2 = (f32[64,1024]{1,0:T(8,128)S(1)}, f32[64,1024]{1,0:T(8,128)S(1)}, u32[]{:S(2)}, u32[]{:S(2)}) collective-permute-start(f32[64,1024]{1,0:T(8,128)S(1)} %get-tuple-element.144), channel_id=1, source_target_pairs={{0,24},{8,16},{16,8},{24,0},{1,25},{9,17},{17,9},{25,1},{2,26},{10... | collective-permute-start | bytes 786440 | tf_op jit(solution)/shard_map/ppermute | solution.py:587
  14.8 12.0 %collective-permute-start = (f32[64,1024]{1,0:T(8,128)S(1)}, f32[64,1024]{1,0:T(8,128)S(1)}, u32[]{:S(2)}, u32[]{:S(2)}) collective-permute-start(f32[64,1024]{1,0:T(8,128)S(1)} %get-tuple-element.145), channel_id=1, source_target_pairs={{0,8},{8,0},{16,24},{24,16},{1,9},{9,1},{17,25},{25,17},{2,10},{10... | collective-permute-start | bytes 786440 | tf_op jit(solution)/shard_map/ppermute | solution.py:587
  26.9 13.9 %collective-permute-start.3 = (f32[64,1024]{1,0:T(8,128)S(1)}, f32[64,1024]{1,0:T(8,128)S(1)}, u32[]{:S(2)}, u32[]{:S(2)}) collective-permute-start(f32[64,1024]{1,0:T(8,128)S(1)} %get-tuple-element.142), channel_id=1, source_target_pairs={{0,8},{8,0},{16,24},{24,16},{1,9},{9,1},{17,25},{25,17},{2,10},{10... | collective-permute-start | bytes 786440 | tf_op jit(solution)/shard_map/ppermute | solution.py:587
  28.7 15.3 %collective-permute-start.1 = (f32[64,1024]{1,0:T(8,128)S(1)}, f32[64,1024]{1,0:T(8,128)S(1)}, u32[]{:S(2)}, u32[]{:S(2)}) collective-permute-start(f32[64,1024]{1,0:T(8,128)S(1)} %get-tuple-element.143), channel_id=1, source_target_pairs={{0,24},{8,16},{16,8},{24,0},{1,25},{9,17},{17,9},{25,1},{2,26},{10... | collective-permute-start | bytes 786440 | tf_op jit(solution)/shard_map/ppermute | solution.py:587
  44.0 12.1 %collective-permute-start.6 = (f32[64,1024]{1,0:T(8,128)S(1)}, f32[64,1024]{1,0:T(8,128)S(1)}, u32[]{:S(2)}, u32[]{:S(2)}) collective-permute-start(f32[64,1024]{1,0:T(8,128)S(1)} %add.37.refs_0_), channel_id=1, source_target_pairs={{0,2},{1,3},{2,0},{3,1},{4,6},{5,7},{6,4},{7,5},{8,10},{9,11},{10,... | collective-permute-start | bytes 786440 | tf_op jit(solution)/shard_map/ppermute | solution.py:18
  44.6 12.0 %collective-permute-start.10 = (f32[64,1024]{1,0:T(8,128)S(1)}, f32[64,1024]{1,0:T(8,128)S(1)}, u32[]{:S(2)}, u32[]{:S(2)}) collective-permute-start(f32[64,1024]{1,0:T(8,128)S(1)} %add.37.refs_0_), channel_id=1, source_target_pairs={{0,4},{1,5},{2,6},{3,7},{4,0},{5,1},{6,2},{7,3},{8,12},{9,13},{10,... | collective-permute-start | bytes 786440 | tf_op jit(solution)/shard_map/ppermute | solution.py:18
  119.5 33.1 %collective-permute-start.46 = (f32[2,128,768]{2,1,0:T(8,128)S(1)}, f32[2,128,768]{2,1,0:T(8,128)S(1)}, u32[]{:S(2)}, u32[]{:S(2)}) collective-permute-start(f32[2,128,768]{2,1,0:T(8,128)S(1)} %get-tuple-element.92), channel_id=1, source_target_pairs={{0,2},{1,3},{2,0},{3,1},{4,6},{5,7},{6,4},{7,5},{8,10},{9,11},{10,... | collective-permute-start | bytes 2359304 | tf_op jit(solution)/shard_map/ppermute | solution.py:18
  122.1 37.7 %collective-permute-start.42 = (f32[16,128,128]{2,1,0:T(8,128)S(1)}, f32[16,128,128]{2,1,0:T(8,128)S(1)}, u32[]{:S(2)}, u32[]{:S(2)}) collective-permute-start(f32[16,128,128]{2,1,0:T(8,128)S(1)} %get-tuple-element.85), channel_id=1, source_target_pairs={{0,1},{1,0},{2,3},{3,2},{4,5},{5,4},{6,7},{7,6},{8,9},{9,8},{10,11... | collective-permute-start | bytes 3145736 | tf_op jit(solution)/shard_map/ppermute | solution.py:18
  130.8 11.0 %collective-permute-start.24 = (f32[64,1024]{1,0:T(8,128)S(1)}, f32[64,1024]{1,0:T(8,128)S(1)}, u32[]{:S(2)}, u32[]{:S(2)}) collective-permute-start(f32[64,1024]{1,0:T(8,128)S(1)} %get-tuple-element.140), channel_id=1, source_target_pairs={{0,24},{8,16},{16,8},{24,0},{1,25},{9,17},{17,9},{25,1},{2,26},{10... | collective-permute-start | bytes 786440 | tf_op jit(solution)/shard_map/ppermute | solution.py:587
  130.9 13.4 %collective-permute-start.22 = (f32[64,1024]{1,0:T(8,128)S(1)}, f32[64,1024]{1,0:T(8,128)S(1)}, u32[]{:S(2)}, u32[]{:S(2)}) collective-permute-start(f32[64,1024]{1,0:T(8,128)S(1)} %get-tuple-element.141), channel_id=1, source_target_pairs={{0,8},{8,0},{16,24},{24,16},{1,9},{9,1},{17,25},{25,17},{2,10},{10... | collective-permute-start | bytes 786440 | tf_op jit(solution)/shard_map/ppermute | solution.py:587
  131.0 27.8 %collective-permute-start.44 = (f32[2,128,768]{2,1,0:T(8,128)S(1)}, f32[2,128,768]{2,1,0:T(8,128)S(1)}, u32[]{:S(2)}, u32[]{:S(2)}) collective-permute-start(f32[2,128,768]{2,1,0:T(8,128)S(1)} %get-tuple-element.89), channel_id=1, source_target_pairs={{0,4},{1,5},{2,6},{3,7},{4,0},{5,1},{6,2},{7,3},{8,12},{9,13},{10,... | collective-permute-start | bytes 2359304 | tf_op jit(solution)/shard_map/ppermute | solution.py:18
  144.7 14.0 %collective-permute-start.23 = (f32[64,1024]{1,0:T(8,128)S(1)}, f32[64,1024]{1,0:T(8,128)S(1)}, u32[]{:S(2)}, u32[]{:S(2)}) collective-permute-start(f32[64,1024]{1,0:T(8,128)S(1)} %get-tuple-element.139), channel_id=1, source_target_pairs={{0,24},{8,16},{16,8},{24,0},{1,25},{9,17},{17,9},{25,1},{2,26},{10... | collective-permute-start | bytes 786440 | tf_op jit(solution)/shard_map/ppermute | solution.py:587
  160.7 13.9 %collective-permute-start.37 = (f32[64,1024]{1,0:T(8,128)S(1)}, f32[64,1024]{1,0:T(8,128)S(1)}, u32[]{:S(2)}, u32[]{:S(2)}) collective-permute-start(f32[64,1024]{1,0:T(8,128)S(1)} %collective-permute-done.33.refs_9_), channel_id=1, source_target_pairs={{0,2},{1,3},{2,0},{3,1},{4,6},{5,7},{6,4},{7,5},{8,10},{9,11},{10,... | collective-permute-start | bytes 786440 | tf_op jit(solution)/shard_map/ppermute | solution.py:18
  162.0 12.7 %collective-permute-start.35 = (f32[64,1024]{1,0:T(8,128)S(1)}, f32[64,1024]{1,0:T(8,128)S(1)}, u32[]{:S(2)}, u32[]{:S(2)}) collective-permute-start(f32[64,1024]{1,0:T(8,128)S(1)} %collective-permute-done.33.refs_9_), channel_id=1, source_target_pairs={{0,1},{1,0},{2,3},{3,2},{4,5},{5,4},{6,7},{7,6},{8,9},{9,8},{10,11... | collective-permute-start | bytes 786440 | tf_op jit(solution)/shard_map/ppermute | solution.py:18
  167.6 95.2 %collective-permute-start.47 = (f32[6,128,768]{2,1,0:T(8,128)}, f32[6,128,768]{2,1,0:T(8,128)S(1)}, u32[]{:S(2)}, u32[]{:S(2)}) collective-permute-start(f32[6,128,768]{2,1,0:T(8,128)} %get-tuple-element.94), channel_id=1, source_target_pairs={{0,2},{1,3},{2,0},{3,1},{4,6},{5,7},{6,4},{7,5},{8,10},{9,11},{10,... | collective-permute-start | bytes 7077896 | tf_op jit(solution)/shard_map/ppermute | solution.py:18
  169.1 95.2 %collective-permute-start.45 = (f32[6,128,768]{2,1,0:T(8,128)}, f32[6,128,768]{2,1,0:T(8,128)S(1)}, u32[]{:S(2)}, u32[]{:S(2)}) collective-permute-start(f32[6,128,768]{2,1,0:T(8,128)} %get-tuple-element.91), channel_id=1, source_target_pairs={{0,4},{1,5},{2,6},{3,7},{4,0},{5,1},{6,2},{7,3},{8,12},{9,13},{10,... | collective-permute-start | bytes 7077896 | tf_op jit(solution)/shard_map/ppermute | solution.py:18
  174.6 52.8 %collective-permute-start.36 = (f32[64,1024]{1,0:T(8,128)S(1)}, f32[64,1024]{1,0:T(8,128)S(1)}, u32[]{:S(2)}, u32[]{:S(2)}) collective-permute-start(f32[64,1024]{1,0:T(8,128)S(1)} %collective-permute-done.28.refs_4_), channel_id=1, source_target_pairs={{0,4},{1,5},{2,6},{3,7},{4,0},{5,1},{6,2},{7,3},{8,12},{9,13},{10,... | collective-permute-start | bytes 786440 | tf_op jit(solution)/shard_map/ppermute | solution.py:18
  175.7 55.5 %collective-permute-start.30 = (f32[64,1024]{1,0:T(8,128)S(1)}, f32[64,1024]{1,0:T(8,128)S(1)}, u32[]{:S(2)}, u32[]{:S(2)}) collective-permute-start(f32[64,1024]{1,0:T(8,128)S(1)} %collective-permute-done.28.refs_4_), channel_id=1, source_target_pairs={{0,1},{1,0},{2,3},{3,2},{4,5},{5,4},{6,7},{7,6},{8,9},{9,8},{10,11... | collective-permute-start | bytes 786440 | tf_op jit(solution)/shard_map/ppermute | solution.py:18
  176.2 55.6 %collective-permute-start.39 = (f32[64,1024]{1,0:T(8,128)S(1)}, f32[64,1024]{1,0:T(8,128)S(1)}, u32[]{:S(2)}, u32[]{:S(2)}) collective-permute-start(f32[64,1024]{1,0:T(8,128)S(1)} %collective-permute-done.37.refs_13_), channel_id=1, source_target_pairs={{0,1},{1,0},{2,3},{3,2},{4,5},{5,4},{6,7},{7,6},{8,9},{9,8},{10,11... | collective-permute-start | bytes 786440 | tf_op jit(solution)/shard_map/ppermute | solution.py:18
  231.2 30.8 %collective-permute-start.43 = (f32[16,128,128]{2,1,0:T(8,128)S(1)}, f32[16,128,128]{2,1,0:T(8,128)S(1)}, u32[]{:S(2)}, u32[]{:S(2)}) collective-permute-start(f32[16,128,128]{2,1,0:T(8,128)S(1)} %get-tuple-element.86), channel_id=1, source_target_pairs={{0,1},{1,0},{2,3},{3,2},{4,5},{5,4},{6,7},{7,6},{8,9},{9,8},{10,11... | collective-permute-start | bytes 3145736 | tf_op jit(solution)/shard_map/ppermute | solution.py:18
  231.7 44.4 %collective-permute-start.48 = (f32[4,128,768]{2,1,0:T(8,128)}, f32[4,128,768]{2,1,0:T(8,128)S(1)}, u32[]{:S(2)}, u32[]{:S(2)}) collective-permute-start(f32[4,128,768]{2,1,0:T(8,128)} %get-tuple-element.116), channel_id=1, source_target_pairs={{0,4},{1,5},{2,6},{3,7},{4,0},{5,1},{6,2},{7,3},{8,12},{9,13},{10,... | collective-permute-start | bytes 4718600 | tf_op jit(solution)/shard_map/ppermute | solution.py:18
  232.1 44.6 %collective-permute-start.49 = (f32[4,128,768]{2,1,0:T(8,128)}, f32[4,128,768]{2,1,0:T(8,128)S(1)}, u32[]{:S(2)}, u32[]{:S(2)}) collective-permute-start(f32[4,128,768]{2,1,0:T(8,128)} %get-tuple-element.118), channel_id=1, source_target_pairs={{0,2},{1,3},{2,0},{3,1},{4,6},{5,7},{6,4},{7,5},{8,10},{9,11},{10,... | collective-permute-start | bytes 4718600 | tf_op jit(solution)/shard_map/ppermute | solution.py:18
  262.0 101.5 %collective-permute-start.40 = (f32[4,128,768]{2,1,0:T(8,128)}, f32[4,128,768]{2,1,0:T(8,128)S(1)}, u32[]{:S(2)}, u32[]{:S(2)}) collective-permute-start(f32[4,128,768]{2,1,0:T(8,128)} %get-tuple-element.82), channel_id=1, source_target_pairs={{0,4},{1,5},{2,6},{3,7},{4,0},{5,1},{6,2},{7,3},{8,12},{9,13},{10,... | collective-permute-start | bytes 4718600 | tf_op jit(solution)/shard_map/ppermute | solution.py:18
  262.8 100.8 %collective-permute-start.41 = (f32[4,128,768]{2,1,0:T(8,128)}, f32[4,128,768]{2,1,0:T(8,128)S(1)}, u32[]{:S(2)}, u32[]{:S(2)}) collective-permute-start(f32[4,128,768]{2,1,0:T(8,128)} %get-tuple-element.84), channel_id=1, source_target_pairs={{0,2},{1,3},{2,0},{3,1},{4,6},{5,7},{6,4},{7,5},{8,10},{9,11},{10,... | collective-permute-start | bytes 4718600 | tf_op jit(solution)/shard_map/ppermute | solution.py:18
  276.1 13.7 %collective-permute-start.68 = (f32[4,2,128,128]{3,2,1,0:T(8,128)S(1)}, f32[4,2,128,128]{3,2,1,0:T(8,128)S(1)}, u32[]{:S(2)}, u32[]{:S(2)}) collective-permute-start(f32[4,2,128,128]{3,2,1,0:T(8,128)S(1)} %get-tuple-element.96), channel_id=1, source_target_pairs={{0,1},{1,0},{2,3},{3,2},{4,5},{5,4},{6,7},{7,6},{8,9},{9,8},{10,11... | collective-permute-start | bytes 1572872 | tf_op jit(solution)/shard_map/ppermute | solution.py:18
  276.1 38.4 %collective-permute-start.69 = (f32[4,2,128,128]{3,2,1,0:T(8,128)S(1)}, f32[4,2,128,128]{3,2,1,0:T(8,128)S(1)}, u32[]{:S(2)}, u32[]{:S(2)}) collective-permute-start(f32[4,2,128,128]{3,2,1,0:T(8,128)S(1)} %get-tuple-element.97), channel_id=1, source_target_pairs={{0,2},{1,3},{2,0},{3,1},{4,6},{5,7},{6,4},{7,5},{8,10},{9,11},{10,... | collective-permute-start | bytes 1572872 | tf_op jit(solution)/shard_map/ppermute | solution.py:18
  276.7 46.8 %collective-permute-start.70 = (f32[4,2,128,128]{3,2,1,0:T(8,128)S(1)}, f32[4,2,128,128]{3,2,1,0:T(8,128)S(1)}, u32[]{:S(2)}, u32[]{:S(2)}) collective-permute-start(f32[4,2,128,128]{3,2,1,0:T(8,128)S(1)} %get-tuple-element.98), channel_id=1, source_target_pairs={{0,3},{1,2},{2,1},{3,0},{4,7},{5,6},{6,5},{7,4},{8,11},{9,10},{10,... | collective-permute-start | bytes 1572872 | tf_op jit(solution)/shard_map/ppermute | solution.py:18
  289.8 48.0 %collective-permute-start.71 = (f32[4,2,128,128]{3,2,1,0:T(8,128)S(1)}, f32[4,2,128,128]{3,2,1,0:T(8,128)S(1)}, u32[]{:S(2)}, u32[]{:S(2)}) collective-permute-start(f32[4,2,128,128]{3,2,1,0:T(8,128)S(1)} %get-tuple-element.100), channel_id=1, source_target_pairs={{0,1},{1,0},{2,3},{3,2},{4,5},{5,4},{6,7},{7,6},{8,9},{9,8},{10,11... | collective-permute-start | bytes 1572872 | tf_op jit(solution)/shard_map/ppermute | solution.py:18
  314.5 23.3 %collective-permute-start.72 = (f32[4,2,128,128]{3,2,1,0:T(8,128)S(1)}, f32[4,2,128,128]{3,2,1,0:T(8,128)S(1)}, u32[]{:S(2)}, u32[]{:S(2)}) collective-permute-start(f32[4,2,128,128]{3,2,1,0:T(8,128)S(1)} %get-tuple-element.101), channel_id=1, source_target_pairs={{0,4},{1,5},{2,6},{3,7},{4,0},{5,1},{6,2},{7,3},{8,12},{9,13},{10,... | collective-permute-start | bytes 1572872 | tf_op jit(solution)/shard_map/ppermute | solution.py:18
  323.5 14.9 %collective-permute-start.73 = (f32[4,2,128,128]{3,2,1,0:T(8,128)S(1)}, f32[4,2,128,128]{3,2,1,0:T(8,128)S(1)}, u32[]{:S(2)}, u32[]{:S(2)}) collective-permute-start(f32[4,2,128,128]{3,2,1,0:T(8,128)S(1)} %get-tuple-element.102), channel_id=1, source_target_pairs={{0,5},{1,4},{2,7},{3,6},{4,1},{5,0},{6,3},{7,2},{8,13},{9,12},{10,... | collective-permute-start | bytes 1572872 | tf_op jit(solution)/shard_map/ppermute | solution.py:18
  337.7 11.4 %collective-permute-start.62 = (f32[4,2,128,128]{3,2,1,0:T(8,128)S(1)}, f32[4,2,128,128]{3,2,1,0:T(8,128)S(1)}, u32[]{:S(2)}, u32[]{:S(2)}) collective-permute-start(f32[4,2,128,128]{3,2,1,0:T(8,128)S(1)} %get-tuple-element.106), channel_id=1, source_target_pairs={{0,1},{1,0},{2,3},{3,2},{4,5},{5,4},{6,7},{7,6},{8,9},{9,8},{10,11... | collective-permute-start | bytes 1572872 | tf_op jit(solution)/shard_map/ppermute | solution.py:18
  337.8 14.9 %collective-permute-start.63 = (f32[4,2,128,128]{3,2,1,0:T(8,128)S(1)}, f32[4,2,128,128]{3,2,1,0:T(8,128)S(1)}, u32[]{:S(2)}, u32[]{:S(2)}) collective-permute-start(f32[4,2,128,128]{3,2,1,0:T(8,128)S(1)} %get-tuple-element.107), channel_id=1, source_target_pairs={{0,2},{1,3},{2,0},{3,1},{4,6},{5,7},{6,4},{7,5},{8,10},{9,11},{10,... | collective-permute-start | bytes 1572872 | tf_op jit(solution)/shard_map/ppermute | solution.py:18
  338.4 24.4 %collective-permute-start.64 = (f32[4,2,128,128]{3,2,1,0:T(8,128)S(1)}, f32[4,2,128,128]{3,2,1,0:T(8,128)S(1)}, u32[]{:S(2)}, u32[]{:S(2)}) collective-permute-start(f32[4,2,128,128]{3,2,1,0:T(8,128)S(1)} %get-tuple-element.108), channel_id=1, source_target_pairs={{0,3},{1,2},{2,1},{3,0},{4,7},{5,6},{6,5},{7,4},{8,11},{9,10},{10,... | collective-permute-start | bytes 1572872 | tf_op jit(solution)/shard_map/ppermute | solution.py:18
  349.2 27.5 %collective-permute-start.65 = (f32[4,2,128,128]{3,2,1,0:T(8,128)S(1)}, f32[4,2,128,128]{3,2,1,0:T(8,128)S(1)}, u32[]{:S(2)}, u32[]{:S(2)}) collective-permute-start(f32[4,2,128,128]{3,2,1,0:T(8,128)S(1)} %get-tuple-element.110), channel_id=1, source_target_pairs={{0,1},{1,0},{2,3},{3,2},{4,5},{5,4},{6,7},{7,6},{8,9},{9,8},{10,11... | collective-permute-start | bytes 1572872 | tf_op jit(solution)/shard_map/ppermute | solution.py:18
  352.7 24.5 %collective-permute-start.66 = (f32[4,2,128,128]{3,2,1,0:T(8,128)S(1)}, f32[4,2,128,128]{3,2,1,0:T(8,128)S(1)}, u32[]{:S(2)}, u32[]{:S(2)}) collective-permute-start(f32[4,2,128,128]{3,2,1,0:T(8,128)S(1)} %get-tuple-element.111), channel_id=1, source_target_pairs={{0,4},{1,5},{2,6},{3,7},{4,0},{5,1},{6,2},{7,3},{8,12},{9,13},{10,... | collective-permute-start | bytes 1572872 | tf_op jit(solution)/shard_map/ppermute | solution.py:18
  362.8 14.7 %collective-permute-start.67 = (f32[4,2,128,128]{3,2,1,0:T(8,128)S(1)}, f32[4,2,128,128]{3,2,1,0:T(8,128)S(1)}, u32[]{:S(2)}, u32[]{:S(2)}) collective-permute-start(f32[4,2,128,128]{3,2,1,0:T(8,128)S(1)} %get-tuple-element.112), channel_id=1, source_target_pairs={{0,5},{1,4},{2,7},{3,6},{4,1},{5,0},{6,3},{7,2},{8,13},{9,12},{10,... | collective-permute-start | bytes 1572872 | tf_op jit(solution)/shard_map/ppermute | solution.py:18
  363.5 15.7 %collective-permute-start.56 = (f32[4,2,128,128]{3,2,1,0:T(8,128)S(1)}, f32[4,2,128,128]{3,2,1,0:T(8,128)S(1)}, u32[]{:S(2)}, u32[]{:S(2)}) collective-permute-start(f32[4,2,128,128]{3,2,1,0:T(8,128)S(1)} %get-tuple-element.120), channel_id=1, source_target_pairs={{0,1},{1,0},{2,3},{3,2},{4,5},{5,4},{6,7},{7,6},{8,9},{9,8},{10,11... | collective-permute-start | bytes 1572872 | tf_op jit(solution)/shard_map/ppermute | solution.py:18
  363.5 15.7 %collective-permute-start.57 = (f32[4,2,128,128]{3,2,1,0:T(8,128)S(1)}, f32[4,2,128,128]{3,2,1,0:T(8,128)S(1)}, u32[]{:S(2)}, u32[]{:S(2)}) collective-permute-start(f32[4,2,128,128]{3,2,1,0:T(8,128)S(1)} %get-tuple-element.121), channel_id=1, source_target_pairs={{0,2},{1,3},{2,0},{3,1},{4,6},{5,7},{6,4},{7,5},{8,10},{9,11},{10,... | collective-permute-start | bytes 1572872 | tf_op jit(solution)/shard_map/ppermute | solution.py:18
  376.7 13.9 %collective-permute-start.58 = (f32[4,2,128,128]{3,2,1,0:T(8,128)S(1)}, f32[4,2,128,128]{3,2,1,0:T(8,128)S(1)}, u32[]{:S(2)}, u32[]{:S(2)}) collective-permute-start(f32[4,2,128,128]{3,2,1,0:T(8,128)S(1)} %get-tuple-element.122), channel_id=1, source_target_pairs={{0,3},{1,2},{2,1},{3,0},{4,7},{5,6},{6,5},{7,4},{8,11},{9,10},{10,... | collective-permute-start | bytes 1572872 | tf_op jit(solution)/shard_map/ppermute | solution.py:18
  377.2 14.1 %collective-permute-start.59 = (f32[4,2,128,128]{3,2,1,0:T(8,128)S(1)}, f32[4,2,128,128]{3,2,1,0:T(8,128)S(1)}, u32[]{:S(2)}, u32[]{:S(2)}) collective-permute-start(f32[4,2,128,128]{3,2,1,0:T(8,128)S(1)} %get-tuple-element.124), channel_id=1, source_target_pairs={{0,1},{1,0},{2,3},{3,2},{4,5},{5,4},{6,7},{7,6},{8,9},{9,8},{10,11... | collective-permute-start | bytes 1572872 | tf_op jit(solution)/shard_map/ppermute | solution.py:18
  377.6 14.9 %collective-permute-start.60 = (f32[4,2,128,128]{3,2,1,0:T(8,128)S(1)}, f32[4,2,128,128]{3,2,1,0:T(8,128)S(1)}, u32[]{:S(2)}, u32[]{:S(2)}) collective-permute-start(f32[4,2,128,128]{3,2,1,0:T(8,128)S(1)} %get-tuple-element.125), channel_id=1, source_target_pairs={{0,4},{1,5},{2,6},{3,7},{4,0},{5,1},{6,2},{7,3},{8,12},{9,13},{10,... | collective-permute-start | bytes 1572872 | tf_op jit(solution)/shard_map/ppermute | solution.py:18
  379.2 22.7 %collective-permute-start.61 = (f32[4,2,128,128]{3,2,1,0:T(8,128)S(1)}, f32[4,2,128,128]{3,2,1,0:T(8,128)S(1)}, u32[]{:S(2)}, u32[]{:S(2)}) collective-permute-start(f32[4,2,128,128]{3,2,1,0:T(8,128)S(1)} %get-tuple-element.126), channel_id=1, source_target_pairs={{0,5},{1,4},{2,7},{3,6},{4,1},{5,0},{6,3},{7,2},{8,13},{9,12},{10,... | collective-permute-start | bytes 1572872 | tf_op jit(solution)/shard_map/ppermute | solution.py:18
  379.2 24.4 %collective-permute-start.50 = (f32[4,2,128,128]{3,2,1,0:T(8,128)S(1)}, f32[4,2,128,128]{3,2,1,0:T(8,128)S(1)}, u32[]{:S(2)}, u32[]{:S(2)}) collective-permute-start(f32[4,2,128,128]{3,2,1,0:T(8,128)S(1)} %get-tuple-element.130), channel_id=1, source_target_pairs={{0,1},{1,0},{2,3},{3,2},{4,5},{5,4},{6,7},{7,6},{8,9},{9,8},{10,11... | collective-permute-start | bytes 1572872 | tf_op jit(solution)/shard_map/ppermute | solution.py:18
  390.7 23.1 %collective-permute-start.51 = (f32[4,2,128,128]{3,2,1,0:T(8,128)S(1)}, f32[4,2,128,128]{3,2,1,0:T(8,128)S(1)}, u32[]{:S(2)}, u32[]{:S(2)}) collective-permute-start(f32[4,2,128,128]{3,2,1,0:T(8,128)S(1)} %get-tuple-element.131), channel_id=1, source_target_pairs={{0,2},{1,3},{2,0},{3,1},{4,6},{5,7},{6,4},{7,5},{8,10},{9,11},{10,... | collective-permute-start | bytes 1572872 | tf_op jit(solution)/shard_map/ppermute | solution.py:18
  391.3 24.3 %collective-permute-start.52 = (f32[4,2,128,128]{3,2,1,0:T(8,128)S(1)}, f32[4,2,128,128]{3,2,1,0:T(8,128)S(1)}, u32[]{:S(2)}, u32[]{:S(2)}) collective-permute-start(f32[4,2,128,128]{3,2,1,0:T(8,128)S(1)} %get-tuple-element.132), channel_id=1, source_target_pairs={{0,3},{1,2},{2,1},{3,0},{4,7},{5,6},{6,5},{7,4},{8,11},{9,10},{10,... | collective-permute-start | bytes 1572872 | tf_op jit(solution)/shard_map/ppermute | solution.py:18
  392.5 23.2 %collective-permute-start.53 = (f32[4,2,128,128]{3,2,1,0:T(8,128)S(1)}, f32[4,2,128,128]{3,2,1,0:T(8,128)S(1)}, u32[]{:S(2)}, u32[]{:S(2)}) collective-permute-start(f32[4,2,128,128]{3,2,1,0:T(8,128)S(1)} %get-tuple-element.134), channel_id=1, source_target_pairs={{0,1},{1,0},{2,3},{3,2},{4,5},{5,4},{6,7},{7,6},{8,9},{9,8},{10,11... | collective-permute-start | bytes 1572872 | tf_op jit(solution)/shard_map/ppermute | solution.py:18
  402.0 14.8 %collective-permute-start.54 = (f32[4,2,128,128]{3,2,1,0:T(8,128)S(1)}, f32[4,2,128,128]{3,2,1,0:T(8,128)S(1)}, u32[]{:S(2)}, u32[]{:S(2)}) collective-permute-start(f32[4,2,128,128]{3,2,1,0:T(8,128)S(1)} %get-tuple-element.135), channel_id=1, source_target_pairs={{0,4},{1,5},{2,6},{3,7},{4,0},{5,1},{6,2},{7,3},{8,12},{9,13},{10,... | collective-permute-start | bytes 1572872 | tf_op jit(solution)/shard_map/ppermute | solution.py:18
  403.6 24.3 %collective-permute-start.55 = (f32[4,2,128,128]{3,2,1,0:T(8,128)S(1)}, f32[4,2,128,128]{3,2,1,0:T(8,128)S(1)}, u32[]{:S(2)}, u32[]{:S(2)}) collective-permute-start(f32[4,2,128,128]{3,2,1,0:T(8,128)S(1)} %get-tuple-element.136), channel_id=1, source_target_pairs={{0,5},{1,4},{2,7},{3,6},{4,1},{5,0},{6,3},{7,2},{8,13},{9,12},{10,... | collective-permute-start | bytes 1572872 | tf_op jit(solution)/shard_map/ppermute | solution.py:18
  (44 other events, 469.8 us)

commit v4 on v3

--- a/solution.py
+++ b/solution.py
@@ -314,7 +314,7 @@
         out_shape=[part] * 4 + [jax.ShapeDtypeStruct((orbitals // devices, orbitals), f32)],
         scratch_shapes=[pltpu.VMEM(square, f32)],
         cost_estimate=cost(6 * orbitals**3, 16 * orbitals**2),
-        compiler_params=room(14),
+        compiler_params=room(16),
         name="compose",
     )(me, *left, *right)
     return out[:2], out[2:4], out[4]
@@ -412,13 +412,17 @@
     )(me, chol_vectors, chol_vectors)
 
 
-def turns(side):
-    return (lambda i: jnp.minimum(i, 1)) if side == 0 else (lambda i: jnp.maximum(i - 2, 0))
+def turns(side, count):
+    if side == 0:
+        return lambda i: jnp.minimum(i, count - 1)
+    return lambda i: jnp.maximum(i - count, 0)
 
 
 def shared_pieces_kernel(bits, kept, me_ref, own, *refs):
-    others, siblings, (upper, lower), refs = refs[:4], refs[4:6], refs[6:8], refs[8:]
-    outs, (left_upper, left_lower, blocks) = refs[:-3], refs[-3:]
+    steps = len(refs) - 7 - 2 * len(bits) * len(bits)
+    others, siblings, refs = refs[:steps], refs[steps : steps + 2], refs[steps + 2 :]
+    (upper, lower), outs, (left_upper, left_lower, blocks) = refs[:2], refs[2:-3], refs[-3:]
+    turn_count = steps // 2
     count, rows, orbitals = own.shape
     pair = orbitals // 4
     half = len(outs) // 2
@@ -435,12 +439,12 @@
     for i, other in enumerate(others):
         @pl.when(step == i)
         def _():
-            for j, k in enumerate(kept[i // 2]):
+            for j, k in enumerate(kept[i // turn_count]):
                 block = other[:, :, j * rows : (j + 1) * rows].reshape(size, rows)
-                put(block, size, me ^ bits[i // 2] ^ k)
+                put(block, size, me ^ bits[i // turn_count] ^ k)
 
     for side in range(2):
-        @pl.when(step // 2 == side)
+        @pl.when(step // turn_count == side)
         def _():
             at = pl.ds(pl.multiple_of((me ^ bits[side]) * rows, rows), rows)
             for p in range(count):
@@ -448,7 +452,7 @@
                 put(siblings[side][p].T, size + p * rows, me ^ 1)
 
     left = left_upper[...], left_lower[...]
-    middle = pl.ds(pl.multiple_of((1 + step // 2) * pair, pair), pair)
+    middle = pl.ds(pl.multiple_of((1 + step // turn_count) * pair, pair), pair)
     for n, at in enumerate((pl.ds(0, pair), middle)):
         value = product(left, (upper[:, at], lower[:, at]))
         for b in range(half // 2):
@@ -456,7 +460,7 @@
                 block = value[p * rows : (p + 1) * rows, b * rows : (b + 1) * rows]
                 blocks[n * (half // 2) + b, p % count, p // count] = block.T
     for side in range(2):
-        @pl.when(step // 2 == side)
+        @pl.when(step // turn_count == side)
         def _():
             for b in range(half):
                 outs[side * half + b][...] = blocks[b]
@@ -465,11 +469,12 @@
 def shared_pieces(bits, kept, near, me, chol_vectors, starts, others, siblings, right):
     _, rows, orbitals = chol_vectors.shape
     half = len(near[0])
+    count = len(others) // 2
     first, second = (start // 2 for start in starts)
     specs = [
         pl.BlockSpec(
             (2, rows, orbitals),
-            lambda i, me: (jnp.where(i < 2, first + i, second + i - 2), 0, 0),
+            lambda i, me: (jnp.where(i < count, first + i, second + i - count), 0, 0),
         )
     ]
     for x, which in others:
@@ -480,7 +485,7 @@
         )
     outs = []
     for side in range(2):
-        turn_of = turns(side)
+        turn_of = turns(side, count)
         specs.append(
             pl.BlockSpec((2, rows, rows), lambda i, me, t=turn_of: (first + t(i), 0, 0))
         )
@@ -494,7 +499,7 @@
         functools.partial(shared_pieces_kernel, bits, kept),
         grid_spec=pltpu.PrefetchScalarGridSpec(
             num_scalar_prefetch=1,
-            grid=(4,),
+            grid=(2 * count,),
             in_specs=specs + [square] * 2,
             out_specs=outs,
             scratch_shapes=[
@@ -503,11 +508,11 @@
                 pltpu.VMEM((half, 2, 2, rows, rows), f32),
             ],
         ),
-        out_shape=[jax.ShapeDtypeStruct((quad, 2, rows, rows), f32)] * (2 * half),
+        out_shape=[jax.ShapeDtypeStruct((2 * count, 2, rows, rows), f32)] * (2 * half),
         cost_estimate=cost(
-            12 * quad * rows * orbitals**2, 16 * quad * rows * orbitals
+            24 * count * rows * orbitals**2, 32 * count * rows * orbitals
         ),
-        compiler_params=room(32),
+        compiler_params=room(30),
         name="shared_pieces",
     )(me, chol_vectors, *(x for x, _ in others), *siblings, *right)
     return out[:half], out[half:]
@@ -518,7 +523,7 @@
     count, rows, _ = out_ref.shape
     half = len(orders[0]) // 2
     for side, order in enumerate(orders):
-        @pl.when(pl.program_id(0) // 2 == side)
+        @pl.when(pl.program_id(0) * 2 // pl.num_programs(0) == side)
         def _():
             for k, (index, which) in enumerate(order):
                 here = pl.ds(k * rows, rows)
@@ -532,27 +537,28 @@
 def shared_rotated(previous, parts, orders, starts, right, shape):
     _, rows, orbitals = shape
     fresh = previous is None
+    pairs = parts[0][0].shape[0] // 2
     first, second = (start // 2 for start in starts)
     specs = []
     for side in range(2):
-        turn_of = turns(side)
+        turn_of = turns(side, pairs)
         specs += [
             pl.BlockSpec((2, 2, rows, rows), lambda i, t=turn_of: (t(i), 0, 0, 0))
         ] * len(parts[side])
     count = 2 + len(specs)
     return pl.pallas_call(
         functools.partial(shared_rotated_kernel, orders),
-        grid=(4,),
+        grid=(2 * pairs,),
         in_specs=[resident((orbitals, orbitals))] * 2
         + specs
         + ([] if fresh else [pl.BlockSpec(memory_space=pl.ANY)]),
         out_specs=pl.BlockSpec(
-            (2, rows, orbitals), lambda i: (jnp.where(i < 2, first + i, second + i - 2), 0, 0)
+            (2, rows, orbitals), lambda i: (jnp.where(i < pairs, first + i, second + i - pairs), 0, 0)
         ),
         out_shape=jax.ShapeDtypeStruct(shape, f32),
         input_output_aliases={} if fresh else {count: 0},
         scratch_shapes=[pltpu.VMEM((2 * rows, orbitals), bf16)] * 2,
-        cost_estimate=cost(12 * quad * rows * orbitals**2, 16 * quad * rows * orbitals),
+        cost_estimate=cost(24 * pairs * rows * orbitals**2, 32 * pairs * rows * orbitals),
         compiler_params=room(16),
         name="shared_rotated",
     )(*right, *parts[0], *parts[1], *([] if fresh else [previous]))
@@ -665,14 +671,15 @@
     next_step = make_step(second_kernel, me, gathered, (turned_upper, turned_lower), 2)
     by_column, by_row, rotation = compose(me, step, next_step, devices)
 
-    groups = middle // quad
-    starts = [(g * quad, middle + g * quad) for g in range(groups)]
+    last = len(place_of) - 1
+    groups = [[0, 1], [2, 3, 4]] + [[h, h + 1] for h in range(5, last, 2)] + [[last]]
+    starts = [(2 * group[0], middle + 2 * group[0]) for group in groups]
     parts = []
 
-    for g in range(groups):
+    for g, group in enumerate(groups):
         others = []
         for s in range(2):
-            for h in (2 * g, 2 * g + 1):
+            for h in group:
                 window, which = place_of[h]
                 others.append((early[window][s], which))
         sent = shared_pieces(
@@ -687,7 +694,7 @@
         )
         by_column = lax.optimization_barrier((*by_column, *sent[0], *sent[1]))[:2]
     rotated = None
-    for g in range(groups):
+    for g in range(len(groups)):
         rotated = shared_rotated(rotated, parts[g], orders, starts[g], by_row, shape)
     return rotated, rotation
 

time: 441 us -> 465 us (1.054)
  the two profiles are of different devices: /device:TPU:0 before, /device:TPU:24 now
where the time goes in v4:
time: 465 us; the launch traced here: 456 us
  waiting for transfers between devices  189 us (41%)
  Pallas kernels  175 us (38%)
  starting transfers between devices  62.4 us (13%)
  local copies, waits for them, and re-layouts  28.6 us (6%)
    ppermute x66, waiting for transfers between devices, swap(): return lax.ppermute(x, 'row', [(i, i ^ k) for i in range(count)])  146 us
    pallas_call x4, Pallas kernels, shared_pieces(): pl.pallas_call(functools.partial(shared_pieces_kernel, bits, kept), grid_...  49.4 us
    ppermute x66, starting transfers between devices, swap(): return lax.ppermute(x, 'row', [(i, i ^ k) for i in range(count)])  47.4 us
    ppermute x8, waiting for transfers between devices, flip(): return lax.ppermute(x, 'vec', [(i, i ^ k) for i in range(count)])  42.9 us
    pallas_call x4, Pallas kernels, shared_rotated(): pl.pallas_call(functools.partial(shared_rotated_kernel, orders), grid=(2...  38.1 us
    pallas_call x2, Pallas kernels, make_step(): pl.pallas_call(functools.partial(kernel, devices), in_specs=[pl.BlockSpec...  31.8 us
    pallas_call x1, Pallas kernels, first_product(): pl.pallas_call(first_product_kernel, grid_spec=pltpu.PrefetchScalarGridSp...  31.7 us
    unnamed x90, local copies, waits for them, and re-layouts  28.5 us
  transfers between devices with their start and end apart: 74, of which 27 were waited for; matrix products, arithmetic and copies ran while one was open for 0% of the time, Pallas kernels for 26%

profile of v4, /device:TPU:24, one launch (start us, length us, event | category | flops | bytes accessed | tf_op | source)
XLA Modules:
  0.0 456.4 jit_solution(9324802571058782555)
XLA Ops:
  0.6 5.8 %copy-done = f32[32,128,1024]{2,1,0:T(8,128)S(1)} copy-done((f32[32,128,1024]{2,1,0:T(8,128)S(1)}, f32[32,128,1024]{2,1,0:T(8,128)}, u32[]{:S(2)}) %copy-start) | copy-done | bytes 16777240
  6.4 3.2 gradient_terms.1
  10.6 10.1 %collective-permute-done.2 = f32[64,1024]{1,0:T(8,128)S(1)} collective-permute-done((f32[64,1024]{1,0:T(8,128)S(1)}, f32[64,1024]{1,0:T(8,128)S(1)}, u32[]{:S(2)}, u32[]{:S(2)}) %collective-permute-start.2) | collective-permute-done | bytes 262176 | tf_op jit(solution)/shard_map/ppermute | solution.py:593
  20.7 2.8 collective-permute-done
  24.0 3.4 collective-permute-start.1
  27.4 3.5 collective-permute-done.3
  33.8 4.4 collective-permute-done.1
  42.1 2.8 collective-permute-done.6.refs_4_
  45.0 2.5 collective-permute-start.14
  48.0 2.3 collective-permute-done.15.refs_13_
  53.4 12.0 %shard_map.30 = (bf16[1024,1024]{1,0:T(8,128)(2,1)S(1)}, bf16[1024,1024]{1,0:T(8,128)(2,1)S(1)}, bf16[1024,1024]{1,0:T(8,128)(2,1)S(1)}, bf16[1024,1024]{1,0:T(8,128)(2,1)S(1)}) custom-call(s32[1]{0:T(128)} %bitcast.me_ref, f32[64,1024]{1,0:T(8,128)S(1)} %add.37.refs_0_, f32[64,1024]{1,0:T(8,128)S(1)} %add.39.refs_1_, ...), custom_call_target="tpu_custom_call" | custom-call | flops 12884901888 | bytes 25165824 | tf_op jit(solution)/shard_map/pallas_call | solution.py:264
  66.8 31.7 %first_product.1 = (bf16[32,128,1024]{2,1,0:T(8,128)(2,1)S(1)}, bf16[32,128,1024]{2,1,0:T(8,128)(2,1)S(1)}, f32[32,1,1024]{2,1,0:T(1,128)S(1)}) custom-call(s32[1]{0:T(128)} %bitcast.me_ref, f32[32,128,1024]{2,1,0:T(8,128)} %own.7, bf16[1024,1024]{1,0:T(8,128)(2,1)S(1)} %get-tuple-element.70.upper.rows_upper.left_upper, ...), custom_call_target="tpu_custom_call" | custom-call | flops 25769803776 | bytes 33554432 | tf_op jit(solution)/shard_map/first_product/pallas_call | solution.py:340
  98.5 3.4 copy-done.9
  103.4 4.0 collective-permute-start.21
  108.0 3.3 collective-permute-done.21
  111.4 2.6 collective-permute-done.20
  114.1 3.4 copy-done.10
  117.4 5.1 %second_terms.1 = f32[128,1024]{1,0:T(8,128)S(1)} custom-call(bf16[32,128,1024]{2,1,0:T(8,128)(2,1)S(1)} %copy-done.10, bf16[32,128,1024]{2,1,0:T(8,128)(2,1)S(1)} %get-tuple-element.73.lower_ref, f32[32,1,1024]{2,1,0:T(1,128)S(1)} %bitcast.10), custom_call_target="tpu_custom_call" | custom-call | flops 8388608 | bytes 16777216 | tf_op jit(solution)/shard_map/second_terms/pallas_call | solution.py:579
  122.6 8.1 %collective-permute-start.24 = (f32[64,1024]{1,0:T(8,128)S(1)}, f32[64,1024]{1,0:T(8,128)S(1)}, u32[]{:S(2)}, u32[]{:S(2)}) collective-permute-start(f32[64,1024]{1,0:T(8,128)S(1)} %get-tuple-element.140), channel_id=1, source_target_pairs={{0,24},{8,16},{16,8},{24,0},{1,25},{9,17},{17,9},{25,1},{2,26},{10... | collective-permute-start | bytes 786440 | tf_op jit(solution)/shard_map/ppermute | solution.py:593
  132.7 5.3 %collective-permute-done.24 = f32[64,1024]{1,0:T(8,128)S(1)} collective-permute-done((f32[64,1024]{1,0:T(8,128)S(1)}, f32[64,1024]{1,0:T(8,128)S(1)}, u32[]{:S(2)}, u32[]{:S(2)}) %collective-permute-start.24) | collective-permute-done | bytes 262176 | tf_op jit(solution)/shard_map/ppermute | solution.py:593
  138.0 5.0 %collective-permute-done.22 = f32[64,1024]{1,0:T(8,128)S(1)} collective-permute-done((f32[64,1024]{1,0:T(8,128)S(1)}, f32[64,1024]{1,0:T(8,128)S(1)}, u32[]{:S(2)}, u32[]{:S(2)}) %collective-permute-start.22) | collective-permute-done | bytes 262176 | tf_op jit(solution)/shard_map/ppermute | solution.py:593
  145.1 11.8 %collective-permute-done.25 = f32[64,1024]{1,0:T(8,128)S(1)} collective-permute-done((f32[64,1024]{1,0:T(8,128)S(1)}, f32[64,1024]{1,0:T(8,128)S(1)}, u32[]{:S(2)}, u32[]{:S(2)}) %collective-permute-start.25) | collective-permute-done | bytes 262176 | tf_op jit(solution)/shard_map/ppermute | solution.py:593
  161.2 3.0 collective-permute-done.33.refs_9_
  164.2 2.3 collective-permute-done.29.refs_5_
  166.6 2.0 collective-permute-start.37
  168.6 2.2 pack.6
  172.4 5.4 %collective-permute-done.37.refs_13_ = f32[64,1024]{1,0:T(8,128)S(1)} collective-permute-done((f32[64,1024]{1,0:T(8,128)S(1)}, f32[64,1024]{1,0:T(8,128)S(1)}, u32[]{:S(2)}, u32[]{:S(2)}) %collective-permute-start.37) | collective-permute-done | bytes 262176 | tf_op jit(solution)/shard_map/ppermute | solution.py:18
  179.5 50.6 %collective-permute-done.36.refs_12_ = f32[64,1024]{1,0:T(8,128)S(1)} collective-permute-done((f32[64,1024]{1,0:T(8,128)S(1)}, f32[64,1024]{1,0:T(8,128)S(1)}, u32[]{:S(2)}, u32[]{:S(2)}) %collective-permute-start.36) | collective-permute-done | bytes 262176 | tf_op jit(solution)/shard_map/ppermute | solution.py:18
  230.7 1.9 pack.7
  234.0 19.7 %shard_map.31 = (bf16[1024,1024]{1,0:T(8,128)(2,1)S(1)}, bf16[1024,1024]{1,0:T(8,128)(2,1)S(1)}) custom-call(s32[1]{0:T(128)} %bitcast.me_ref, f32[64,1024]{1,0:T(8,128)S(1)} %add.45.refs_0_, f32[64,1024]{1,0:T(8,128)S(1)} %add.47.refs_1_, f32[64,1024]{1,0:T(8,128)S(1)} %collective-permute-done.26.refs_2_, f32[64,1024]{1,0:T(8,128)S(1)} %collective-permute-done.27.refs_3_, ...), custom_call_target="tpu_custom_call" | custom-call | flops 12884901888 | bytes 25165824 | tf_op jit(solution)/shard_map/pallas_call | solution.py:264
  256.7 8.7 %compose.1 = (bf16[1024,1024]{1,0:T(8,128)(2,1)S(1)}, bf16[1024,1024]{1,0:T(8,128)(2,1)S(1)}, bf16[1024,1024]{1,0:T(8,128)(2,1)S(1)}, bf16[1024,1024]{1,0:T(8,128)(2,1)S(1)}, f32[128,1024]{1,0:T(8,128)}) custom-call(s32[1]{0:T(128)} %bitcast.me_ref, bf16[1024,1024]{1,0:T(8,128)(2,1)S(1)} %copy-done.30, bf16[1024,1024]{1,0:T(8,128)(2,1)S(1)} %copy-done.32, ...), custom_call_target="tpu_custom_call" | custom-call | flops 6442450944 | bytes 16777216 | tf_op jit(solution)/shard_map/compose/pallas_call | solution.py:310
  277.3 12.8 %shared_pieces.4 = (f32[4,2,128,128]{3,2,1,0:T(8,128)S(1)}, f32[4,2,128,128]{3,2,1,0:T(8,128)S(1)}, f32[4,2,128,128]{3,2,1,0:T(8,128)}, f32[4,2,128,128]{3,2,1,0...) custom-call(s32[1]{0:T(128)} %bitcast.me_ref, ...), custom_call_target="tpu_custom_call" | custom-call | flops 6442450944 | bytes 8388608 | tf_op jit(solution)/shard_map/shared_pieces/pallas_call | solution.py:498
  290.9 2.0 pack.4
  296.3 17.8 %shared_pieces.5 = (f32[6,2,128,128]{3,2,1,0:T(8,128)S(1)}, f32[6,2,128,128]{3,2,1,0:T(8,128)S(1)}, f32[6,2,128,128]{3,2,1,0:T(8,128)S(1)}, f32[6,2,128,128]{3,2...) custom-call(s32[1]{0:T(128)} %bitcast.me_ref, ...), custom_call_target="tpu_custom_call" | custom-call | flops 9663676416 | bytes 12582912 | tf_op jit(solution)/shard_map/shared_pieces/pallas_call | solution.py:498
  314.2 28.4 %collective-permute-done.69.refs_2_ = f32[4,2,128,128]{3,2,1,0:T(8,128)S(1)} collective-permute-done((f32[4,2,128,128]{3,2,1,0:T(8,128)}, f32[4,2,128,128]{3,2,1,0:T(8,128)S(1)}, u32[]{:S(2)}, u32[]{:S(2)}) %collective-permute-start.69) | collective-permute-done | bytes 524320 | tf_op jit(solution)/shard_map/ppermute | solution.py:18
  342.5 9.6 %collective-permute-done.70.refs_3_ = f32[4,2,128,128]{3,2,1,0:T(8,128)S(1)} collective-permute-done((f32[4,2,128,128]{3,2,1,0:T(8,128)S(1)}, f32[4,2,128,128]{3,2,1,0:T(8,128)S(1)}, u32[]{:S(2)}, u32[]{:S(2)}) %collective-permute-start.70) | collective-permute-done | bytes 524320 | tf_op jit(solution)/shard_map/ppermute | solution.py:18
  356.8 12.2 %shared_pieces.6 = (f32[4,2,128,128]{3,2,1,0:T(8,128)S(1)}, f32[4,2,128,128]{3,2,1,0:T(8,128)S(1)}, f32[4,2,128,128]{3,2,1,0:T(8,128)S(1)}, f32[4,2,128,128]{3,2...) custom-call(s32[1]{0:T(128)} %bitcast.me_ref, ...), custom_call_target="tpu_custom_call" | custom-call | flops 6442450944 | bytes 8388608 | tf_op jit(solution)/shard_map/shared_pieces/pallas_call | solution.py:498
  369.8 7.7 %collective-permute-done.73.refs_7_ = f32[4,2,128,128]{3,2,1,0:T(8,128)S(1)} collective-permute-done((f32[4,2,128,128]{3,2,1,0:T(8,128)}, f32[4,2,128,128]{3,2,1,0:T(8,128)S(1)}, u32[]{:S(2)}, u32[]{:S(2)}) %collective-permute-start.73) | collective-permute-done | bytes 524320 | tf_op jit(solution)/shard_map/ppermute | solution.py:18
  379.3 6.5 %shared_pieces.7 = (f32[2,2,128,128]{3,2,1,0:T(8,128)S(1)}, f32[2,2,128,128]{3,2,1,0:T(8,128)S(1)}, f32[2,2,128,128]{3,2,1,0:T(8,128)S(1)}, f32[2,2,128,128]{3,2...) custom-call(s32[1]{0:T(128)} %bitcast.me_ref, ...), custom_call_target="tpu_custom_call" | custom-call | flops 3221225472 | bytes 4194304 | tf_op jit(solution)/shard_map/shared_pieces/pallas_call | solution.py:498
  386.2 3.5 collective-permute-done.64.refs_3_
  390.7 9.6 %shared_rotated.4.refs_8_ = f32[32,128,1024]{2,1,0:T(8,128)} custom-call(bf16[1024,1024]{1,0:T(8,128)(2,1)S(1)} %copy-done.2, bf16[1024,1024]{1,0:T(8,128)(2,1)S(1)} %copy-done.4, f32[4,2,128,128]{3,2,1,0:T(8,128)S(1)} %copy-done.18, f32[4,2,128,128]{3,2,1,0:T(8,128)S(1)} %collective-permute-done.68.refs_1_, ...), custom_call_target="tpu_custom_call" | custom-call | flops 6442450944 | bytes 8388608 | tf_op jit(solution)/shard_map/shared_rotated/pallas_call | solution.py:549
  401.7 12.0 %collective-permute-done.67.refs_7_ = f32[6,2,128,128]{3,2,1,0:T(8,128)S(1)} collective-permute-done((f32[6,2,128,128]{3,2,1,0:T(8,128)S(1)}, f32[6,2,128,128]{3,2,1,0:T(8,128)S(1)}, u32[]{:S(2)}, u32[]{:S(2)}) %collective-permute-start.67) | collective-permute-done | bytes 786464 | tf_op jit(solution)/shard_map/ppermute | solution.py:18
  415.7 13.8 %shared_rotated.5.refs_8_ = f32[32,128,1024]{2,1,0:T(8,128)} custom-call(bf16[1024,1024]{1,0:T(8,128)(2,1)S(1)} %copy-done.2, bf16[1024,1024]{1,0:T(8,128)(2,1)S(1)} %copy-done.4, f32[6,2,128,128]{3,2,1,0:T(8,128)S(1)} %get-tuple-element.109.refs_0_, f32[6,2,128,128]{3,2,1,0:T(8,128)S(1)} %collective-permute-done.62.refs_1_, ...), custom_call_target="tpu_custom_call", output_to_operand_aliasing={{}: (10, {})} | custom-call | flops 9663676416 | bytes 12582912 | tf_op jit(solution)/shard_map/shared_rotated/pallas_call | solution.py:549
  429.8 1.8 collective-permute-start.52
  432.9 6.2 %collective-permute-done.61.refs_7_ = f32[4,2,128,128]{3,2,1,0:T(8,128)S(1)} collective-permute-done((f32[4,2,128,128]{3,2,1,0:T(8,128)S(1)}, f32[4,2,128,128]{3,2,1,0:T(8,128)S(1)}, u32[]{:S(2)}, u32[]{:S(2)}) %collective-permute-start.61) | collective-permute-done | bytes 524320 | tf_op jit(solution)/shard_map/ppermute | solution.py:18
  439.0 2.2 collective-permute-start.55
  441.2 9.5 %shared_rotated.6.refs_8_ = f32[32,128,1024]{2,1,0:T(8,128)} custom-call(bf16[1024,1024]{1,0:T(8,128)(2,1)S(1)} %copy-done.2, bf16[1024,1024]{1,0:T(8,128)(2,1)S(1)} %copy-done.4, f32[4,2,128,128]{3,2,1,0:T(8,128)S(1)} %get-tuple-element.119.refs_0_, f32[4,2,128,128]{3,2,1,0:T(8,128)S(1)} %collective-permute-done.56.refs_1_, ...), custom_call_target="tpu_custom_call", output_to_operand_aliasing={{}: (10, {})} | custom-call | flops 6442450944 | bytes 8388608 | tf_op jit(solution)/shard_map/shared_rotated/pallas_call | solution.py:549
  450.8 5.3 %shared_rotated.7 = f32[32,128,1024]{2,1,0:T(8,128)} custom-call(bf16[1024,1024]{1,0:T(8,128)(2,1)S(1)} %copy-done.2, bf16[1024,1024]{1,0:T(8,128)(2,1)S(1)} %copy-done.4, f32[2,2,128,128]{3,2,1,0:T(8,128)S(1)} %get-tuple-element.129.refs_0_, f32[2,2,128,128]{3,2,1,0:T(8,128)S(1)} %collective-permute-done.50.refs_1_, ...), custom_call_target="tpu_custom_call", output_to_operand_aliasing={{}: (10, {})} | custom-call | flops 3221225472 | bytes 4194304 | tf_op jit(solution)/shard_map/shared_rotated/pallas_call | solution.py:549
  (221 shorter events, 61.7 us)
Async XLA Ops:
  9.7 11.0 %collective-permute-start.2 = (f32[64,1024]{1,0:T(8,128)S(1)}, f32[64,1024]{1,0:T(8,128)S(1)}, u32[]{:S(2)}, u32[]{:S(2)}) collective-permute-start(f32[64,1024]{1,0:T(8,128)S(1)} %get-tuple-element.144), channel_id=1, source_target_pairs={{0,24},{8,16},{16,8},{24,0},{1,25},{9,17},{17,9},{25,1},{2,26},{10... | collective-permute-start | bytes 786440 | tf_op jit(solution)/shard_map/ppermute | solution.py:593
  9.8 13.7 %collective-permute-start = (f32[64,1024]{1,0:T(8,128)S(1)}, f32[64,1024]{1,0:T(8,128)S(1)}, u32[]{:S(2)}, u32[]{:S(2)}) collective-permute-start(f32[64,1024]{1,0:T(8,128)S(1)} %get-tuple-element.145), channel_id=1, source_target_pairs={{0,8},{8,0},{16,24},{24,16},{1,9},{9,1},{17,25},{25,17},{2,10},{10... | collective-permute-start | bytes 786440 | tf_op jit(solution)/shard_map/ppermute | solution.py:593
  24.0 14.2 %collective-permute-start.1 = (f32[64,1024]{1,0:T(8,128)S(1)}, f32[64,1024]{1,0:T(8,128)S(1)}, u32[]{:S(2)}, u32[]{:S(2)}) collective-permute-start(f32[64,1024]{1,0:T(8,128)S(1)} %get-tuple-element.143), channel_id=1, source_target_pairs={{0,24},{8,16},{16,8},{24,0},{1,25},{9,17},{17,9},{25,1},{2,26},{10... | collective-permute-start | bytes 786440 | tf_op jit(solution)/shard_map/ppermute | solution.py:593
  31.0 10.4 %collective-permute-start.11 = (f32[64,1024]{1,0:T(8,128)S(1)}, f32[64,1024]{1,0:T(8,128)S(1)}, u32[]{:S(2)}, u32[]{:S(2)}) collective-permute-start(f32[64,1024]{1,0:T(8,128)S(1)} %add.39.refs_1_), channel_id=1, source_target_pairs={{0,4},{1,5},{2,6},{3,7},{4,0},{5,1},{6,2},{7,3},{8,12},{9,13},{10,... | collective-permute-start | bytes 786440 | tf_op jit(solution)/shard_map/ppermute | solution.py:18
  122.6 15.4 %collective-permute-start.24 = (f32[64,1024]{1,0:T(8,128)S(1)}, f32[64,1024]{1,0:T(8,128)S(1)}, u32[]{:S(2)}, u32[]{:S(2)}) collective-permute-start(f32[64,1024]{1,0:T(8,128)S(1)} %get-tuple-element.140), channel_id=1, source_target_pairs={{0,24},{8,16},{16,8},{24,0},{1,25},{9,17},{17,9},{25,1},{2,26},{10... | collective-permute-start | bytes 786440 | tf_op jit(solution)/shard_map/ppermute | solution.py:593
  130.7 12.2 %collective-permute-start.22 = (f32[64,1024]{1,0:T(8,128)S(1)}, f32[64,1024]{1,0:T(8,128)S(1)}, u32[]{:S(2)}, u32[]{:S(2)}) collective-permute-start(f32[64,1024]{1,0:T(8,128)S(1)} %get-tuple-element.141), channel_id=1, source_target_pairs={{0,8},{8,0},{16,24},{24,16},{1,9},{9,1},{17,25},{25,17},{2,10},{10... | collective-permute-start | bytes 786440 | tf_op jit(solution)/shard_map/ppermute | solution.py:593
  131.0 29.1 %collective-permute-start.46 = (f32[2,128,768]{2,1,0:T(8,128)S(1)}, f32[2,128,768]{2,1,0:T(8,128)S(1)}, u32[]{:S(2)}, u32[]{:S(2)}) collective-permute-start(f32[2,128,768]{2,1,0:T(8,128)S(1)} %get-tuple-element.92), channel_id=1, source_target_pairs={{0,2},{1,3},{2,0},{3,1},{4,6},{5,7},{6,4},{7,5},{8,10},{9,11},{10,... | collective-permute-start | bytes 2359304 | tf_op jit(solution)/shard_map/ppermute | solution.py:18
  143.0 13.9 %collective-permute-start.25 = (f32[64,1024]{1,0:T(8,128)S(1)}, f32[64,1024]{1,0:T(8,128)S(1)}, u32[]{:S(2)}, u32[]{:S(2)}) collective-permute-start(f32[64,1024]{1,0:T(8,128)S(1)} %get-tuple-element.138), channel_id=1, source_target_pairs={{0,8},{8,0},{16,24},{24,16},{1,9},{9,1},{17,25},{25,17},{2,10},{10... | collective-permute-start | bytes 786440 | tf_op jit(solution)/shard_map/ppermute | solution.py:593
  144.8 14.6 %collective-permute-start.23 = (f32[64,1024]{1,0:T(8,128)S(1)}, f32[64,1024]{1,0:T(8,128)S(1)}, u32[]{:S(2)}, u32[]{:S(2)}) collective-permute-start(f32[64,1024]{1,0:T(8,128)S(1)} %get-tuple-element.139), channel_id=1, source_target_pairs={{0,24},{8,16},{16,8},{24,0},{1,25},{9,17},{17,9},{25,1},{2,26},{10... | collective-permute-start | bytes 786440 | tf_op jit(solution)/shard_map/ppermute | solution.py:593
  159.4 11.3 %collective-permute-start.32 = (f32[64,1024]{1,0:T(8,128)S(1)}, f32[64,1024]{1,0:T(8,128)S(1)}, u32[]{:S(2)}, u32[]{:S(2)}) collective-permute-start(f32[64,1024]{1,0:T(8,128)S(1)} %add.45.refs_0_), channel_id=1, source_target_pairs={{0,4},{1,5},{2,6},{3,7},{4,0},{5,1},{6,2},{7,3},{8,12},{9,13},{10,... | collective-permute-start | bytes 786440 | tf_op jit(solution)/shard_map/ppermute | solution.py:18
  160.1 12.1 %collective-permute-start.28 = (f32[64,1024]{1,0:T(8,128)S(1)}, f32[64,1024]{1,0:T(8,128)S(1)}, u32[]{:S(2)}, u32[]{:S(2)}) collective-permute-start(f32[64,1024]{1,0:T(8,128)S(1)} %add.45.refs_0_), channel_id=1, source_target_pairs={{0,2},{1,3},{2,0},{3,1},{4,6},{5,7},{6,4},{7,5},{8,10},{9,11},{10,... | collective-permute-start | bytes 786440 | tf_op jit(solution)/shard_map/ppermute | solution.py:18
  166.6 11.2 %collective-permute-start.37 = (f32[64,1024]{1,0:T(8,128)S(1)}, f32[64,1024]{1,0:T(8,128)S(1)}, u32[]{:S(2)}, u32[]{:S(2)}) collective-permute-start(f32[64,1024]{1,0:T(8,128)S(1)} %collective-permute-done.33.refs_9_), channel_id=1, source_target_pairs={{0,2},{1,3},{2,0},{3,1},{4,6},{5,7},{6,4},{7,5},{8,10},{9,11},{10,... | collective-permute-start | bytes 786440 | tf_op jit(solution)/shard_map/ppermute | solution.py:18
  168.6 9.2 %collective-permute-start.35 = (f32[64,1024]{1,0:T(8,128)S(1)}, f32[64,1024]{1,0:T(8,128)S(1)}, u32[]{:S(2)}, u32[]{:S(2)}) collective-permute-start(f32[64,1024]{1,0:T(8,128)S(1)} %collective-permute-done.33.refs_9_), channel_id=1, source_target_pairs={{0,1},{1,0},{2,3},{3,2},{4,5},{5,4},{6,7},{7,6},{8,9},{9,8},{10,11... | collective-permute-start | bytes 786440 | tf_op jit(solution)/shard_map/ppermute | solution.py:18
  170.7 98.8 %collective-permute-start.47 = (f32[6,128,768]{2,1,0:T(8,128)}, f32[6,128,768]{2,1,0:T(8,128)S(1)}, u32[]{:S(2)}, u32[]{:S(2)}) collective-permute-start(f32[6,128,768]{2,1,0:T(8,128)} %get-tuple-element.94), channel_id=1, source_target_pairs={{0,2},{1,3},{2,0},{3,1},{4,6},{5,7},{6,4},{7,5},{8,10},{9,11},{10,... | collective-permute-start | bytes 7077896 | tf_op jit(solution)/shard_map/ppermute | solution.py:18
  172.2 98.7 %collective-permute-start.45 = (f32[6,128,768]{2,1,0:T(8,128)S(1)}, f32[6,128,768]{2,1,0:T(8,128)S(1)}, u32[]{:S(2)}, u32[]{:S(2)}) collective-permute-start(f32[6,128,768]{2,1,0:T(8,128)S(1)} %get-tuple-element.91), channel_id=1, source_target_pairs={{0,4},{1,5},{2,6},{3,7},{4,0},{5,1},{6,2},{7,3},{8,12},{9,13},{10,... | collective-permute-start | bytes 7077896 | tf_op jit(solution)/shard_map/ppermute | solution.py:18
  177.8 52.3 %collective-permute-start.36 = (f32[64,1024]{1,0:T(8,128)S(1)}, f32[64,1024]{1,0:T(8,128)S(1)}, u32[]{:S(2)}, u32[]{:S(2)}) collective-permute-start(f32[64,1024]{1,0:T(8,128)S(1)} %collective-permute-done.28.refs_4_), channel_id=1, source_target_pairs={{0,4},{1,5},{2,6},{3,7},{4,0},{5,1},{6,2},{7,3},{8,12},{9,13},{10,... | collective-permute-start | bytes 786440 | tf_op jit(solution)/shard_map/ppermute | solution.py:18
  177.8 54.8 %collective-permute-start.30 = (f32[64,1024]{1,0:T(8,128)S(1)}, f32[64,1024]{1,0:T(8,128)S(1)}, u32[]{:S(2)}, u32[]{:S(2)}) collective-permute-start(f32[64,1024]{1,0:T(8,128)S(1)} %collective-permute-done.28.refs_4_), channel_id=1, source_target_pairs={{0,1},{1,0},{2,3},{3,2},{4,5},{5,4},{6,7},{7,6},{8,9},{9,8},{10,11... | collective-permute-start | bytes 786440 | tf_op jit(solution)/shard_map/ppermute | solution.py:18
  179.3 53.6 %collective-permute-start.39 = (f32[64,1024]{1,0:T(8,128)S(1)}, f32[64,1024]{1,0:T(8,128)S(1)}, u32[]{:S(2)}, u32[]{:S(2)}) collective-permute-start(f32[64,1024]{1,0:T(8,128)S(1)} %collective-permute-done.37.refs_13_), channel_id=1, source_target_pairs={{0,1},{1,0},{2,3},{3,2},{4,5},{5,4},{6,7},{7,6},{8,9},{9,8},{10,11... | collective-permute-start | bytes 786440 | tf_op jit(solution)/shard_map/ppermute | solution.py:18
  232.6 21.2 %collective-permute-start.44 = (f32[2,128,768]{2,1,0:T(8,128)S(1)}, f32[2,128,768]{2,1,0:T(8,128)S(1)}, u32[]{:S(2)}, u32[]{:S(2)}) collective-permute-start(f32[2,128,768]{2,1,0:T(8,128)S(1)} %get-tuple-element.89), channel_id=1, source_target_pairs={{0,4},{1,5},{2,6},{3,7},{4,0},{5,1},{6,2},{7,3},{8,12},{9,13},{10,... | collective-permute-start | bytes 2359304 | tf_op jit(solution)/shard_map/ppermute | solution.py:18
  232.9 22.1 %collective-permute-start.42 = (f32[16,128,128]{2,1,0:T(8,128)S(1)}, f32[16,128,128]{2,1,0:T(8,128)S(1)}, u32[]{:S(2)}, u32[]{:S(2)}) collective-permute-start(f32[16,128,128]{2,1,0:T(8,128)S(1)} %get-tuple-element.85), channel_id=1, source_target_pairs={{0,1},{1,0},{2,3},{3,2},{4,5},{5,4},{6,7},{7,6},{8,9},{9,8},{10,11... | collective-permute-start | bytes 3145736 | tf_op jit(solution)/shard_map/ppermute | solution.py:18
  233.2 36.3 %collective-permute-start.43 = (f32[16,128,128]{2,1,0:T(8,128)S(1)}, f32[16,128,128]{2,1,0:T(8,128)S(1)}, u32[]{:S(2)}, u32[]{:S(2)}) collective-permute-start(f32[16,128,128]{2,1,0:T(8,128)S(1)} %get-tuple-element.86), channel_id=1, source_target_pairs={{0,1},{1,0},{2,3},{3,2},{4,5},{5,4},{6,7},{7,6},{8,9},{9,8},{10,11... | collective-permute-start | bytes 3145736 | tf_op jit(solution)/shard_map/ppermute | solution.py:18
  253.8 40.3 %collective-permute-start.48 = (f32[4,128,768]{2,1,0:T(8,128)}, f32[4,128,768]{2,1,0:T(8,128)}, u32[]{:S(2)}, u32[]{:S(2)}) collective-permute-start(f32[4,128,768]{2,1,0:T(8,128)} %get-tuple-element.106), channel_id=1, source_target_pairs={{0,4},{1,5},{2,6},{3,7},{4,0},{5,1},{6,2},{7,3},{8,12},{9,13},{10,... | collective-permute-start | bytes 4718600 | tf_op jit(solution)/shard_map/ppermute | solution.py:18
  255.0 40.8 %collective-permute-start.49 = (f32[4,128,768]{2,1,0:T(8,128)}, f32[4,128,768]{2,1,0:T(8,128)}, u32[]{:S(2)}, u32[]{:S(2)}) collective-permute-start(f32[4,128,768]{2,1,0:T(8,128)} %get-tuple-element.108), channel_id=1, source_target_pairs={{0,2},{1,3},{2,0},{3,1},{4,6},{5,7},{6,4},{7,5},{8,10},{9,11},{10,... | collective-permute-start | bytes 4718600 | tf_op jit(solution)/shard_map/ppermute | solution.py:18
  292.9 61.2 %collective-permute-start.40 = (f32[4,128,768]{2,1,0:T(8,128)}, f32[4,128,768]{2,1,0:T(8,128)S(1)}, u32[]{:S(2)}, u32[]{:S(2)}) collective-permute-start(f32[4,128,768]{2,1,0:T(8,128)} %get-tuple-element.82), channel_id=1, source_target_pairs={{0,4},{1,5},{2,6},{3,7},{4,0},{5,1},{6,2},{7,3},{8,12},{9,13},{10,... | collective-permute-start | bytes 4718600 | tf_op jit(solution)/shard_map/ppermute | solution.py:18
  293.8 60.6 %collective-permute-start.41 = (f32[4,128,768]{2,1,0:T(8,128)}, f32[4,128,768]{2,1,0:T(8,128)S(1)}, u32[]{:S(2)}, u32[]{:S(2)}) collective-permute-start(f32[4,128,768]{2,1,0:T(8,128)} %get-tuple-element.84), channel_id=1, source_target_pairs={{0,2},{1,3},{2,0},{3,1},{4,6},{5,7},{6,4},{7,5},{8,10},{9,11},{10,... | collective-permute-start | bytes 4718600 | tf_op jit(solution)/shard_map/ppermute | solution.py:18
  294.2 48.4 %collective-permute-start.69 = (f32[4,2,128,128]{3,2,1,0:T(8,128)}, f32[4,2,128,128]{3,2,1,0:T(8,128)S(1)}, u32[]{:S(2)}, u32[]{:S(2)}) collective-permute-start(f32[4,2,128,128]{3,2,1,0:T(8,128)} %get-tuple-element.97), channel_id=1, source_target_pairs={{0,2},{1,3},{2,0},{3,1},{4,6},{5,7},{6,4},{7,5},{8,10},{9,11},{10,... | collective-permute-start | bytes 1572872 | tf_op jit(solution)/shard_map/ppermute | solution.py:18
  295.8 56.3 %collective-permute-start.70 = (f32[4,2,128,128]{3,2,1,0:T(8,128)S(1)}, f32[4,2,128,128]{3,2,1,0:T(8,128)S(1)}, u32[]{:S(2)}, u32[]{:S(2)}) collective-permute-start(f32[4,2,128,128]{3,2,1,0:T(8,128)S(1)} %get-tuple-element.98), channel_id=1, source_target_pairs={{0,3},{1,2},{2,1},{3,0},{4,7},{5,6},{6,5},{7,4},{8,11},{9,10},{10,... | collective-permute-start | bytes 1572872 | tf_op jit(solution)/shard_map/ppermute | solution.py:18
  295.8 57.4 %collective-permute-start.71 = (f32[4,2,128,128]{3,2,1,0:T(8,128)S(1)}, f32[4,2,128,128]{3,2,1,0:T(8,128)S(1)}, u32[]{:S(2)}, u32[]{:S(2)}) collective-permute-start(f32[4,2,128,128]{3,2,1,0:T(8,128)S(1)} %get-tuple-element.100), channel_id=1, source_target_pairs={{0,1},{1,0},{2,3},{3,2},{4,5},{5,4},{6,7},{7,6},{8,9},{9,8},{10,11... | collective-permute-start | bytes 1572872 | tf_op jit(solution)/shard_map/ppermute | solution.py:18
  342.5 36.1 %collective-permute-start.62 = (f32[6,2,128,128]{3,2,1,0:T(8,128)S(1)}, f32[6,2,128,128]{3,2,1,0:T(8,128)S(1)}, u32[]{:S(2)}, u32[]{:S(2)}) collective-permute-start(f32[6,2,128,128]{3,2,1,0:T(8,128)S(1)} %get-tuple-element.110), channel_id=1, source_target_pairs={{0,1},{1,0},{2,3},{3,2},{4,5},{5,4},{6,7},{7,6},{8,9},{9,8},{10,11... | collective-permute-start | bytes 2359304 | tf_op jit(solution)/shard_map/ppermute | solution.py:18
  352.1 17.0 %collective-permute-start.72 = (f32[4,2,128,128]{3,2,1,0:T(8,128)S(1)}, f32[4,2,128,128]{3,2,1,0:T(8,128)S(1)}, u32[]{:S(2)}, u32[]{:S(2)}) collective-permute-start(f32[4,2,128,128]{3,2,1,0:T(8,128)S(1)} %get-tuple-element.101), channel_id=1, source_target_pairs={{0,4},{1,5},{2,6},{3,7},{4,0},{5,1},{6,2},{7,3},{8,12},{9,13},{10,... | collective-permute-start | bytes 1572872 | tf_op jit(solution)/shard_map/ppermute | solution.py:18
  353.2 24.3 %collective-permute-start.73 = (f32[4,2,128,128]{3,2,1,0:T(8,128)}, f32[4,2,128,128]{3,2,1,0:T(8,128)S(1)}, u32[]{:S(2)}, u32[]{:S(2)}) collective-permute-start(f32[4,2,128,128]{3,2,1,0:T(8,128)} %get-tuple-element.102), channel_id=1, source_target_pairs={{0,5},{1,4},{2,7},{3,6},{4,1},{5,0},{6,3},{7,2},{8,13},{9,12},{10,... | collective-permute-start | bytes 1572872 | tf_op jit(solution)/shard_map/ppermute | solution.py:18
  354.1 31.7 %collective-permute-start.63 = (f32[6,2,128,128]{3,2,1,0:T(8,128)S(1)}, f32[6,2,128,128]{3,2,1,0:T(8,128)S(1)}, u32[]{:S(2)}, u32[]{:S(2)}) collective-permute-start(f32[6,2,128,128]{3,2,1,0:T(8,128)S(1)} %get-tuple-element.111), channel_id=1, source_target_pairs={{0,2},{1,3},{2,0},{3,1},{4,6},{5,7},{6,4},{7,5},{8,10},{9,11},{10,... | collective-permute-start | bytes 2359304 | tf_op jit(solution)/shard_map/ppermute | solution.py:18
  354.5 35.3 %collective-permute-start.64 = (f32[6,2,128,128]{3,2,1,0:T(8,128)S(1)}, f32[6,2,128,128]{3,2,1,0:T(8,128)S(1)}, u32[]{:S(2)}, u32[]{:S(2)}) collective-permute-start(f32[6,2,128,128]{3,2,1,0:T(8,128)S(1)} %get-tuple-element.112), channel_id=1, source_target_pairs={{0,3},{1,2},{2,1},{3,0},{4,7},{5,6},{6,5},{7,4},{8,11},{9,10},{10,... | collective-permute-start | bytes 2359304 | tf_op jit(solution)/shard_map/ppermute | solution.py:18
  369.1 31.1 %collective-permute-start.65 = (f32[6,2,128,128]{3,2,1,0:T(8,128)S(1)}, f32[6,2,128,128]{3,2,1,0:T(8,128)S(1)}, u32[]{:S(2)}, u32[]{:S(2)}) collective-permute-start(f32[6,2,128,128]{3,2,1,0:T(8,128)S(1)} %get-tuple-element.114), channel_id=1, source_target_pairs={{0,1},{1,0},{2,3},{3,2},{4,5},{5,4},{6,7},{7,6},{8,9},{9,8},{10,11... | collective-permute-start | bytes 2359304 | tf_op jit(solution)/shard_map/ppermute | solution.py:18
  377.5 23.3 %collective-permute-start.66 = (f32[6,2,128,128]{3,2,1,0:T(8,128)S(1)}, f32[6,2,128,128]{3,2,1,0:T(8,128)S(1)}, u32[]{:S(2)}, u32[]{:S(2)}) collective-permute-start(f32[6,2,128,128]{3,2,1,0:T(8,128)S(1)} %get-tuple-element.115), channel_id=1, source_target_pairs={{0,4},{1,5},{2,6},{3,7},{4,0},{5,1},{6,2},{7,3},{8,12},{9,13},{10,... | collective-permute-start | bytes 2359304 | tf_op jit(solution)/shard_map/ppermute | solution.py:18
  378.6 35.1 %collective-permute-start.67 = (f32[6,2,128,128]{3,2,1,0:T(8,128)S(1)}, f32[6,2,128,128]{3,2,1,0:T(8,128)S(1)}, u32[]{:S(2)}, u32[]{:S(2)}) collective-permute-start(f32[6,2,128,128]{3,2,1,0:T(8,128)S(1)} %get-tuple-element.116), channel_id=1, source_target_pairs={{0,5},{1,4},{2,7},{3,6},{4,1},{5,0},{6,3},{7,2},{8,13},{9,12},{10,... | collective-permute-start | bytes 2359304 | tf_op jit(solution)/shard_map/ppermute | solution.py:18
  385.8 29.7 %collective-permute-start.56 = (f32[4,2,128,128]{3,2,1,0:T(8,128)S(1)}, f32[4,2,128,128]{3,2,1,0:T(8,128)S(1)}, u32[]{:S(2)}, u32[]{:S(2)}) collective-permute-start(f32[4,2,128,128]{3,2,1,0:T(8,128)S(1)} %get-tuple-element.120), channel_id=1, source_target_pairs={{0,1},{1,0},{2,3},{3,2},{4,5},{5,4},{6,7},{7,6},{8,9},{9,8},{10,11... | collective-permute-start | bytes 1572872 | tf_op jit(solution)/shard_map/ppermute | solution.py:18
  389.7 24.6 %collective-permute-start.50 = (f32[2,2,128,128]{3,2,1,0:T(8,128)S(1)}, f32[2,2,128,128]{3,2,1,0:T(8,128)S(1)}, u32[]{:S(2)}, u32[]{:S(2)}) collective-permute-start(f32[2,2,128,128]{3,2,1,0:T(8,128)S(1)} %get-tuple-element.130), channel_id=1, source_target_pairs={{0,1},{1,0},{2,3},{3,2},{4,5},{5,4},{6,7},{7,6},{8,9},{9,8},{10,11... | collective-permute-start | bytes 786440 | tf_op jit(solution)/shard_map/ppermute | solution.py:18
  400.3 29.2 %collective-permute-start.57 = (f32[4,2,128,128]{3,2,1,0:T(8,128)S(1)}, f32[4,2,128,128]{3,2,1,0:T(8,128)S(1)}, u32[]{:S(2)}, u32[]{:S(2)}) collective-permute-start(f32[4,2,128,128]{3,2,1,0:T(8,128)S(1)} %get-tuple-element.121), channel_id=1, source_target_pairs={{0,2},{1,3},{2,0},{3,1},{4,6},{5,7},{6,4},{7,5},{8,10},{9,11},{10,... | collective-permute-start | bytes 1572872 | tf_op jit(solution)/shard_map/ppermute | solution.py:18
  400.8 29.1 %collective-permute-start.58 = (f32[4,2,128,128]{3,2,1,0:T(8,128)S(1)}, f32[4,2,128,128]{3,2,1,0:T(8,128)S(1)}, u32[]{:S(2)}, u32[]{:S(2)}) collective-permute-start(f32[4,2,128,128]{3,2,1,0:T(8,128)S(1)} %get-tuple-element.122), channel_id=1, source_target_pairs={{0,3},{1,2},{2,1},{3,0},{4,7},{5,6},{6,5},{7,4},{8,11},{9,10},{10,... | collective-permute-start | bytes 1572872 | tf_op jit(solution)/shard_map/ppermute | solution.py:18
  413.7 17.9 %collective-permute-start.59 = (f32[4,2,128,128]{3,2,1,0:T(8,128)S(1)}, f32[4,2,128,128]{3,2,1,0:T(8,128)S(1)}, u32[]{:S(2)}, u32[]{:S(2)}) collective-permute-start(f32[4,2,128,128]{3,2,1,0:T(8,128)S(1)} %get-tuple-element.124), channel_id=1, source_target_pairs={{0,1},{1,0},{2,3},{3,2},{4,5},{5,4},{6,7},{7,6},{8,9},{9,8},{10,11... | collective-permute-start | bytes 1572872 | tf_op jit(solution)/shard_map/ppermute | solution.py:18
  414.3 17.3 %collective-permute-start.60 = (f32[4,2,128,128]{3,2,1,0:T(8,128)S(1)}, f32[4,2,128,128]{3,2,1,0:T(8,128)S(1)}, u32[]{:S(2)}, u32[]{:S(2)}) collective-permute-start(f32[4,2,128,128]{3,2,1,0:T(8,128)S(1)} %get-tuple-element.125), channel_id=1, source_target_pairs={{0,4},{1,5},{2,6},{3,7},{4,0},{5,1},{6,2},{7,3},{8,12},{9,13},{10,... | collective-permute-start | bytes 1572872 | tf_op jit(solution)/shard_map/ppermute | solution.py:18
  415.5 23.5 %collective-permute-start.61 = (f32[4,2,128,128]{3,2,1,0:T(8,128)S(1)}, f32[4,2,128,128]{3,2,1,0:T(8,128)S(1)}, u32[]{:S(2)}, u32[]{:S(2)}) collective-permute-start(f32[4,2,128,128]{3,2,1,0:T(8,128)S(1)} %get-tuple-element.126), channel_id=1, source_target_pairs={{0,5},{1,4},{2,7},{3,6},{4,1},{5,0},{6,3},{7,2},{8,13},{9,12},{10,... | collective-permute-start | bytes 1572872 | tf_op jit(solution)/shard_map/ppermute | solution.py:18
  429.5 21.2 %collective-permute-start.51 = (f32[2,2,128,128]{3,2,1,0:T(8,128)S(1)}, f32[2,2,128,128]{3,2,1,0:T(8,128)S(1)}, u32[]{:S(2)}, u32[]{:S(2)}) collective-permute-start(f32[2,2,128,128]{3,2,1,0:T(8,128)S(1)} %copy-done.28), channel_id=1, source_target_pairs={{0,2},{1,3},{2,0},{3,1},{4,6},{5,7},{6,4},{7,5},{8,10},{9,11},{10,... | collective-permute-start | bytes 786440 | tf_op jit(solution)/shard_map/ppermute | solution.py:18
  429.8 20.9 %collective-permute-start.52 = (f32[2,2,128,128]{3,2,1,0:T(8,128)S(1)}, f32[2,2,128,128]{3,2,1,0:T(8,128)S(1)}, u32[]{:S(2)}, u32[]{:S(2)}) collective-permute-start(f32[2,2,128,128]{3,2,1,0:T(8,128)S(1)} %copy-done.26), channel_id=1, source_target_pairs={{0,3},{1,2},{2,1},{3,0},{4,7},{5,6},{6,5},{7,4},{8,11},{9,10},{10,... | collective-permute-start | bytes 786440 | tf_op jit(solution)/shard_map/ppermute | solution.py:18
  431.7 19.1 %collective-permute-start.53 = (f32[2,2,128,128]{3,2,1,0:T(8,128)S(1)}, f32[2,2,128,128]{3,2,1,0:T(8,128)S(1)}, u32[]{:S(2)}, u32[]{:S(2)}) collective-permute-start(f32[2,2,128,128]{3,2,1,0:T(8,128)S(1)} %copy-done.24), channel_id=1, source_target_pairs={{0,1},{1,0},{2,3},{3,2},{4,5},{5,4},{6,7},{7,6},{8,9},{9,8},{10,11... | collective-permute-start | bytes 786440 | tf_op jit(solution)/shard_map/ppermute | solution.py:18
  431.7 19.1 %collective-permute-start.54 = (f32[2,2,128,128]{3,2,1,0:T(8,128)S(1)}, f32[2,2,128,128]{3,2,1,0:T(8,128)S(1)}, u32[]{:S(2)}, u32[]{:S(2)}) collective-permute-start(f32[2,2,128,128]{3,2,1,0:T(8,128)S(1)} %copy-done.22), channel_id=1, source_target_pairs={{0,4},{1,5},{2,6},{3,7},{4,0},{5,1},{6,2},{7,3},{8,12},{9,13},{10,... | collective-permute-start | bytes 786440 | tf_op jit(solution)/shard_map/ppermute | solution.py:18
  439.0 11.7 %collective-permute-start.55 = (f32[2,2,128,128]{3,2,1,0:T(8,128)S(1)}, f32[2,2,128,128]{3,2,1,0:T(8,128)S(1)}, u32[]{:S(2)}, u32[]{:S(2)}) collective-permute-start(f32[2,2,128,128]{3,2,1,0:T(8,128)S(1)} %get-tuple-element.136), channel_id=1, source_target_pairs={{0,5},{1,4},{2,7},{3,6},{4,1},{5,0},{6,3},{7,2},{8,13},{9,12},{10,... | collective-permute-start | bytes 786440 | tf_op jit(solution)/shard_map/ppermute | solution.py:18
  (71 other events, 1011.7 us)
